TPU v7x, 512 devices: a whole 4x8x8 slice. The times are simulated.
512 devices in a mesh: dp: 32 (over z, y_lo, core), ctx: 16 (over y_hi, x).
Axes of the slice: x: 4, y: 8 (y_hi: 4, y_lo: 2; y = y_hi * 2 + y_lo), z: 8, core: 2. Of those that a mesh axis runs over, the one named last changes fastest.
Arguments:
- activations: bfloat16 [32, 2048, 2048], P('dp', 'ctx'), may hold values from -8 to 8
- out_grads: bfloat16 [32, 2048, 2048], P('dp', 'ctx'), may hold values from -64 to 64
- segment_ids: int32 [32, 2048], P('dp', 'ctx'), may hold values from -1 to 7, as said below
Outputs:
- weight_grad: float32 [2048, 2048], P('ctx', 'dp')
- clip_factors: float32 [32, 8], P('dp')
Inputs may be any that keep to these rules, and one draw needn't show every extreme that they name: `segment_ids`: each sequence holds 8 documents, numbered in order; each occupies one or more whole consecutive blocks of 128 tokens, and -1 (padding) occurs only at the end of a document's last block; every document has at least one token.
All inputs are finite; a program needn't handle non-finite values.
Results may differ from a plain program's by a relative error of at most 0.0016.
Values may be sent and summed in bfloat16 or wider, within the bound.
No kernel may reach another device: no remote copies, remote signals or barrier semaphores. Data moves between devices by JAX's collectives and lax.ppermute only.
A program may use at most 128 MiB of HBM per device.

v0:
```python
import functools

import jax
import jax.numpy as jnp
import numpy as np
from jax import lax
from jax.experimental import pallas as pl
from jax.experimental.pallas import tpu as pltpu
from jax.sharding import Mesh
from jax.sharding import PartitionSpec as P


INTERPRET = False
CLIP = 600.0
BLOCK = 128
COLS = 64
DOCS = 8
SLABS = 16
PART = 4 * BLOCK
TAIL = 8
PAD = 16

AXES = ("zh", "zl", "yl", "c", "yh", "x")
MOVE = ("yl", "c", "yh", "x")
GROUP = ("yl", "c", "x")
SUMMED = ("zh", "zl", "yh")


def table(sizes, axes, to):
    dims = [sizes[a] for a in axes]
    pairs = []
    for src in range(int(np.prod(dims))):
        at = dict(zip(axes, np.unravel_index(src, dims)))
        dst = to(**at)
        pairs.append((src, int(np.ravel_multi_index([int(dst[a]) for a in axes], dims))))
    return pairs


def to_group(k, yl, c, yh, x):
    j = (yh + k) % 4
    return dict(yl=j // 2, c=j % 2, yh=c * 2 + yl, x=(x + k) % 4)


def prep_kernel(pos, ids_ref, a_ref, g_ref, *rest):
    outs, gt_ref = rest[:4], rest[4]
    x, yh = pos[0], pos[1]
    chunks = g_ref.shape[1] // BLOCK
    ids = ids_ref[...]
    kept = ids >= 0
    doc = jnp.max(ids.astype(jnp.float32), axis=1, keepdims=True)
    doc = jnp.broadcast_to(doc, (PAD, BLOCK)).astype(jnp.bfloat16)
    for n in range(chunks):
        t = g_ref[:, n * BLOCK : (n + 1) * BLOCK].astype(jnp.float32).T
        gt_ref[n * BLOCK : (n + 1) * BLOCK, :] = jnp.where(kept, t, 0.0).astype(jnp.bfloat16)
    wide = chunks * BLOCK // 4
    for k in range(4):
        i = (x + k) % 4
        j = (yh + k) % 4
        for z in range(wide // COLS):
            at = pl.multiple_of((z * 4 + j) * COLS, COLS)
            outs[k][z * COLS : (z + 1) * COLS, :] = gt_ref[pl.ds(at, COLS), :]
        for r in range(4):
            at = pl.multiple_of((r * 4 + i) * BLOCK, BLOCK)
            outs[k][wide + r * BLOCK : wide + (r + 1) * BLOCK, :] = a_ref[:, pl.ds(at, BLOCK)]
        outs[k][wide + PART :, :] = doc


def fetch(pos, parts, a_s, g_s, doc_s, sems):
    x, j = pos[0], pos[2]
    copies = []

    def copy(src, dst):
        copies.append(pltpu.make_async_copy(src, dst, sems.at[len(copies)]))

    for k in range(4):
        for m in range(4):
            t = ((j ^ m) + 4 - k) % 4 * 4 + (x + 4 - k) % 4
            at = pl.multiple_of(t * BLOCK, BLOCK)
            for r in range(4):
                rows = slice(r * BLOCK, (r + 1) * BLOCK)
                copy(parts[m].at[k, rows], a_s.at[pl.ds(at, BLOCK), rows])
            copy(parts[m].at[k, PART:], doc_s.at[t])
        for m in range(4):
            if k < 2:
                src, sender = parts[4 + m].at[k], (x + 4 - m) % 4
            else:
                src, sender = parts[8].at[m, k - 2], m
            t = (j + 4 - k) % 4 * 4 + (sender + 4 - k) % 4
            at = pl.multiple_of(t * BLOCK, BLOCK)
            copy(src, g_s.at[:, pl.ds(at, BLOCK)])
    for cp in copies:
        cp.start()
    for cp in copies:
        cp.wait()


COPIES = 16 * 6


def norm_kernel(pos, *refs):
    parts, out, a_s, g_s, doc_s, acc, starts, sems = refs[:9], *refs[9:]
    fetch(pos, parts, a_s, g_s, doc_s, sems)
    a_s[SLABS * BLOCK :, :] = jnp.zeros((BLOCK, a_s.shape[1]), a_s.dtype)
    out[...] = jnp.zeros_like(out)
    doc = jnp.int32(-1)
    for t in range(SLABS):
        here = jnp.maximum(doc, jnp.max(doc_s[t].astype(jnp.float32)).astype(jnp.int32))
        new = here != doc

        @pl.when(new)
        def _(here=here, t=t):
            starts[here] = t

        doc = here
    starts[DOCS] = SLABS
    lane = lax.broadcasted_iota(jnp.int32, (1, BLOCK), 1)
    second = lax.broadcasted_iota(jnp.int32, (1, 2 * BLOCK), 1) >= BLOCK

    def product(first, end):
        at = pl.multiple_of(first * BLOCK, BLOCK)
        g = g_s[:, pl.ds(at, 2 * BLOCK)]
        g = jnp.where(jnp.logical_and(second, first + 1 >= end), jnp.zeros_like(g), g)
        return jnp.dot(g, a_s[pl.ds(at, 2 * BLOCK), :], preferred_element_type=jnp.float32)

    def squared(w, d):
        total = jnp.sum(jnp.sum(w * w, axis=0, keepdims=True), axis=1, keepdims=True)
        out[...] = jnp.where(lane == d, total, out[...])

    def document(d, carry):
        first, end = starts[d], starts[d + 1]

        @pl.when(end - first <= 2)
        def _():
            squared(product(first, end), d)

        @pl.when(end - first > 2)
        def _():
            acc[...] = product(first, end)

            def more(n, c):
                acc[...] = acc[...] + product(first + 2 * n, end)
                return c

            lax.fori_loop(1, (end - first + 1) // 2, more, 0)
            squared(acc[...], d)

        return carry

    lax.fori_loop(0, DOCS, document, 0)


def grad_kernel(pos, *refs):
    norms, own, parts = refs[0], refs[1], refs[2:11]
    out, clip_out, a_s, g_s, doc_s, acc, sems = refs[11:]
    fetch(pos, parts, a_s, g_s, doc_s, sems)
    norm_sq = jnp.sum(norms[...], axis=0)
    clip = CLIP / jnp.sqrt(jnp.maximum(norm_sq, CLIP * CLIP))
    clip_out[...] = clip
    bound = jnp.sum(jnp.minimum(jnp.sqrt(own[...]), CLIP), axis=1, keepdims=True)
    shift = jnp.ceil(jnp.log2(jnp.maximum(bound, 1e-18))) - 14.0
    lane = lax.broadcasted_iota(jnp.int32, (1, BLOCK), 1).astype(jnp.float32)
    for t in range(SLABS):
        here = doc_s[t, 0:1, :].astype(jnp.float32) == lane
        factor = jnp.sum(jnp.where(here, clip, 0.0), axis=1, keepdims=True)
        g = g_s[:, t * BLOCK : (t + 1) * BLOCK].astype(jnp.float32)
        g_s[:, t * BLOCK : (t + 1) * BLOCK] = (g * factor).astype(jnp.bfloat16)
    tokens = SLABS * BLOCK
    acc[...] = jnp.dot(g_s[:, :tokens], a_s[:tokens, :], preferred_element_type=jnp.float32)
    scale = jnp.exp2(-shift)
    tail = jnp.broadcast_to(shift, (TAIL, BLOCK))
    for z in range(out.shape[0]):
        for y in range(4):
            piece = acc[z * COLS : (z + 1) * COLS, y * BLOCK : (y + 1) * BLOCK]
            out[z, y, :COLS] = piece * scale
            out[z, y, COLS:] = tail


def body(sizes, activations, out_grads, segment_ids):
    a, g, ids = activations[0], out_grads[0], segment_ids
    levels = sizes["zh"] * sizes["zl"]
    wide = levels * COLS
    bf16, f32 = jnp.bfloat16, jnp.float32
    x = lax.axis_index("x")
    yh = lax.axis_index("yh")
    j = lax.axis_index("yl") * 2 + lax.axis_index("c")
    pos = jnp.stack([x, yh, j]).astype(jnp.int32)
    smem = pl.BlockSpec(memory_space=pltpu.SMEM)
    vmem = pl.BlockSpec(memory_space=pltpu.VMEM)
    anywhere = pl.BlockSpec(memory_space=pl.ANY)

    payload = pl.pallas_call(
        prep_kernel,
        out_shape=[jax.ShapeDtypeStruct((wide + PART + PAD, BLOCK), bf16)] * 4,
        in_specs=[smem, vmem, vmem, vmem],
        out_specs=[vmem] * 4,
        scratch_shapes=[pltpu.VMEM((g.shape[1], BLOCK), bf16)],
        interpret=INTERPRET,
        name="prep",
    )(pos, ids, a, g)

    arrived = [
        lax.ppermute(payload[k], MOVE, table(sizes, MOVE, functools.partial(to_group, k))) for k in range(4)
    ]
    flip = [(0, 1), (1, 0)]
    last_g = jnp.stack([p[:wide] for p in arrived[2:]])
    last_g = lax.all_to_all(
        jnp.broadcast_to(last_g, (4, *last_g.shape)), "x", split_axis=0, concat_axis=0, tiled=True
    )
    own_a = jnp.stack([p[wide:] for p in arrived])
    own_g = jnp.stack([p[:wide] for p in arrived[:2]])
    partner = lax.ppermute(own_a, "yl", flip)
    own_other = lax.ppermute(own_a, "c", flip)
    g_parts = [own_g]
    for m in (1, 2, 3):
        g_parts.append(lax.ppermute(own_g, "x", [(s, (s + m) % 4) for s in range(4)]))
    partner_other = lax.ppermute(partner, "c", flip)
    a_parts = [own_a, own_other, partner, partner_other]
    parts = a_parts + g_parts + [last_g]

    stores = [
        pltpu.VMEM(((SLABS + 1) * BLOCK, PART), bf16),
        pltpu.VMEM((wide, (SLABS + 1) * BLOCK), bf16),
        pltpu.VMEM((SLABS, PAD, BLOCK), bf16),
        pltpu.VMEM((wide, PART), f32),
    ]
    sems = [pltpu.SemaphoreType.DMA((COPIES,))]
    row = jax.ShapeDtypeStruct((1, BLOCK), f32)
    partial = pl.pallas_call(
        norm_kernel,
        out_shape=row,
        in_specs=[smem] + [anywhere] * 9,
        out_specs=vmem,
        scratch_shapes=stores + [pltpu.SMEM((DOCS + 1,), jnp.int32)] + sems,
        interpret=INTERPRET,
        name="norms",
    )(pos, *parts)
    norms = lax.all_to_all(
        jnp.broadcast_to(partial, (16, 1, BLOCK)), GROUP, split_axis=0, concat_axis=0, tiled=True
    )
    pieces, clip = pl.pallas_call(
        grad_kernel,
        out_shape=[jax.ShapeDtypeStruct((levels, 4, COLS + TAIL, BLOCK), f32), row],
        in_specs=[smem, vmem, vmem] + [anywhere] * 9,
        out_specs=[vmem] * 2,
        scratch_shapes=stores + sems,
        interpret=INTERPRET,
        name="grads",
    )(pos, norms, partial, *parts)
    pieces = pieces.astype(jnp.float16).reshape(levels * 4, COLS + TAIL, BLOCK)
    summands = lax.all_to_all(pieces, SUMMED, split_axis=0, concat_axis=0, tiled=True).astype(f32)
    weight_grad = jnp.sum(summands[:, :COLS] * jnp.exp2(summands[:, COLS : COLS + 1]), axis=0).T
    home = [(dst, src) for src, dst in table(sizes, MOVE, functools.partial(to_group, 0))]
    clip = lax.ppermute(clip, MOVE, home)
    return weight_grad, clip[:, :DOCS]


def solution(mesh):
    heights = mesh.devices.size // 128
    dims = (heights, 2, 2, 2, 4, 4)
    fine = Mesh(mesh.devices.reshape(dims), AXES)
    dp, ctx = AXES[:4], AXES[4:]
    placed = (P(dp, ctx, None), P(dp, ctx, None), P(dp, ctx))
    return jax.shard_map(
        functools.partial(body, dict(zip(AXES, dims))),
        mesh=fine,
        in_specs=placed,
        out_specs=(P(ctx, dp), P(dp, None)),
        check_vma=False,
    )
```

profile of v0, /device:TPU:1, one launch (start us, length us, event | category | flops | bytes accessed | tf_op | source)
XLA Modules:
  0.0 141.3 jit_solution(9356921280226347787)
XLA Ops:
  0.6 0.7 pad_add_fusion.pos
  1.3 2.5 %prep.1 = (bf16[1040,128]{1,0:T(8,128)(2,1)}, bf16[1040,128]{1,0:T(8,128)(2,1)}, bf16[1040,128]{1,0:T(8,128)(2,1)}, bf16[1040,128]{1,0:T(8,128)(2,1)}) custom-call(s32[3]{0:T(128)} %pad_add_fusion.pos, s32[1,128]{1,0:T(1,128)} %ids_ref.1, bf16[128,2048]{1,0:T(8,128)(2,1)} %bitcast.26, bf16[128,2048]{1,0:T(8,128)(2,1)} %bitcast.27), custom_call_target="tpu_custom_call" | custom-call | tf_op jit(solution)/shard_map/prep/pallas_call | solution.py:191
  3.8 8.8 %collective-permute-start = (bf16[1040,128]{1,0:T(8,128)(2,1)}, bf16[1040,128]{1,0:T(8,128)(2,1)S(1)}, u32[]{:S(2)}, u32[]{:S(2)}) collective-permute-start(bf16[1040,128]{1,0:T(8,128)(2,1)} %get-tuple-element.8), channel_id=1, source_target_pairs={{0,0},{1,1},{2,2},{3,3},{4,16},{5,17},{6,18},{7,19},{8,32},{9,33},... | collective-permute-start | bytes 798728 | tf_op jit(solution)/shard_map/ppermute | solution.py:202
  12.6 3.2 %collective-permute-start.1 = (bf16[1040,128]{1,0:T(8,128)(2,1)}, bf16[1040,128]{1,0:T(8,128)(2,1)S(1)}, u32[]{:S(2)}, u32[]{:S(2)}) collective-permute-start(bf16[1040,128]{1,0:T(8,128)(2,1)} %get-tuple-element.9), channel_id=1, source_target_pairs={{0,17},{1,18},{2,19},{3,16},{4,33},{5,34},{6,35},{7,32},{8,49},{9,... | collective-permute-start | bytes 798728 | tf_op jit(solution)/shard_map/ppermute | solution.py:202
  15.9 6.3 %collective-permute-start.2 = (bf16[1040,128]{1,0:T(8,128)(2,1)}, bf16[1040,128]{1,0:T(8,128)(2,1)S(1)}, u32[]{:S(2)}, u32[]{:S(2)}) collective-permute-start(bf16[1040,128]{1,0:T(8,128)(2,1)} %get-tuple-element.10), channel_id=1, source_target_pairs={{0,34},{1,35},{2,32},{3,33},{4,50},{5,51},{6,48},{7,49},{8,2},{9,3... | collective-permute-start | bytes 798728 | tf_op jit(solution)/shard_map/ppermute | solution.py:202
  22.2 1.9 %collective-permute-start.3 = (bf16[1040,128]{1,0:T(8,128)(2,1)}, bf16[1040,128]{1,0:T(8,128)(2,1)S(1)}, u32[]{:S(2)}, u32[]{:S(2)}) collective-permute-start(bf16[1040,128]{1,0:T(8,128)(2,1)} %get-tuple-element.11), channel_id=1, source_target_pairs={{0,51},{1,48},{2,49},{3,50},{4,3},{5,0},{6,1},{7,2},{8,19},{9,16},... | collective-permute-start | bytes 798728 | tf_op jit(solution)/shard_map/ppermute | solution.py:202
  24.2 3.0 %collective-permute-done.1 = bf16[1040,128]{1,0:T(8,128)(2,1)S(1)} collective-permute-done((bf16[1040,128]{1,0:T(8,128)(2,1)}, bf16[1040,128]{1,0:T(8,128)(2,1)S(1)}, u32[]{:S(2)}, u32[]{:S(2)}) %collective-permute-start.1) | collective-permute-done | bytes 266272 | tf_op jit(solution)/shard_map/ppermute | solution.py:202
  27.2 7.1 %collective-permute-done.2 = bf16[1040,128]{1,0:T(8,128)(2,1)S(1)} collective-permute-done((bf16[1040,128]{1,0:T(8,128)(2,1)}, bf16[1040,128]{1,0:T(8,128)(2,1)S(1)}, u32[]{:S(2)}, u32[]{:S(2)}) %collective-permute-start.2) | collective-permute-done | bytes 266272 | tf_op jit(solution)/shard_map/ppermute | solution.py:202
  34.2 5.0 %collective-permute-done.3 = bf16[1040,128]{1,0:T(8,128)(2,1)S(1)} collective-permute-done((bf16[1040,128]{1,0:T(8,128)(2,1)}, bf16[1040,128]{1,0:T(8,128)(2,1)S(1)}, u32[]{:S(2)}, u32[]{:S(2)}) %collective-permute-start.3) | collective-permute-done | bytes 266272 | tf_op jit(solution)/shard_map/ppermute | solution.py:202
  39.3 1.9 %collective-permute-start.5 = (bf16[4,528,128]{2,1,0:T(8,128)(2,1)S(1)}, bf16[4,528,128]{2,1,0:T(8,128)(2,1)S(1)}, u32[]{:S(2)}, u32[]{:S(2)}) collective-permute-start(bf16[4,528,128]{2,1,0:T(8,128)(2,1)S(1)} %pad_maximum_fusion.refs_0_.refs_2_), channel_id=1, source_target_pairs={{0,32},{32,0},{1,33},{33,1},{2,34},{34,2},{3,35},{35,3},{4,36},{36... | collective-permute-start | bytes 1622024 | tf_op jit(solution)/shard_map/ppermute | solution.py:211
  41.2 1.9 %collective-permute-start.4 = (bf16[4,528,128]{2,1,0:T(8,128)(2,1)S(1)}, bf16[4,528,128]{2,1,0:T(8,128)(2,1)S(1)}, u32[]{:S(2)}, u32[]{:S(2)}) collective-permute-start(bf16[4,528,128]{2,1,0:T(8,128)(2,1)S(1)} %pad_maximum_fusion.refs_0_.refs_2_), channel_id=1, source_target_pairs={{0,16},{16,0},{1,17},{17,1},{2,18},{18,2},{3,19},{19,3},{4,20},{20... | collective-permute-start | bytes 1622024 | tf_op jit(solution)/shard_map/ppermute | solution.py:212
  43.2 1.1 broadcast_in_dim.6
  44.4 3.7 %all-to-all-start = ((bf16[4,2,512,128]{3,2,1,0:T(8,128)(2,1)}), bf16[4,2,512,128]{3,2,1,0:T(8,128)(2,1)S(1)}, u32[]{:S(2)}, u32[]{:S(2)}) async-start(bf16[4,2,512,128]{3,2,1,0:T(8,128)(2,1)} %broadcast_in_dim.6), calls=%async_computation | async-start | bytes 2097152 | tf_op jit(solution)/shard_map/all_to_all | solution.py:206
  48.1 6.0 %collective-permute-done.5.refs_2_.refs_4_ = bf16[4,528,128]{2,1,0:T(8,128)(2,1)S(1)} collective-permute-done((bf16[4,528,128]{2,1,0:T(8,128)(2,1)S(1)}, bf16[4,528,128]{2,1,0:T(8,128)(2,1)S(1)}, u32[]{:S(2)}, u32[]{:S(2)}) %collective-permute-start.5) | collective-permute-done | bytes 540704 | tf_op jit(solution)/shard_map/ppermute | solution.py:211
  54.1 1.9 %collective-permute-start.6 = (bf16[4,528,128]{2,1,0:T(8,128)(2,1)S(1)}, bf16[4,528,128]{2,1,0:T(8,128)(2,1)S(1)}, u32[]{:S(2)}, u32[]{:S(2)}) collective-permute-start(bf16[4,528,128]{2,1,0:T(8,128)(2,1)S(1)} %collective-permute-done.5.refs_2_.refs_4_), channel_id=1, source_target_pairs={{0,16},{16,0},{1,17},{17,1},{2,18},{18,2},{3,19},{19,3},{4,20},{20... | collective-permute-start | bytes 1622024 | tf_op jit(solution)/shard_map/ppermute | solution.py:216
  56.1 3.4 %collective-permute-start.9 = (bf16[2,512,128]{2,1,0:T(8,128)(2,1)S(1)}, bf16[2,512,128]{2,1,0:T(8,128)(2,1)S(1)}, u32[]{:S(2)}, u32[]{:S(2)}) collective-permute-start(bf16[2,512,128]{2,1,0:T(8,128)(2,1)S(1)} %pad_maximum_fusion.1.refs_4_.refs_6_), channel_id=1, source_target_pairs={{0,3},{1,0},{2,1},{3,2},{4,7},{5,4},{6,5},{7,6},{8,11},{9,8},{10,9... | collective-permute-start | bytes 786440 | tf_op jit(solution)/shard_map/ppermute | solution.py:215
  59.5 2.8 %collective-permute-start.8 = (bf16[2,512,128]{2,1,0:T(8,128)(2,1)S(1)}, bf16[2,512,128]{2,1,0:T(8,128)(2,1)S(1)}, u32[]{:S(2)}, u32[]{:S(2)}) collective-permute-start(bf16[2,512,128]{2,1,0:T(8,128)(2,1)S(1)} %pad_maximum_fusion.1.refs_4_.refs_6_), channel_id=1, source_target_pairs={{0,2},{1,3},{2,0},{3,1},{4,6},{5,7},{6,4},{7,5},{8,10},{9,11},{10,... | collective-permute-start | bytes 786440 | tf_op jit(solution)/shard_map/ppermute | solution.py:215
  62.3 2.5 %collective-permute-start.7 = (bf16[2,512,128]{2,1,0:T(8,128)(2,1)S(1)}, bf16[2,512,128]{2,1,0:T(8,128)(2,1)S(1)}, u32[]{:S(2)}, u32[]{:S(2)}) collective-permute-start(bf16[2,512,128]{2,1,0:T(8,128)(2,1)S(1)} %pad_maximum_fusion.1.refs_4_.refs_6_), channel_id=1, source_target_pairs={{0,1},{1,2},{2,3},{3,0},{4,5},{5,6},{6,7},{7,4},{8,9},{9,10},{10,1... | collective-permute-start | bytes 786440 | tf_op jit(solution)/shard_map/ppermute | solution.py:215
  64.9 1.8 %collective-permute-done.9.refs_7_.refs_9_ = bf16[2,512,128]{2,1,0:T(8,128)(2,1)S(1)} collective-permute-done((bf16[2,512,128]{2,1,0:T(8,128)(2,1)S(1)}, bf16[2,512,128]{2,1,0:T(8,128)(2,1)S(1)}, u32[]{:S(2)}, u32[]{:S(2)}) %collective-permute-start.9) | collective-permute-done | bytes 262176 | tf_op jit(solution)/shard_map/ppermute | solution.py:215
  66.6 3.4 %collective-permute-done.8.refs_6_.refs_8_ = bf16[2,512,128]{2,1,0:T(8,128)(2,1)S(1)} collective-permute-done((bf16[2,512,128]{2,1,0:T(8,128)(2,1)S(1)}, bf16[2,512,128]{2,1,0:T(8,128)(2,1)S(1)}, u32[]{:S(2)}, u32[]{:S(2)}) %collective-permute-start.8) | collective-permute-done | bytes 262176 | tf_op jit(solution)/shard_map/ppermute | solution.py:215
  70.0 6.7 %collective-permute-done.7.refs_5_.refs_7_ = bf16[2,512,128]{2,1,0:T(8,128)(2,1)S(1)} collective-permute-done((bf16[2,512,128]{2,1,0:T(8,128)(2,1)S(1)}, bf16[2,512,128]{2,1,0:T(8,128)(2,1)S(1)}, u32[]{:S(2)}, u32[]{:S(2)}) %collective-permute-start.7) | collective-permute-done | bytes 262176 | tf_op jit(solution)/shard_map/ppermute | solution.py:215
  76.8 0.7 copy-done.8
  77.5 0.7 copy-done.4
  78.6 0.8 copy-done.5
  79.5 8.8 %norms.1.refs_1_ = f32[1,128]{1,0:T(1,128)} custom-call(s32[3]{0:T(128)} %pad_add_fusion.pos, bf16[4,528,128]{2,1,0:T(8,128)(2,1)} %copy-done.1, bf16[4,528,128]{2,1,0:T(8,128)(2,1)} %copy-done.4, bf16[4,528,128]{2,1,0:T(8,128)(2,1)} %copy-done.3, bf16[4,528,128]{2,1,0:T(8,128)(2,1)} %copy-done.5, bf16[2,512,128]{2,1,0:T(8,128)(2,1)} %copy-done.2, ...), custom_call_target="tpu_custom_call" | custom-call | tf_op jit(solution)/shard_map/norms/pallas_call | solution.py:228
  88.9 8.9 %all_to_all.15.refs_0_ = f32[16,1,128]{2,1,0:T(1,128)} all-to-all(f32[16,1,128]{2,1,0:T(1,128)S(1)} %broadcast_in_dim.7), channel_id=1, replica_groups=mesh['zh'=4,'zl'=2,'yl'=2,'c'=2,'yh'=4,'x'=4] {'yl','c','x'}, dimensions={0} | all-to-all | bytes 16384 | tf_op jit(solution)/shard_map/all_to_all | solution.py:237
  97.8 6.3 %grads.1 = (f32[8,4,72,128]{3,2,1,0:T(8,128)}, f32[1,128]{1,0:T(1,128)}) custom-call(s32[3]{0:T(128)} %pad_add_fusion.pos, f32[16,1,128]{2,1,0:T(1,128)} %all_to_all.15.refs_0_, f32[1,128]{1,0:T(1,128)} %norms.1.refs_1_, bf16[4,528,128]{2,1,0:T(8,128)(2,1)} %copy-done.1, bf16[4,528,128]{2,1,0:T(8,128)(2,1)} %copy-done.4, bf16[4,528,128]{2,1,0:T(8,128)(2,1)} %copy-done.3, ...), custom_call_target="tpu_custom_call" | custom-call | tf_op jit(solution)/shard_map/grads/pallas_call | solution.py:240
  104.1 2.2 %convert_element_type.6 = f16[8,4,72,128]{3,2,1,0:T(8,128)(2,1)} convert(f32[8,4,72,128]{3,2,1,0:T(8,128)} %get-tuple-element.12) | non-fusion elementwise | flops 294912 | bytes 1769472 | tf_op jit(solution)/shard_map/convert_element_type | solution.py:249
  106.3 14.8 %all-to-all-start.2 = ((f16[32,72,128]{2,1,0:T(8,128)(2,1)}), f16[32,72,128]{2,1,0:T(8,128)(2,1)S(1)}, u32[]{:S(2)}, u32[]{:S(2)}) async-start(f16[32,72,128]{2,1,0:T(8,128)(2,1)} %bitcast.14), calls=%async_computation.2 | async-start | bytes 1179648 | tf_op jit(solution)/shard_map/all_to_all | solution.py:250
  121.1 5.3 %collective-permute-start.10 = (f32[1,128]{1,0:T(1,128)S(1)}, f32[1,128]{1,0:T(1,128)S(1)}, u32[]{:S(2)}, u32[]{:S(2)}) collective-permute-start(f32[1,128]{1,0:T(1,128)S(1)} %copy-done.9), channel_id=1, source_target_pairs={{0,0},{1,1},{2,2},{3,3},{16,4},{17,5},{18,6},{19,7},{32,8},{33,9},... | collective-permute-start | bytes 1544 | tf_op jit(solution)/shard_map/ppermute | solution.py:253
  126.5 13.0 %collective-permute-done.10 = f32[1,128]{1,0:T(1,128)S(1)} collective-permute-done((f32[1,128]{1,0:T(1,128)S(1)}, f32[1,128]{1,0:T(1,128)S(1)}, u32[]{:S(2)}, u32[]{:S(2)}) %collective-permute-start.10) | collective-permute-done | bytes 544 | tf_op jit(solution)/shard_map/ppermute | solution.py:253
  140.1 0.7 fusion
  (37 shorter events, 2.4 us)
Async XLA Ops:
  3.8 20.3 %collective-permute-start = (bf16[1040,128]{1,0:T(8,128)(2,1)}, bf16[1040,128]{1,0:T(8,128)(2,1)S(1)}, u32[]{:S(2)}, u32[]{:S(2)}) collective-permute-start(bf16[1040,128]{1,0:T(8,128)(2,1)} %get-tuple-element.8), channel_id=1, source_target_pairs={{0,0},{1,1},{2,2},{3,3},{4,16},{5,17},{6,18},{7,19},{8,32},{9,33},... | collective-permute-start | bytes 798728 | tf_op jit(solution)/shard_map/ppermute | solution.py:202
  12.6 14.5 %collective-permute-start.1 = (bf16[1040,128]{1,0:T(8,128)(2,1)}, bf16[1040,128]{1,0:T(8,128)(2,1)S(1)}, u32[]{:S(2)}, u32[]{:S(2)}) collective-permute-start(bf16[1040,128]{1,0:T(8,128)(2,1)} %get-tuple-element.9), channel_id=1, source_target_pairs={{0,17},{1,18},{2,19},{3,16},{4,33},{5,34},{6,35},{7,32},{8,49},{9,... | collective-permute-start | bytes 798728 | tf_op jit(solution)/shard_map/ppermute | solution.py:202
  15.9 18.3 %collective-permute-start.2 = (bf16[1040,128]{1,0:T(8,128)(2,1)}, bf16[1040,128]{1,0:T(8,128)(2,1)S(1)}, u32[]{:S(2)}, u32[]{:S(2)}) collective-permute-start(bf16[1040,128]{1,0:T(8,128)(2,1)} %get-tuple-element.10), channel_id=1, source_target_pairs={{0,34},{1,35},{2,32},{3,33},{4,50},{5,51},{6,48},{7,49},{8,2},{9,3... | collective-permute-start | bytes 798728 | tf_op jit(solution)/shard_map/ppermute | solution.py:202
  22.2 17.0 %collective-permute-start.3 = (bf16[1040,128]{1,0:T(8,128)(2,1)}, bf16[1040,128]{1,0:T(8,128)(2,1)S(1)}, u32[]{:S(2)}, u32[]{:S(2)}) collective-permute-start(bf16[1040,128]{1,0:T(8,128)(2,1)} %get-tuple-element.11), channel_id=1, source_target_pairs={{0,51},{1,48},{2,49},{3,50},{4,3},{5,0},{6,1},{7,2},{8,19},{9,16},... | collective-permute-start | bytes 798728 | tf_op jit(solution)/shard_map/ppermute | solution.py:202
  39.3 5.1 %copy-start.1 = (bf16[4,528,128]{2,1,0:T(8,128)(2,1)}, bf16[4,528,128]{2,1,0:T(8,128)(2,1)S(1)}, u32[]{:S(2)}) copy-start(bf16[4,528,128]{2,1,0:T(8,128)(2,1)S(1)} %pad_maximum_fusion.refs_0_.refs_2_) | copy-start | bytes 1622020
  39.3 14.8 %collective-permute-start.5 = (bf16[4,528,128]{2,1,0:T(8,128)(2,1)S(1)}, bf16[4,528,128]{2,1,0:T(8,128)(2,1)S(1)}, u32[]{:S(2)}, u32[]{:S(2)}) collective-permute-start(bf16[4,528,128]{2,1,0:T(8,128)(2,1)S(1)} %pad_maximum_fusion.refs_0_.refs_2_), channel_id=1, source_target_pairs={{0,32},{32,0},{1,33},{33,1},{2,34},{34,2},{3,35},{35,3},{4,36},{36... | collective-permute-start | bytes 1622024 | tf_op jit(solution)/shard_map/ppermute | solution.py:211
  41.2 36.3 %collective-permute-start.4 = (bf16[4,528,128]{2,1,0:T(8,128)(2,1)S(1)}, bf16[4,528,128]{2,1,0:T(8,128)(2,1)S(1)}, u32[]{:S(2)}, u32[]{:S(2)}) collective-permute-start(bf16[4,528,128]{2,1,0:T(8,128)(2,1)S(1)} %pad_maximum_fusion.refs_0_.refs_2_), channel_id=1, source_target_pairs={{0,16},{16,0},{1,17},{17,1},{2,18},{18,2},{3,19},{19,3},{4,20},{20... | collective-permute-start | bytes 1622024 | tf_op jit(solution)/shard_map/ppermute | solution.py:212
  44.4 33.1 %all-to-all-start = ((bf16[4,2,512,128]{3,2,1,0:T(8,128)(2,1)}), bf16[4,2,512,128]{3,2,1,0:T(8,128)(2,1)S(1)}, u32[]{:S(2)}, u32[]{:S(2)}) async-start(bf16[4,2,512,128]{3,2,1,0:T(8,128)(2,1)} %broadcast_in_dim.6), calls=%async_computation | async-start | bytes 2097152 | tf_op jit(solution)/shard_map/all_to_all | solution.py:206
  54.1 23.4 %copy-start.3 = (bf16[4,528,128]{2,1,0:T(8,128)(2,1)}, bf16[4,528,128]{2,1,0:T(8,128)(2,1)S(1)}, u32[]{:S(2)}) copy-start(bf16[4,528,128]{2,1,0:T(8,128)(2,1)S(1)} %collective-permute-done.5.refs_2_.refs_4_) | copy-start | bytes 1622020
  54.1 23.4 %collective-permute-start.6 = (bf16[4,528,128]{2,1,0:T(8,128)(2,1)S(1)}, bf16[4,528,128]{2,1,0:T(8,128)(2,1)S(1)}, u32[]{:S(2)}, u32[]{:S(2)}) collective-permute-start(bf16[4,528,128]{2,1,0:T(8,128)(2,1)S(1)} %collective-permute-done.5.refs_2_.refs_4_), channel_id=1, source_target_pairs={{0,16},{16,0},{1,17},{17,1},{2,18},{18,2},{3,19},{19,3},{4,20},{20... | collective-permute-start | bytes 1622024 | tf_op jit(solution)/shard_map/ppermute | solution.py:216
  56.1 21.5 %copy-start.2 = (bf16[2,512,128]{2,1,0:T(8,128)(2,1)}, bf16[2,512,128]{2,1,0:T(8,128)(2,1)S(1)}, u32[]{:S(2)}) copy-start(bf16[2,512,128]{2,1,0:T(8,128)(2,1)S(1)} %pad_maximum_fusion.1.refs_4_.refs_6_) | copy-start | bytes 786436
  56.1 10.5 %collective-permute-start.9 = (bf16[2,512,128]{2,1,0:T(8,128)(2,1)S(1)}, bf16[2,512,128]{2,1,0:T(8,128)(2,1)S(1)}, u32[]{:S(2)}, u32[]{:S(2)}) collective-permute-start(bf16[2,512,128]{2,1,0:T(8,128)(2,1)S(1)} %pad_maximum_fusion.1.refs_4_.refs_6_), channel_id=1, source_target_pairs={{0,3},{1,0},{2,1},{3,2},{4,7},{5,4},{6,5},{7,6},{8,11},{9,8},{10,9... | collective-permute-start | bytes 786440 | tf_op jit(solution)/shard_map/ppermute | solution.py:215
  59.5 10.5 %collective-permute-start.8 = (bf16[2,512,128]{2,1,0:T(8,128)(2,1)S(1)}, bf16[2,512,128]{2,1,0:T(8,128)(2,1)S(1)}, u32[]{:S(2)}, u32[]{:S(2)}) collective-permute-start(bf16[2,512,128]{2,1,0:T(8,128)(2,1)S(1)} %pad_maximum_fusion.1.refs_4_.refs_6_), channel_id=1, source_target_pairs={{0,2},{1,3},{2,0},{3,1},{4,6},{5,7},{6,4},{7,5},{8,10},{9,11},{10,... | collective-permute-start | bytes 786440 | tf_op jit(solution)/shard_map/ppermute | solution.py:215
  62.3 14.4 %collective-permute-start.7 = (bf16[2,512,128]{2,1,0:T(8,128)(2,1)S(1)}, bf16[2,512,128]{2,1,0:T(8,128)(2,1)S(1)}, u32[]{:S(2)}, u32[]{:S(2)}) collective-permute-start(bf16[2,512,128]{2,1,0:T(8,128)(2,1)S(1)} %pad_maximum_fusion.1.refs_4_.refs_6_), channel_id=1, source_target_pairs={{0,1},{1,2},{2,3},{3,0},{4,5},{5,6},{6,7},{7,4},{8,9},{9,10},{10,1... | collective-permute-start | bytes 786440 | tf_op jit(solution)/shard_map/ppermute | solution.py:215
  66.6 10.1 %copy-start.6 = (bf16[2,512,128]{2,1,0:T(8,128)(2,1)}, bf16[2,512,128]{2,1,0:T(8,128)(2,1)S(1)}, u32[]{:S(2)}) copy-start(bf16[2,512,128]{2,1,0:T(8,128)(2,1)S(1)} %collective-permute-done.9.refs_7_.refs_9_) | copy-start | bytes 786436
  70.0 6.7 %copy-start.7 = (bf16[2,512,128]{2,1,0:T(8,128)(2,1)}, bf16[2,512,128]{2,1,0:T(8,128)(2,1)S(1)}, u32[]{:S(2)}) copy-start(bf16[2,512,128]{2,1,0:T(8,128)(2,1)S(1)} %collective-permute-done.8.refs_6_.refs_8_) | copy-start | bytes 786436
  76.8 0.7 copy-start.8
  77.5 0.8 copy-start.4
  77.5 1.2 copy-start
  78.6 0.8 copy-start.5
  104.1 17.0 %copy-start.9 = (f32[1,128]{1,0:T(1,128)S(1)}, f32[1,128]{1,0:T(1,128)}, u32[]{:S(2)}) copy-start(f32[1,128]{1,0:T(1,128)} %get-tuple-element.13) | copy-start | bytes 1540
  106.3 33.7 %all-to-all-start.2 = ((f16[32,72,128]{2,1,0:T(8,128)(2,1)}), f16[32,72,128]{2,1,0:T(8,128)(2,1)S(1)}, u32[]{:S(2)}, u32[]{:S(2)}) async-start(f16[32,72,128]{2,1,0:T(8,128)(2,1)} %bitcast.14), calls=%async_computation.2 | async-start | bytes 1179648 | tf_op jit(solution)/shard_map/all_to_all | solution.py:250
  121.1 18.3 %collective-permute-start.10 = (f32[1,128]{1,0:T(1,128)S(1)}, f32[1,128]{1,0:T(1,128)S(1)}, u32[]{:S(2)}, u32[]{:S(2)}) collective-permute-start(f32[1,128]{1,0:T(1,128)S(1)} %copy-done.9), channel_id=1, source_target_pairs={{0,0},{1,1},{2,2},{3,3},{16,4},{17,5},{18,6},{19,7},{32,8},{33,9},... | collective-permute-start | bytes 1544 | tf_op jit(solution)/shard_map/ppermute | solution.py:253
where the time goes:
time: 144 us; the launch traced here: 141 us
  starting transfers between devices  58.7 us (41%)
  waiting for transfers between devices  46.4 us (32%)
  Pallas kernels  17.6 us (12%)
  blocking collectives  8.91 us (6%)
  local copies, waits for them, and re-layouts  5.07 us (4%)
  other arithmetic  3.78 us (3%)
    ppermute x4, starting transfers between devices, body(): lax.ppermute(payload[k], MOVE, table(sizes, MOVE, functools.partial(to_gr...  20.3 us
    ppermute x4, waiting for transfers between devices, body(): lax.ppermute(payload[k], MOVE, table(sizes, MOVE, functools.partial(to_gr...  15 us
    all_to_all x1, starting transfers between devices, body(): lax.all_to_all(pieces, SUMMED, split_axis=0, concat_axis=0, tiled=True)  14.8 us
    ppermute x1, waiting for transfers between devices, body(): clip = lax.ppermute(clip, MOVE, home)  13 us
    ppermute x3, waiting for transfers between devices, body(): lax.ppermute(own_g, 'x', [(s, (s + m) % 4) for s in range(4)])  11.9 us
    all_to_all x1, blocking collectives, body(): lax.all_to_all(jnp.broadcast_to(partial, (16, 1, BLOCK)), GROUP, split_ax...  8.91 us
    pallas_call x1, Pallas kernels, body(): pl.pallas_call(norm_kernel, out_shape=row, in_specs=[smem] + [anywhere] *...  8.77 us
    ppermute x3, starting transfers between devices, body(): lax.ppermute(own_g, 'x', [(s, (s + m) % 4) for s in range(4)])  8.76 us
  transfers between devices with their start and end apart: 13, of which 9 were waited for; matrix products, arithmetic and copies ran while one was open for 1% of the time, Pallas kernels for 0%

commit v1 on v0

--- a/solution.py
+++ b/solution.py
@@ -20,6 +20,7 @@
 TAIL = 8
 PAD = 16
 
+ORDER = (1, 3, 0, 2)
 AXES = ("zh", "zl", "yl", "c", "yh", "x")
 MOVE = ("yl", "c", "yh", "x")
 GROUP = ("yl", "c", "x")
@@ -41,9 +42,9 @@
     return dict(yl=j // 2, c=j % 2, yh=c * 2 + yl, x=(x + k) % 4)
 
 
-def prep_kernel(pos, ids_ref, a_ref, g_ref, *rest):
+def prep_kernel(ids_ref, a_ref, g_ref, *rest):
     outs, gt_ref = rest[:4], rest[4]
-    x, yh = pos[0], pos[1]
+    x, yh = lax.axis_index("x"), lax.axis_index("yh")
     chunks = g_ref.shape[1] // BLOCK
     ids = ids_ref[...]
     kept = ids >= 0
@@ -53,43 +54,51 @@
         t = g_ref[:, n * BLOCK : (n + 1) * BLOCK].astype(jnp.float32).T
         gt_ref[n * BLOCK : (n + 1) * BLOCK, :] = jnp.where(kept, t, 0.0).astype(jnp.bfloat16)
     wide = chunks * BLOCK // 4
-    for k in range(4):
+    for n, k in enumerate(ORDER):
         i = (x + k) % 4
         j = (yh + k) % 4
         for z in range(wide // COLS):
             at = pl.multiple_of((z * 4 + j) * COLS, COLS)
-            outs[k][z * COLS : (z + 1) * COLS, :] = gt_ref[pl.ds(at, COLS), :]
+            outs[n][z * COLS : (z + 1) * COLS, :] = gt_ref[pl.ds(at, COLS), :]
         for r in range(4):
             at = pl.multiple_of((r * 4 + i) * BLOCK, BLOCK)
-            outs[k][wide + r * BLOCK : wide + (r + 1) * BLOCK, :] = a_ref[:, pl.ds(at, BLOCK)]
-        outs[k][wide + PART :, :] = doc
-
-
-def fetch(pos, parts, a_s, g_s, doc_s, sems):
-    x, j = pos[0], pos[2]
+            outs[n][wide + r * BLOCK : wide + (r + 1) * BLOCK, :] = a_ref[:, pl.ds(at, BLOCK)]
+        outs[n][wide + PART :, :] = doc
+
+
+def fetch(parts, a_s, g_s, doc_s, sems):
+    x, j = lax.axis_index("x"), lax.axis_index("yl") * 2 + lax.axis_index("c")
     copies = []
 
     def copy(src, dst):
         copies.append(pltpu.make_async_copy(src, dst, sems.at[len(copies)]))
 
-    for k in range(4):
+    def slab(j, k, x):
+        return (j + 4 - k) % 4 * 4 + (x + 4 - k) % 4
+
+    for n, k in enumerate(ORDER):
         for m in range(4):
-            t = ((j ^ m) + 4 - k) % 4 * 4 + (x + 4 - k) % 4
-            at = pl.multiple_of(t * BLOCK, BLOCK)
+            copy(parts[m].at[n, PART:], doc_s.at[slab(j ^ m, k, x)])
+    for n, k in enumerate(ORDER):
+        for m in range(4):
+            if n < 2:
+                src, sender = parts[4 + m].at[n], (x + 4 - m) % 4
+            else:
+                src, sender = parts[8].at[m, n - 2], m
+            at = pl.multiple_of(slab(j, k, sender) * BLOCK, BLOCK)
+            copy(src, g_s.at[:, pl.ds(at, BLOCK)])
+    for n, k in enumerate(ORDER):
+        for m in range(4):
+            at = pl.multiple_of(slab(j ^ m, k, x) * BLOCK, BLOCK)
             for r in range(4):
                 rows = slice(r * BLOCK, (r + 1) * BLOCK)
-                copy(parts[m].at[k, rows], a_s.at[pl.ds(at, BLOCK), rows])
-            copy(parts[m].at[k, PART:], doc_s.at[t])
-        for m in range(4):
-            if k < 2:
-                src, sender = parts[4 + m].at[k], (x + 4 - m) % 4
-            else:
-                src, sender = parts[8].at[m, k - 2], m
-            t = (j + 4 - k) % 4 * 4 + (sender + 4 - k) % 4
-            at = pl.multiple_of(t * BLOCK, BLOCK)
-            copy(src, g_s.at[:, pl.ds(at, BLOCK)])
+                copy(parts[m].at[n, rows], a_s.at[pl.ds(at, BLOCK), rows])
     for cp in copies:
         cp.start()
+    return copies[:16], copies[16:32], copies[32:]
+
+
+def wait(copies):
     for cp in copies:
         cp.wait()
 
@@ -97,11 +106,12 @@
 COPIES = 16 * 6
 
 
-def norm_kernel(pos, *refs):
-    parts, out, a_s, g_s, doc_s, acc, starts, sems = refs[:9], *refs[9:]
-    fetch(pos, parts, a_s, g_s, doc_s, sems)
+def norm_kernel(*refs):
+    parts, out, a_s, g_s, doc_s, acc, starts, norms, sems = refs[:9], *refs[9:]
+    docs, grads, acts = fetch(parts, a_s, g_s, doc_s, sems)
     a_s[SLABS * BLOCK :, :] = jnp.zeros((BLOCK, a_s.shape[1]), a_s.dtype)
-    out[...] = jnp.zeros_like(out)
+    norms[...] = jnp.zeros_like(norms)
+    wait(docs)
     doc = jnp.int32(-1)
     for t in range(SLABS):
         here = jnp.maximum(doc, jnp.max(doc_s[t].astype(jnp.float32)).astype(jnp.int32))
@@ -113,6 +123,8 @@
 
         doc = here
     starts[DOCS] = SLABS
+    wait(grads)
+    wait(acts)
     lane = lax.broadcasted_iota(jnp.int32, (1, BLOCK), 1)
     second = lax.broadcasted_iota(jnp.int32, (1, 2 * BLOCK), 1) >= BLOCK
 
@@ -124,7 +136,7 @@
 
     def squared(w, d):
         total = jnp.sum(jnp.sum(w * w, axis=0, keepdims=True), axis=1, keepdims=True)
-        out[...] = jnp.where(lane == d, total, out[...])
+        norms[...] = jnp.where(lane == d, total, norms[...])
 
     def document(d, carry):
         first, end = starts[d], starts[d + 1]
@@ -147,24 +159,28 @@
         return carry
 
     lax.fori_loop(0, DOCS, document, 0)
-
-
-def grad_kernel(pos, *refs):
+    out[...] = jnp.broadcast_to(norms[...][None], out.shape)
+
+
+def grad_kernel(*refs):
     norms, own, parts = refs[0], refs[1], refs[2:11]
     out, clip_out, a_s, g_s, doc_s, acc, sems = refs[11:]
-    fetch(pos, parts, a_s, g_s, doc_s, sems)
+    docs, grads, acts = fetch(parts, a_s, g_s, doc_s, sems)
     norm_sq = jnp.sum(norms[...], axis=0)
     clip = CLIP / jnp.sqrt(jnp.maximum(norm_sq, CLIP * CLIP))
     clip_out[...] = clip
-    bound = jnp.sum(jnp.minimum(jnp.sqrt(own[...]), CLIP), axis=1, keepdims=True)
+    bound = jnp.sum(jnp.minimum(jnp.sqrt(own[0]), CLIP), axis=1, keepdims=True)
     shift = jnp.ceil(jnp.log2(jnp.maximum(bound, 1e-18))) - 14.0
     lane = lax.broadcasted_iota(jnp.int32, (1, BLOCK), 1).astype(jnp.float32)
+    wait(docs)
+    wait(grads)
     for t in range(SLABS):
         here = doc_s[t, 0:1, :].astype(jnp.float32) == lane
         factor = jnp.sum(jnp.where(here, clip, 0.0), axis=1, keepdims=True)
         g = g_s[:, t * BLOCK : (t + 1) * BLOCK].astype(jnp.float32)
         g_s[:, t * BLOCK : (t + 1) * BLOCK] = (g * factor).astype(jnp.bfloat16)
     tokens = SLABS * BLOCK
+    wait(acts)
     acc[...] = jnp.dot(g_s[:, :tokens], a_s[:tokens, :], preferred_element_type=jnp.float32)
     scale = jnp.exp2(-shift)
     tail = jnp.broadcast_to(shift, (TAIL, BLOCK))
@@ -180,26 +196,22 @@
     levels = sizes["zh"] * sizes["zl"]
     wide = levels * COLS
     bf16, f32 = jnp.bfloat16, jnp.float32
-    x = lax.axis_index("x")
-    yh = lax.axis_index("yh")
-    j = lax.axis_index("yl") * 2 + lax.axis_index("c")
-    pos = jnp.stack([x, yh, j]).astype(jnp.int32)
-    smem = pl.BlockSpec(memory_space=pltpu.SMEM)
     vmem = pl.BlockSpec(memory_space=pltpu.VMEM)
     anywhere = pl.BlockSpec(memory_space=pl.ANY)
 
     payload = pl.pallas_call(
         prep_kernel,
         out_shape=[jax.ShapeDtypeStruct((wide + PART + PAD, BLOCK), bf16)] * 4,
-        in_specs=[smem, vmem, vmem, vmem],
+        in_specs=[vmem, vmem, vmem],
         out_specs=[vmem] * 4,
         scratch_shapes=[pltpu.VMEM((g.shape[1], BLOCK), bf16)],
         interpret=INTERPRET,
         name="prep",
-    )(pos, ids, a, g)
+    )(ids, a, g)
 
     arrived = [
-        lax.ppermute(payload[k], MOVE, table(sizes, MOVE, functools.partial(to_group, k))) for k in range(4)
+        lax.ppermute(payload[n], MOVE, table(sizes, MOVE, functools.partial(to_group, k)))
+        for n, k in enumerate(ORDER)
     ]
     flip = [(0, 1), (1, 0)]
     last_g = jnp.stack([p[:wide] for p in arrived[2:]])
@@ -227,25 +239,23 @@
     row = jax.ShapeDtypeStruct((1, BLOCK), f32)
     partial = pl.pallas_call(
         norm_kernel,
-        out_shape=row,
-        in_specs=[smem] + [anywhere] * 9,
+        out_shape=jax.ShapeDtypeStruct((16, 1, BLOCK), f32),
+        in_specs=[anywhere] * 9,
         out_specs=vmem,
-        scratch_shapes=stores + [pltpu.SMEM((DOCS + 1,), jnp.int32)] + sems,
+        scratch_shapes=stores + [pltpu.SMEM((DOCS + 1,), jnp.int32), pltpu.VMEM((1, BLOCK), f32)] + sems,
         interpret=INTERPRET,
         name="norms",
-    )(pos, *parts)
-    norms = lax.all_to_all(
-        jnp.broadcast_to(partial, (16, 1, BLOCK)), GROUP, split_axis=0, concat_axis=0, tiled=True
-    )
+    )(*parts)
+    norms = lax.all_to_all(partial, GROUP, split_axis=0, concat_axis=0, tiled=True)
     pieces, clip = pl.pallas_call(
         grad_kernel,
         out_shape=[jax.ShapeDtypeStruct((levels, 4, COLS + TAIL, BLOCK), f32), row],
-        in_specs=[smem, vmem, vmem] + [anywhere] * 9,
+        in_specs=[vmem, vmem] + [anywhere] * 9,
         out_specs=[vmem] * 2,
         scratch_shapes=stores + sems,
         interpret=INTERPRET,
         name="grads",
-    )(pos, norms, partial, *parts)
+    )(norms, partial, *parts)
     pieces = pieces.astype(jnp.float16).reshape(levels * 4, COLS + TAIL, BLOCK)
     summands = lax.all_to_all(pieces, SUMMED, split_axis=0, concat_axis=0, tiled=True).astype(f32)
     weight_grad = jnp.sum(summands[:, :COLS] * jnp.exp2(summands[:, COLS : COLS + 1]), axis=0).T

time: 144 us -> 144 us (level)
  starting transfers between devices: 58.7 us -> 66.2 us
  waiting for transfers between devices: 46.4 us -> 40.2 us
    ppermute x1, waiting for transfers between devices: 6 us -> 2.09 us  [body(): partner = lax.ppermute(own_a, 'yl', flip)]
    ppermute x1, starting transfers between devices: 1.91 us -> 5.17 us  [body(): partner_other = lax.ppermute(partner, 'c', flip)]
    ppermute x1, starting transfers between devices: 1.92 us -> 4.54 us  [body(): own_other = lax.ppermute(own_a, 'c', flip)]
    ppermute x4, waiting for transfers between devices: 15 us -> 13.1 us  [body(): lax.ppermute(payload[n], MOVE, table(sizes, MOVE, functools.partial(to_gr...]
    ppermute x4, starting transfers between devices: 20.3 us -> 21.9 us  [body(): lax.ppermute(payload[n], MOVE, table(sizes, MOVE, functools.partial(to_gr...]
where the time goes in v1:
time: 144 us; the launch traced here: 141 us
  starting transfers between devices  66.2 us (46%)
  waiting for transfers between devices  40.2 us (28%)
  Pallas kernels  16.7 us (12%)
  blocking collectives  9.73 us (7%)
  local copies, waits for them, and re-layouts  4.41 us (3%)
  other arithmetic  3.11 us (2%)
    ppermute x4, starting transfers between devices, body(): lax.ppermute(payload[n], MOVE, table(sizes, MOVE, functools.partial(to_gr...  21.9 us
    all_to_all x1, starting transfers between devices, body(): lax.all_to_all(pieces, SUMMED, split_axis=0, concat_axis=0, tiled=True)  15 us
    ppermute x4, waiting for transfers between devices, body(): lax.ppermute(payload[n], MOVE, table(sizes, MOVE, functools.partial(to_gr...  13.1 us
    ppermute x1, waiting for transfers between devices, body(): clip = lax.ppermute(clip, MOVE, home)  12.9 us
    ppermute x3, waiting for transfers between devices, body(): lax.ppermute(own_g, 'x', [(s, (s + m) % 4) for s in range(4)])  11.4 us
    all_to_all x1, blocking collectives, body(): lax.all_to_all(partial, GROUP, split_axis=0, concat_axis=0, tiled=True)  9.73 us
    ppermute x3, starting transfers between devices, body(): lax.ppermute(own_g, 'x', [(s, (s + m) % 4) for s in range(4)])  8.84 us
    pallas_call x1, Pallas kernels, body(): pl.pallas_call(norm_kernel, out_shape=jax.ShapeDtypeStruct((16, 1, BLOCK)...  7.87 us
  transfers between devices with their start and end apart: 13, of which 9 were waited for; matrix products, arithmetic and copies ran while one was open for 1% of the time, Pallas kernels for 0%

profile of v1, /device:TPU:1, one launch (start us, length us, event | category | flops | bytes accessed | tf_op | source)
XLA Modules:
  0.0 141.3 jit_solution(7299647358948630573)
XLA Ops:
  0.6 2.5 %prep.1 = (bf16[1040,128]{1,0:T(8,128)(2,1)}, bf16[1040,128]{1,0:T(8,128)(2,1)}, bf16[1040,128]{1,0:T(8,128)(2,1)}, bf16[1040,128]{1,0:T(8,128)(2,1)}) custom-call(s32[1,128]{1,0:T(1,128)} %ids_ref.1, bf16[128,2048]{1,0:T(8,128)(2,1)} %bitcast.22, bf16[128,2048]{1,0:T(8,128)(2,1)} %bitcast.23), custom_call_target="tpu_custom_call" | custom-call | tf_op jit(solution)/shard_map/prep/pallas_call | solution.py:202
  3.1 9.2 %collective-permute-start = (bf16[1040,128]{1,0:T(8,128)(2,1)}, bf16[1040,128]{1,0:T(8,128)(2,1)S(1)}, u32[]{:S(2)}, u32[]{:S(2)}) collective-permute-start(bf16[1040,128]{1,0:T(8,128)(2,1)} %get-tuple-element.8), channel_id=1, source_target_pairs={{0,17},{1,18},{2,19},{3,16},{4,33},{5,34},{6,35},{7,32},{8,49},{9,... | collective-permute-start | bytes 798728 | tf_op jit(solution)/shard_map/ppermute | solution.py:213
  12.3 2.8 %collective-permute-start.1 = (bf16[1040,128]{1,0:T(8,128)(2,1)}, bf16[1040,128]{1,0:T(8,128)(2,1)S(1)}, u32[]{:S(2)}, u32[]{:S(2)}) collective-permute-start(bf16[1040,128]{1,0:T(8,128)(2,1)} %get-tuple-element.9), channel_id=1, source_target_pairs={{0,51},{1,48},{2,49},{3,50},{4,3},{5,0},{6,1},{7,2},{8,19},{9,16},... | collective-permute-start | bytes 798728 | tf_op jit(solution)/shard_map/ppermute | solution.py:213
  15.2 7.8 %collective-permute-start.2 = (bf16[1040,128]{1,0:T(8,128)(2,1)}, bf16[1040,128]{1,0:T(8,128)(2,1)S(1)}, u32[]{:S(2)}, u32[]{:S(2)}) collective-permute-start(bf16[1040,128]{1,0:T(8,128)(2,1)} %get-tuple-element.10), channel_id=1, source_target_pairs={{0,0},{1,1},{2,2},{3,3},{4,16},{5,17},{6,18},{7,19},{8,32},{9,33},... | collective-permute-start | bytes 798728 | tf_op jit(solution)/shard_map/ppermute | solution.py:213
  23.0 2.0 %collective-permute-start.3 = (bf16[1040,128]{1,0:T(8,128)(2,1)}, bf16[1040,128]{1,0:T(8,128)(2,1)S(1)}, u32[]{:S(2)}, u32[]{:S(2)}) collective-permute-start(bf16[1040,128]{1,0:T(8,128)(2,1)} %get-tuple-element.11), channel_id=1, source_target_pairs={{0,34},{1,35},{2,32},{3,33},{4,50},{5,51},{6,48},{7,49},{8,2},{9,3... | collective-permute-start | bytes 798728 | tf_op jit(solution)/shard_map/ppermute | solution.py:213
  25.1 4.8 %collective-permute-done.1 = bf16[1040,128]{1,0:T(8,128)(2,1)S(1)} collective-permute-done((bf16[1040,128]{1,0:T(8,128)(2,1)}, bf16[1040,128]{1,0:T(8,128)(2,1)S(1)}, u32[]{:S(2)}, u32[]{:S(2)}) %collective-permute-start.1) | collective-permute-done | bytes 266272 | tf_op jit(solution)/shard_map/ppermute | solution.py:213
  29.9 1.6 %collective-permute-done.2 = bf16[1040,128]{1,0:T(8,128)(2,1)S(1)} collective-permute-done((bf16[1040,128]{1,0:T(8,128)(2,1)}, bf16[1040,128]{1,0:T(8,128)(2,1)S(1)}, u32[]{:S(2)}, u32[]{:S(2)}) %collective-permute-start.2) | collective-permute-done | bytes 266272 | tf_op jit(solution)/shard_map/ppermute | solution.py:213
  31.5 6.8 %collective-permute-done.3 = bf16[1040,128]{1,0:T(8,128)(2,1)S(1)} collective-permute-done((bf16[1040,128]{1,0:T(8,128)(2,1)}, bf16[1040,128]{1,0:T(8,128)(2,1)S(1)}, u32[]{:S(2)}, u32[]{:S(2)}) %collective-permute-start.3) | collective-permute-done | bytes 266272 | tf_op jit(solution)/shard_map/ppermute | solution.py:213
  38.4 1.9 %collective-permute-start.5 = (bf16[4,528,128]{2,1,0:T(8,128)(2,1)S(1)}, bf16[4,528,128]{2,1,0:T(8,128)(2,1)S(1)}, u32[]{:S(2)}, u32[]{:S(2)}) collective-permute-start(bf16[4,528,128]{2,1,0:T(8,128)(2,1)S(1)} %pad_maximum_fusion.refs_0_.refs_2_), channel_id=1, source_target_pairs={{0,32},{32,0},{1,33},{33,1},{2,34},{34,2},{3,35},{35,3},{4,36},{36... | collective-permute-start | bytes 1622024 | tf_op jit(solution)/shard_map/ppermute | solution.py:223
  40.3 4.5 %collective-permute-start.4 = (bf16[4,528,128]{2,1,0:T(8,128)(2,1)S(1)}, bf16[4,528,128]{2,1,0:T(8,128)(2,1)S(1)}, u32[]{:S(2)}, u32[]{:S(2)}) collective-permute-start(bf16[4,528,128]{2,1,0:T(8,128)(2,1)S(1)} %pad_maximum_fusion.refs_0_.refs_2_), channel_id=1, source_target_pairs={{0,16},{16,0},{1,17},{17,1},{2,18},{18,2},{3,19},{19,3},{4,20},{20... | collective-permute-start | bytes 1622024 | tf_op jit(solution)/shard_map/ppermute | solution.py:224
  44.9 1.1 broadcast_in_dim.3
  46.0 3.5 %all-to-all-start = ((bf16[4,2,512,128]{3,2,1,0:T(8,128)(2,1)}), bf16[4,2,512,128]{3,2,1,0:T(8,128)(2,1)S(1)}, u32[]{:S(2)}, u32[]{:S(2)}) async-start(bf16[4,2,512,128]{3,2,1,0:T(8,128)(2,1)} %broadcast_in_dim.3), calls=%async_computation | async-start | bytes 2097152 | tf_op jit(solution)/shard_map/all_to_all | solution.py:218
  49.6 2.1 %collective-permute-done.5.refs_2_.refs_4_ = bf16[4,528,128]{2,1,0:T(8,128)(2,1)S(1)} collective-permute-done((bf16[4,528,128]{2,1,0:T(8,128)(2,1)S(1)}, bf16[4,528,128]{2,1,0:T(8,128)(2,1)S(1)}, u32[]{:S(2)}, u32[]{:S(2)}) %collective-permute-start.5) | collective-permute-done | bytes 540704 | tf_op jit(solution)/shard_map/ppermute | solution.py:223
  51.7 5.2 %collective-permute-start.6 = (bf16[4,528,128]{2,1,0:T(8,128)(2,1)S(1)}, bf16[4,528,128]{2,1,0:T(8,128)(2,1)S(1)}, u32[]{:S(2)}, u32[]{:S(2)}) collective-permute-start(bf16[4,528,128]{2,1,0:T(8,128)(2,1)S(1)} %collective-permute-done.5.refs_2_.refs_4_), channel_id=1, source_target_pairs={{0,16},{16,0},{1,17},{17,1},{2,18},{18,2},{3,19},{19,3},{4,20},{20... | collective-permute-start | bytes 1622024 | tf_op jit(solution)/shard_map/ppermute | solution.py:228
  56.9 3.0 %collective-permute-start.9 = (bf16[2,512,128]{2,1,0:T(8,128)(2,1)S(1)}, bf16[2,512,128]{2,1,0:T(8,128)(2,1)S(1)}, u32[]{:S(2)}, u32[]{:S(2)}) collective-permute-start(bf16[2,512,128]{2,1,0:T(8,128)(2,1)S(1)} %pad_maximum_fusion.1.refs_4_.refs_6_), channel_id=1, source_target_pairs={{0,3},{1,0},{2,1},{3,2},{4,7},{5,4},{6,5},{7,6},{8,11},{9,8},{10,9... | collective-permute-start | bytes 786440 | tf_op jit(solution)/shard_map/ppermute | solution.py:227
  59.9 3.9 %collective-permute-start.8 = (bf16[2,512,128]{2,1,0:T(8,128)(2,1)S(1)}, bf16[2,512,128]{2,1,0:T(8,128)(2,1)S(1)}, u32[]{:S(2)}, u32[]{:S(2)}) collective-permute-start(bf16[2,512,128]{2,1,0:T(8,128)(2,1)S(1)} %pad_maximum_fusion.1.refs_4_.refs_6_), channel_id=1, source_target_pairs={{0,2},{1,3},{2,0},{3,1},{4,6},{5,7},{6,4},{7,5},{8,10},{9,11},{10,... | collective-permute-start | bytes 786440 | tf_op jit(solution)/shard_map/ppermute | solution.py:227
  63.8 1.9 %collective-permute-start.7 = (bf16[2,512,128]{2,1,0:T(8,128)(2,1)S(1)}, bf16[2,512,128]{2,1,0:T(8,128)(2,1)S(1)}, u32[]{:S(2)}, u32[]{:S(2)}) collective-permute-start(bf16[2,512,128]{2,1,0:T(8,128)(2,1)S(1)} %pad_maximum_fusion.1.refs_4_.refs_6_), channel_id=1, source_target_pairs={{0,1},{1,2},{2,3},{3,0},{4,5},{5,6},{6,7},{7,4},{8,9},{9,10},{10,1... | collective-permute-start | bytes 786440 | tf_op jit(solution)/shard_map/ppermute | solution.py:227
  65.8 3.1 %collective-permute-done.9.refs_7_.refs_9_ = bf16[2,512,128]{2,1,0:T(8,128)(2,1)S(1)} collective-permute-done((bf16[2,512,128]{2,1,0:T(8,128)(2,1)S(1)}, bf16[2,512,128]{2,1,0:T(8,128)(2,1)S(1)}, u32[]{:S(2)}, u32[]{:S(2)}) %collective-permute-start.9) | collective-permute-done | bytes 262176 | tf_op jit(solution)/shard_map/ppermute | solution.py:227
  68.8 2.0 %collective-permute-done.8.refs_6_.refs_8_ = bf16[2,512,128]{2,1,0:T(8,128)(2,1)S(1)} collective-permute-done((bf16[2,512,128]{2,1,0:T(8,128)(2,1)S(1)}, bf16[2,512,128]{2,1,0:T(8,128)(2,1)S(1)}, u32[]{:S(2)}, u32[]{:S(2)}) %collective-permute-start.8) | collective-permute-done | bytes 262176 | tf_op jit(solution)/shard_map/ppermute | solution.py:227
  70.9 6.3 %collective-permute-done.7.refs_5_.refs_7_ = bf16[2,512,128]{2,1,0:T(8,128)(2,1)S(1)} collective-permute-done((bf16[2,512,128]{2,1,0:T(8,128)(2,1)S(1)}, bf16[2,512,128]{2,1,0:T(8,128)(2,1)S(1)}, u32[]{:S(2)}, u32[]{:S(2)}) %collective-permute-start.7) | collective-permute-done | bytes 262176 | tf_op jit(solution)/shard_map/ppermute | solution.py:227
  77.2 0.7 copy-done.8
  77.9 0.7 copy-done.4
  79.0 0.8 copy-done.5
  79.9 7.9 %norms.1.refs_1_ = f32[16,1,128]{2,1,0:T(1,128)} custom-call(bf16[4,528,128]{2,1,0:T(8,128)(2,1)} %copy-done.1, bf16[4,528,128]{2,1,0:T(8,128)(2,1)} %copy-done.4, bf16[4,528,128]{2,1,0:T(8,128)(2,1)} %copy-done.3, bf16[4,528,128]{2,1,0:T(8,128)(2,1)} %copy-done.5, bf16[2,512,128]{2,1,0:T(8,128)(2,1)} %copy-done.2, bf16[2,512,128]{2,1,0:T(8,128)(2,1)} %copy-done.8, ...), custom_call_target="tpu_custom_call" | custom-call | tf_op jit(solution)/shard_map/norms/pallas_call | solution.py:240
  87.7 9.7 %all_to_all.15.refs_0_ = f32[16,1,128]{2,1,0:T(1,128)} all-to-all(f32[16,1,128]{2,1,0:T(1,128)} %norms.1.refs_1_), channel_id=1, replica_groups=mesh['zh'=4,'zl'=2,'yl'=2,'c'=2,'yh'=4,'x'=4] {'yl','c','x'}, dimensions={0} | all-to-all | bytes 16384 | tf_op jit(solution)/shard_map/all_to_all | solution.py:249
  97.5 6.3 %grads.1 = (f32[8,4,72,128]{3,2,1,0:T(8,128)}, f32[1,128]{1,0:T(1,128)}) custom-call(f32[16,1,128]{2,1,0:T(1,128)} %all_to_all.15.refs_0_, f32[16,1,128]{2,1,0:T(1,128)} %norms.1.refs_1_, bf16[4,528,128]{2,1,0:T(8,128)(2,1)} %copy-done.1, bf16[4,528,128]{2,1,0:T(8,128)(2,1)} %copy-done.4, bf16[4,528,128]{2,1,0:T(8,128)(2,1)} %copy-done.3, ...), custom_call_target="tpu_custom_call" | custom-call | tf_op jit(solution)/shard_map/grads/pallas_call | solution.py:250
  103.8 2.2 %convert_element_type.6 = f16[8,4,72,128]{3,2,1,0:T(8,128)(2,1)} convert(f32[8,4,72,128]{3,2,1,0:T(8,128)} %get-tuple-element.12) | non-fusion elementwise | flops 294912 | bytes 1769472 | tf_op jit(solution)/shard_map/convert_element_type | solution.py:259
  106.0 15.0 %all-to-all-start.2 = ((f16[32,72,128]{2,1,0:T(8,128)(2,1)}), f16[32,72,128]{2,1,0:T(8,128)(2,1)S(1)}, u32[]{:S(2)}, u32[]{:S(2)}) async-start(f16[32,72,128]{2,1,0:T(8,128)(2,1)} %bitcast.10), calls=%async_computation.2 | async-start | bytes 1179648 | tf_op jit(solution)/shard_map/all_to_all | solution.py:260
  121.0 5.3 %collective-permute-start.10 = (f32[1,128]{1,0:T(1,128)S(1)}, f32[1,128]{1,0:T(1,128)S(1)}, u32[]{:S(2)}, u32[]{:S(2)}) collective-permute-start(f32[1,128]{1,0:T(1,128)S(1)} %copy-done.9), channel_id=1, source_target_pairs={{0,0},{1,1},{2,2},{3,3},{16,4},{17,5},{18,6},{19,7},{32,8},{33,9},... | collective-permute-start | bytes 1544 | tf_op jit(solution)/shard_map/ppermute | solution.py:263
  126.3 12.9 %collective-permute-done.10 = f32[1,128]{1,0:T(1,128)S(1)} collective-permute-done((f32[1,128]{1,0:T(1,128)S(1)}, f32[1,128]{1,0:T(1,128)S(1)}, u32[]{:S(2)}, u32[]{:S(2)}) %collective-permute-start.10) | collective-permute-done | bytes 544 | tf_op jit(solution)/shard_map/ppermute | solution.py:263
  139.2 0.7 all-to-all-done.2
  140.0 0.7 fusion
  (35 shorter events, 1.2 us)
Async XLA Ops:
  3.1 21.9 %collective-permute-start = (bf16[1040,128]{1,0:T(8,128)(2,1)}, bf16[1040,128]{1,0:T(8,128)(2,1)S(1)}, u32[]{:S(2)}, u32[]{:S(2)}) collective-permute-start(bf16[1040,128]{1,0:T(8,128)(2,1)} %get-tuple-element.8), channel_id=1, source_target_pairs={{0,17},{1,18},{2,19},{3,16},{4,33},{5,34},{6,35},{7,32},{8,49},{9,... | collective-permute-start | bytes 798728 | tf_op jit(solution)/shard_map/ppermute | solution.py:213
  12.3 17.5 %collective-permute-start.1 = (bf16[1040,128]{1,0:T(8,128)(2,1)}, bf16[1040,128]{1,0:T(8,128)(2,1)S(1)}, u32[]{:S(2)}, u32[]{:S(2)}) collective-permute-start(bf16[1040,128]{1,0:T(8,128)(2,1)} %get-tuple-element.9), channel_id=1, source_target_pairs={{0,51},{1,48},{2,49},{3,50},{4,3},{5,0},{6,1},{7,2},{8,19},{9,16},... | collective-permute-start | bytes 798728 | tf_op jit(solution)/shard_map/ppermute | solution.py:213
  15.2 16.3 %collective-permute-start.2 = (bf16[1040,128]{1,0:T(8,128)(2,1)}, bf16[1040,128]{1,0:T(8,128)(2,1)S(1)}, u32[]{:S(2)}, u32[]{:S(2)}) collective-permute-start(bf16[1040,128]{1,0:T(8,128)(2,1)} %get-tuple-element.10), channel_id=1, source_target_pairs={{0,0},{1,1},{2,2},{3,3},{4,16},{5,17},{6,18},{7,19},{8,32},{9,33},... | collective-permute-start | bytes 798728 | tf_op jit(solution)/shard_map/ppermute | solution.py:213
  23.0 15.3 %collective-permute-start.3 = (bf16[1040,128]{1,0:T(8,128)(2,1)}, bf16[1040,128]{1,0:T(8,128)(2,1)S(1)}, u32[]{:S(2)}, u32[]{:S(2)}) collective-permute-start(bf16[1040,128]{1,0:T(8,128)(2,1)} %get-tuple-element.11), channel_id=1, source_target_pairs={{0,34},{1,35},{2,32},{3,33},{4,50},{5,51},{6,48},{7,49},{8,2},{9,3... | collective-permute-start | bytes 798728 | tf_op jit(solution)/shard_map/ppermute | solution.py:213
  38.3 7.7 %copy-start.1 = (bf16[4,528,128]{2,1,0:T(8,128)(2,1)}, bf16[4,528,128]{2,1,0:T(8,128)(2,1)S(1)}, u32[]{:S(2)}) copy-start(bf16[4,528,128]{2,1,0:T(8,128)(2,1)S(1)} %pad_maximum_fusion.refs_0_.refs_2_) | copy-start | bytes 1622020
  38.4 13.3 %collective-permute-start.5 = (bf16[4,528,128]{2,1,0:T(8,128)(2,1)S(1)}, bf16[4,528,128]{2,1,0:T(8,128)(2,1)S(1)}, u32[]{:S(2)}, u32[]{:S(2)}) collective-permute-start(bf16[4,528,128]{2,1,0:T(8,128)(2,1)S(1)} %pad_maximum_fusion.refs_0_.refs_2_), channel_id=1, source_target_pairs={{0,32},{32,0},{1,33},{33,1},{2,34},{34,2},{3,35},{35,3},{4,36},{36... | collective-permute-start | bytes 1622024 | tf_op jit(solution)/shard_map/ppermute | solution.py:223
  40.3 37.6 %collective-permute-start.4 = (bf16[4,528,128]{2,1,0:T(8,128)(2,1)S(1)}, bf16[4,528,128]{2,1,0:T(8,128)(2,1)S(1)}, u32[]{:S(2)}, u32[]{:S(2)}) collective-permute-start(bf16[4,528,128]{2,1,0:T(8,128)(2,1)S(1)} %pad_maximum_fusion.refs_0_.refs_2_), channel_id=1, source_target_pairs={{0,16},{16,0},{1,17},{17,1},{2,18},{18,2},{3,19},{19,3},{4,20},{20... | collective-permute-start | bytes 1622024 | tf_op jit(solution)/shard_map/ppermute | solution.py:224
  46.0 31.9 %all-to-all-start = ((bf16[4,2,512,128]{3,2,1,0:T(8,128)(2,1)}), bf16[4,2,512,128]{3,2,1,0:T(8,128)(2,1)S(1)}, u32[]{:S(2)}, u32[]{:S(2)}) async-start(bf16[4,2,512,128]{3,2,1,0:T(8,128)(2,1)} %broadcast_in_dim.3), calls=%async_computation | async-start | bytes 2097152 | tf_op jit(solution)/shard_map/all_to_all | solution.py:218
  51.7 26.3 %copy-start.3 = (bf16[4,528,128]{2,1,0:T(8,128)(2,1)}, bf16[4,528,128]{2,1,0:T(8,128)(2,1)S(1)}, u32[]{:S(2)}) copy-start(bf16[4,528,128]{2,1,0:T(8,128)(2,1)S(1)} %collective-permute-done.5.refs_2_.refs_4_) | copy-start | bytes 1622020
  51.7 26.2 %collective-permute-start.6 = (bf16[4,528,128]{2,1,0:T(8,128)(2,1)S(1)}, bf16[4,528,128]{2,1,0:T(8,128)(2,1)S(1)}, u32[]{:S(2)}, u32[]{:S(2)}) collective-permute-start(bf16[4,528,128]{2,1,0:T(8,128)(2,1)S(1)} %collective-permute-done.5.refs_2_.refs_4_), channel_id=1, source_target_pairs={{0,16},{16,0},{1,17},{17,1},{2,18},{18,2},{3,19},{19,3},{4,20},{20... | collective-permute-start | bytes 1622024 | tf_op jit(solution)/shard_map/ppermute | solution.py:228
  56.9 21.0 %copy-start.2 = (bf16[2,512,128]{2,1,0:T(8,128)(2,1)}, bf16[2,512,128]{2,1,0:T(8,128)(2,1)S(1)}, u32[]{:S(2)}) copy-start(bf16[2,512,128]{2,1,0:T(8,128)(2,1)S(1)} %pad_maximum_fusion.1.refs_4_.refs_6_) | copy-start | bytes 786436
  56.9 11.9 %collective-permute-start.9 = (bf16[2,512,128]{2,1,0:T(8,128)(2,1)S(1)}, bf16[2,512,128]{2,1,0:T(8,128)(2,1)S(1)}, u32[]{:S(2)}, u32[]{:S(2)}) collective-permute-start(bf16[2,512,128]{2,1,0:T(8,128)(2,1)S(1)} %pad_maximum_fusion.1.refs_4_.refs_6_), channel_id=1, source_target_pairs={{0,3},{1,0},{2,1},{3,2},{4,7},{5,4},{6,5},{7,6},{8,11},{9,8},{10,9... | collective-permute-start | bytes 786440 | tf_op jit(solution)/shard_map/ppermute | solution.py:227
  59.9 11.0 %collective-permute-start.8 = (bf16[2,512,128]{2,1,0:T(8,128)(2,1)S(1)}, bf16[2,512,128]{2,1,0:T(8,128)(2,1)S(1)}, u32[]{:S(2)}, u32[]{:S(2)}) collective-permute-start(bf16[2,512,128]{2,1,0:T(8,128)(2,1)S(1)} %pad_maximum_fusion.1.refs_4_.refs_6_), channel_id=1, source_target_pairs={{0,2},{1,3},{2,0},{3,1},{4,6},{5,7},{6,4},{7,5},{8,10},{9,11},{10,... | collective-permute-start | bytes 786440 | tf_op jit(solution)/shard_map/ppermute | solution.py:227
  63.8 13.3 %collective-permute-start.7 = (bf16[2,512,128]{2,1,0:T(8,128)(2,1)S(1)}, bf16[2,512,128]{2,1,0:T(8,128)(2,1)S(1)}, u32[]{:S(2)}, u32[]{:S(2)}) collective-permute-start(bf16[2,512,128]{2,1,0:T(8,128)(2,1)S(1)} %pad_maximum_fusion.1.refs_4_.refs_6_), channel_id=1, source_target_pairs={{0,1},{1,2},{2,3},{3,0},{4,5},{5,6},{6,7},{7,4},{8,9},{9,10},{10,1... | collective-permute-start | bytes 786440 | tf_op jit(solution)/shard_map/ppermute | solution.py:227
  68.8 8.3 %copy-start.6 = (bf16[2,512,128]{2,1,0:T(8,128)(2,1)}, bf16[2,512,128]{2,1,0:T(8,128)(2,1)S(1)}, u32[]{:S(2)}) copy-start(bf16[2,512,128]{2,1,0:T(8,128)(2,1)S(1)} %collective-permute-done.9.refs_7_.refs_9_) | copy-start | bytes 786436
  70.9 6.3 %copy-start.7 = (bf16[2,512,128]{2,1,0:T(8,128)(2,1)}, bf16[2,512,128]{2,1,0:T(8,128)(2,1)S(1)}, u32[]{:S(2)}) copy-start(bf16[2,512,128]{2,1,0:T(8,128)(2,1)S(1)} %collective-permute-done.8.refs_6_.refs_8_) | copy-start | bytes 786436
  77.1 0.7 copy-start.8
  77.9 0.8 copy-start.4
  77.9 1.2 copy-start
  79.0 0.8 copy-start.5
  103.8 17.2 %copy-start.9 = (f32[1,128]{1,0:T(1,128)S(1)}, f32[1,128]{1,0:T(1,128)}, u32[]{:S(2)}) copy-start(f32[1,128]{1,0:T(1,128)} %get-tuple-element.13) | copy-start | bytes 1540
  106.0 33.9 %all-to-all-start.2 = ((f16[32,72,128]{2,1,0:T(8,128)(2,1)}), f16[32,72,128]{2,1,0:T(8,128)(2,1)S(1)}, u32[]{:S(2)}, u32[]{:S(2)}) async-start(f16[32,72,128]{2,1,0:T(8,128)(2,1)} %bitcast.10), calls=%async_computation.2 | async-start | bytes 1179648 | tf_op jit(solution)/shard_map/all_to_all | solution.py:260
  121.0 18.3 %collective-permute-start.10 = (f32[1,128]{1,0:T(1,128)S(1)}, f32[1,128]{1,0:T(1,128)S(1)}, u32[]{:S(2)}, u32[]{:S(2)}) collective-permute-start(f32[1,128]{1,0:T(1,128)S(1)} %copy-done.9), channel_id=1, source_target_pairs={{0,0},{1,1},{2,2},{3,3},{16,4},{17,5},{18,6},{19,7},{32,8},{33,9},... | collective-permute-start | bytes 1544 | tf_op jit(solution)/shard_map/ppermute | solution.py:263

commit v2 on v1

--- a/solution.py
+++ b/solution.py
@@ -38,7 +38,7 @@
 
 
 def to_group(k, yl, c, yh, x):
-    j = (yh + k) % 4
+    j = yh ^ k
     return dict(yl=j // 2, c=j % 2, yh=c * 2 + yl, x=(x + k) % 4)
 
 
@@ -56,7 +56,7 @@
     wide = chunks * BLOCK // 4
     for n, k in enumerate(ORDER):
         i = (x + k) % 4
-        j = (yh + k) % 4
+        j = yh ^ k
         for z in range(wide // COLS):
             at = pl.multiple_of((z * 4 + j) * COLS, COLS)
             outs[n][z * COLS : (z + 1) * COLS, :] = gt_ref[pl.ds(at, COLS), :]
@@ -66,73 +66,51 @@
         outs[n][wide + PART :, :] = doc
 
 
-def fetch(parts, a_s, g_s, doc_s, sems):
-    x, j = lax.axis_index("x"), lax.axis_index("yl") * 2 + lax.axis_index("c")
-    copies = []
-
-    def copy(src, dst):
-        copies.append(pltpu.make_async_copy(src, dst, sems.at[len(copies)]))
-
-    def slab(j, k, x):
-        return (j + 4 - k) % 4 * 4 + (x + 4 - k) % 4
-
+def here():
+    return lax.axis_index("x"), lax.axis_index("yl") * 2 + lax.axis_index("c")
+
+
+def grads_of(parts, back, n, x):
+    if n < 2:
+        return parts[4 + back][n]
+    return parts[8][(x + 4 - back) % 4, n - 2]
+
+
+def features(slab):
+    return jnp.concatenate([slab[r * BLOCK : (r + 1) * BLOCK] for r in range(4)], axis=1)
+
+
+def number(slab):
+    return slab[PART : PART + PAD].astype(jnp.float32)
+
+
+def norm_kernel(*refs):
+    parts, out, a_s, g_s, acc, starts, norms = refs[:9], *refs[9:]
+    x, j = here()
     for n, k in enumerate(ORDER):
         for m in range(4):
-            copy(parts[m].at[n, PART:], doc_s.at[slab(j ^ m, k, x)])
-    for n, k in enumerate(ORDER):
-        for m in range(4):
-            if n < 2:
-                src, sender = parts[4 + m].at[n], (x + 4 - m) % 4
-            else:
-                src, sender = parts[8].at[m, n - 2], m
-            at = pl.multiple_of(slab(j, k, sender) * BLOCK, BLOCK)
-            copy(src, g_s.at[:, pl.ds(at, BLOCK)])
-    for n, k in enumerate(ORDER):
-        for m in range(4):
-            at = pl.multiple_of(slab(j ^ m, k, x) * BLOCK, BLOCK)
-            for r in range(4):
-                rows = slice(r * BLOCK, (r + 1) * BLOCK)
-                copy(parts[m].at[n, rows], a_s.at[pl.ds(at, BLOCK), rows])
-    for cp in copies:
-        cp.start()
-    return copies[:16], copies[16:32], copies[32:]
-
-
-def wait(copies):
-    for cp in copies:
-        cp.wait()
-
-
-COPIES = 16 * 6
-
-
-def norm_kernel(*refs):
-    parts, out, a_s, g_s, doc_s, acc, starts, norms, sems = refs[:9], *refs[9:]
-    docs, grads, acts = fetch(parts, a_s, g_s, doc_s, sems)
-    a_s[SLABS * BLOCK :, :] = jnp.zeros((BLOCK, a_s.shape[1]), a_s.dtype)
+            a_s[(j ^ (m ^ k)) * 4 + (x + 4 - k) % 4] = parts[m][n]
+            g_s[(j ^ k) * 4 + (x + 8 - m - k) % 4] = grads_of(parts, m, n, x)
+    a_s[SLABS] = jnp.zeros(a_s.shape[1:], a_s.dtype)
     norms[...] = jnp.zeros_like(norms)
-    wait(docs)
     doc = jnp.int32(-1)
     for t in range(SLABS):
-        here = jnp.maximum(doc, jnp.max(doc_s[t].astype(jnp.float32)).astype(jnp.int32))
-        new = here != doc
-
-        @pl.when(new)
-        def _(here=here, t=t):
-            starts[here] = t
-
-        doc = here
+        this = jnp.maximum(doc, jnp.max(number(a_s[t])).astype(jnp.int32))
+
+        @pl.when(this != doc)
+        def _(this=this, t=t):
+            starts[this] = t
+
+        doc = this
     starts[DOCS] = SLABS
-    wait(grads)
-    wait(acts)
     lane = lax.broadcasted_iota(jnp.int32, (1, BLOCK), 1)
     second = lax.broadcasted_iota(jnp.int32, (1, 2 * BLOCK), 1) >= BLOCK
 
     def product(first, end):
-        at = pl.multiple_of(first * BLOCK, BLOCK)
-        g = g_s[:, pl.ds(at, 2 * BLOCK)]
+        g = jnp.concatenate([g_s[first], g_s[first + 1]], axis=1)
         g = jnp.where(jnp.logical_and(second, first + 1 >= end), jnp.zeros_like(g), g)
-        return jnp.dot(g, a_s[pl.ds(at, 2 * BLOCK), :], preferred_element_type=jnp.float32)
+        a = jnp.concatenate([features(a_s[first]), features(a_s[first + 1])], axis=0)
+        return jnp.dot(g, a, preferred_element_type=jnp.float32)
 
     def squared(w, d):
         total = jnp.sum(jnp.sum(w * w, axis=0, keepdims=True), axis=1, keepdims=True)
@@ -164,24 +142,27 @@
 
 def grad_kernel(*refs):
     norms, own, parts = refs[0], refs[1], refs[2:11]
-    out, clip_out, a_s, g_s, doc_s, acc, sems = refs[11:]
-    docs, grads, acts = fetch(parts, a_s, g_s, doc_s, sems)
+    out, clip_out, g_s, acc = refs[11:]
+    x, _ = here()
     norm_sq = jnp.sum(norms[...], axis=0)
     clip = CLIP / jnp.sqrt(jnp.maximum(norm_sq, CLIP * CLIP))
     clip_out[...] = clip
     bound = jnp.sum(jnp.minimum(jnp.sqrt(own[0]), CLIP), axis=1, keepdims=True)
     shift = jnp.ceil(jnp.log2(jnp.maximum(bound, 1e-18))) - 14.0
     lane = lax.broadcasted_iota(jnp.int32, (1, BLOCK), 1).astype(jnp.float32)
-    wait(docs)
-    wait(grads)
-    for t in range(SLABS):
-        here = doc_s[t, 0:1, :].astype(jnp.float32) == lane
-        factor = jnp.sum(jnp.where(here, clip, 0.0), axis=1, keepdims=True)
-        g = g_s[:, t * BLOCK : (t + 1) * BLOCK].astype(jnp.float32)
-        g_s[:, t * BLOCK : (t + 1) * BLOCK] = (g * factor).astype(jnp.bfloat16)
-    tokens = SLABS * BLOCK
-    wait(acts)
-    acc[...] = jnp.dot(g_s[:, :tokens], a_s[:tokens, :], preferred_element_type=jnp.float32)
+    acts = []
+    for n, k in enumerate(ORDER):
+        for m in range(4):
+            a = parts[m][n]
+            factor = jnp.sum(jnp.where(number(a)[0:1] == lane, clip, 0.0), axis=1, keepdims=True)
+            g = grads_of(parts, (k - (m ^ k)) % 4, ORDER.index(m ^ k), x)
+            g_s[len(acts)] = (g.astype(jnp.float32) * factor).astype(jnp.bfloat16)
+            acts.append(features(a))
+    acc[...] = jnp.dot(
+        jnp.concatenate([g_s[t] for t in range(SLABS)], axis=1),
+        jnp.concatenate(acts, axis=0),
+        preferred_element_type=jnp.float32,
+    )
     scale = jnp.exp2(-shift)
     tail = jnp.broadcast_to(shift, (TAIL, BLOCK))
     for z in range(out.shape[0]):
@@ -197,7 +178,7 @@
     wide = levels * COLS
     bf16, f32 = jnp.bfloat16, jnp.float32
     vmem = pl.BlockSpec(memory_space=pltpu.VMEM)
-    anywhere = pl.BlockSpec(memory_space=pl.ANY)
+    small = pltpu.CompilerParams(vmem_limit_bytes=20 << 20)
 
     payload = pl.pallas_call(
         prep_kernel,
@@ -206,6 +187,7 @@
         out_specs=[vmem] * 4,
         scratch_shapes=[pltpu.VMEM((g.shape[1], BLOCK), bf16)],
         interpret=INTERPRET,
+        compiler_params=small,
         name="prep",
     )(ids, a, g)
 
@@ -229,31 +211,30 @@
     a_parts = [own_a, own_other, partner, partner_other]
     parts = a_parts + g_parts + [last_g]
 
-    stores = [
-        pltpu.VMEM(((SLABS + 1) * BLOCK, PART), bf16),
-        pltpu.VMEM((wide, (SLABS + 1) * BLOCK), bf16),
-        pltpu.VMEM((SLABS, PAD, BLOCK), bf16),
-        pltpu.VMEM((wide, PART), f32),
-    ]
-    sems = [pltpu.SemaphoreType.DMA((COPIES,))]
+    acts = pltpu.VMEM((SLABS + 1, PART + PAD, BLOCK), bf16)
+    grads = pltpu.VMEM((SLABS + 1, wide, BLOCK), bf16)
+    total = pltpu.VMEM((wide, PART), f32)
+    starts = pltpu.SMEM((DOCS + 1,), jnp.int32)
     row = jax.ShapeDtypeStruct((1, BLOCK), f32)
     partial = pl.pallas_call(
         norm_kernel,
         out_shape=jax.ShapeDtypeStruct((16, 1, BLOCK), f32),
-        in_specs=[anywhere] * 9,
+        in_specs=[vmem] * 9,
         out_specs=vmem,
-        scratch_shapes=stores + [pltpu.SMEM((DOCS + 1,), jnp.int32), pltpu.VMEM((1, BLOCK), f32)] + sems,
+        scratch_shapes=[acts, grads, total, starts, pltpu.VMEM((1, BLOCK), f32)],
         interpret=INTERPRET,
+        compiler_params=small,
         name="norms",
     )(*parts)
     norms = lax.all_to_all(partial, GROUP, split_axis=0, concat_axis=0, tiled=True)
     pieces, clip = pl.pallas_call(
         grad_kernel,
         out_shape=[jax.ShapeDtypeStruct((levels, 4, COLS + TAIL, BLOCK), f32), row],
-        in_specs=[vmem, vmem] + [anywhere] * 9,
+        in_specs=[vmem, vmem] + [vmem] * 9,
         out_specs=[vmem] * 2,
-        scratch_shapes=stores + sems,
+        scratch_shapes=[grads, total],
         interpret=INTERPRET,
+        compiler_params=small,
         name="grads",
     )(norms, partial, *parts)
     pieces = pieces.astype(jnp.float16).reshape(levels * 4, COLS + TAIL, BLOCK)

time: 144 us -> 135 us (0.938)
  Pallas kernels: 16.7 us -> 6.32 us
  local copies, waits for them, and re-layouts: 4.41 us -> 9.37 us
  waiting for transfers between devices: 40.2 us -> 38 us
    pallas_call x1, Pallas kernels: 6.31 us -> 1.34 us  [body(): pl.pallas_call(grad_kernel, out_shape=[jax.ShapeDtypeStruct((levels, 4, C...]
    unnamed x21 -> x19, local copies, waits for them, and re-layouts: 3.2 us -> 8.16 us
    ppermute x1, starting transfers between devices: 4.54 us -> 8.44 us  [body(): own_other = lax.ppermute(own_a, 'c', flip)]
    all_to_all x1, starting transfers between devices: 15 us -> 11.7 us  [body(): lax.all_to_all(pieces, SUMMED, split_axis=0, concat_axis=0, tiled=True)]
    pallas_call x1, Pallas kernels: 7.87 us -> 4.65 us  [body(): pl.pallas_call(norm_kernel, out_shape=jax.ShapeDtypeStruct((16, 1, BLOCK)...]
    pallas_call x1, Pallas kernels: 2.51 us -> 0.33 us  [body(): pl.pallas_call(prep_kernel, out_shape=[jax.ShapeDtypeStruct((wide + PART...]
    ppermute x1, waiting for transfers between devices: 2.09 us -> 0.01 us  [body(): partner = lax.ppermute(own_a, 'yl', flip)]
  transfers between devices with their start and end apart: 13 -> 13, of which waited for: 9 -> 8; matrix products, arithmetic and copies ran while one was open for 1% -> 1% of each run, Pallas kernels for 0% -> 0%
where the time goes in v2:
time: 135 us; the launch traced here: 133 us
  starting transfers between devices  66.5 us (49%)
  waiting for transfers between devices  38 us (28%)
  blocking collectives  10.2 us (8%)
  local copies, waits for them, and re-layouts  9.37 us (7%)
  Pallas kernels  6.32 us (5%)
  other arithmetic  1.86 us (1%)
    ppermute x4, starting transfers between devices, body(): lax.ppermute(payload[n], MOVE, table(sizes, MOVE, functools.partial(to_gr...  21.8 us
    ppermute x1, waiting for transfers between devices, body(): clip = lax.ppermute(clip, MOVE, home)  13 us
    ppermute x4, waiting for transfers between devices, body(): lax.ppermute(payload[n], MOVE, table(sizes, MOVE, functools.partial(to_gr...  11.9 us
    all_to_all x1, starting transfers between devices, body(): lax.all_to_all(pieces, SUMMED, split_axis=0, concat_axis=0, tiled=True)  11.7 us
    ppermute x3, waiting for transfers between devices, body(): lax.ppermute(own_g, 'x', [(s, (s + m) % 4) for s in range(4)])  11.5 us
    all_to_all x1, blocking collectives, body(): lax.all_to_all(partial, GROUP, split_axis=0, concat_axis=0, tiled=True)  10.2 us
    ppermute x3, starting transfers between devices, body(): lax.ppermute(own_g, 'x', [(s, (s + m) % 4) for s in range(4)])  9.47 us
    ppermute x1, starting transfers between devices, body(): own_other = lax.ppermute(own_a, 'c', flip)  8.44 us
  transfers between devices with their start and end apart: 13, of which 8 were waited for; matrix products, arithmetic and copies ran while one was open for 1% of the time, Pallas kernels for 0%

profile of v2, /device:TPU:1, one launch (start us, length us, event | category | flops | bytes accessed | tf_op | source)
XLA Modules:
  0.0 133.2 jit_solution(7866285706455971454)
XLA Ops:
  0.6 1.0 copy-done.6
  1.7 1.0 copy-done.7
  3.7 9.2 %collective-permute-start = (bf16[1040,128]{1,0:T(8,128)(2,1)S(1)}, bf16[1040,128]{1,0:T(8,128)(2,1)S(1)}, u32[]{:S(2)}, u32[]{:S(2)}) collective-permute-start(bf16[1040,128]{1,0:T(8,128)(2,1)S(1)} %get-tuple-element.8), channel_id=1, source_target_pairs={{0,17},{1,18},{2,19},{3,16},{4,1},{5,2},{6,3},{7,0},{8,49},{9,50},... | collective-permute-start | bytes 798728 | tf_op jit(solution)/shard_map/ppermute | solution.py:195
  12.9 2.8 %collective-permute-start.1 = (bf16[1040,128]{1,0:T(8,128)(2,1)S(1)}, bf16[1040,128]{1,0:T(8,128)(2,1)S(1)}, u32[]{:S(2)}, u32[]{:S(2)}) collective-permute-start(bf16[1040,128]{1,0:T(8,128)(2,1)S(1)} %get-tuple-element.9), channel_id=1, source_target_pairs={{0,51},{1,48},{2,49},{3,50},{4,35},{5,32},{6,33},{7,34},{8,19},{9,... | collective-permute-start | bytes 798728 | tf_op jit(solution)/shard_map/ppermute | solution.py:195
  15.8 7.8 %collective-permute-start.2 = (bf16[1040,128]{1,0:T(8,128)(2,1)S(1)}, bf16[1040,128]{1,0:T(8,128)(2,1)S(1)}, u32[]{:S(2)}, u32[]{:S(2)}) collective-permute-start(bf16[1040,128]{1,0:T(8,128)(2,1)S(1)} %get-tuple-element.10), channel_id=1, source_target_pairs={{0,0},{1,1},{2,2},{3,3},{4,16},{5,17},{6,18},{7,19},{8,32},{9,33},... | collective-permute-start | bytes 798728 | tf_op jit(solution)/shard_map/ppermute | solution.py:195
  23.6 1.9 %collective-permute-start.3 = (bf16[1040,128]{1,0:T(8,128)(2,1)S(1)}, bf16[1040,128]{1,0:T(8,128)(2,1)S(1)}, u32[]{:S(2)}, u32[]{:S(2)}) collective-permute-start(bf16[1040,128]{1,0:T(8,128)(2,1)S(1)} %get-tuple-element.11), channel_id=1, source_target_pairs={{0,34},{1,35},{2,32},{3,33},{4,50},{5,51},{6,48},{7,49},{8,2},{9,3... | collective-permute-start | bytes 798728 | tf_op jit(solution)/shard_map/ppermute | solution.py:195
  25.6 10.4 %collective-permute-done.1 = bf16[1040,128]{1,0:T(8,128)(2,1)S(1)} collective-permute-done((bf16[1040,128]{1,0:T(8,128)(2,1)S(1)}, bf16[1040,128]{1,0:T(8,128)(2,1)S(1)}, u32[]{:S(2)}, u32[]{:S(2)}) %collective-permute-start.1) | collective-permute-done | bytes 266272 | tf_op jit(solution)/shard_map/ppermute | solution.py:195
  36.6 0.8 collective-permute-done.3
  37.6 1.9 %collective-permute-start.5 = (bf16[4,528,128]{2,1,0:T(8,128)(2,1)S(1)}, bf16[4,528,128]{2,1,0:T(8,128)(2,1)S(1)}, u32[]{:S(2)}, u32[]{:S(2)}) collective-permute-start(bf16[4,528,128]{2,1,0:T(8,128)(2,1)S(1)} %pad_maximum_fusion.refs_0_.refs_2_), channel_id=1, source_target_pairs={{0,32},{32,0},{1,33},{33,1},{2,34},{34,2},{3,35},{35,3},{4,36},{36... | collective-permute-start | bytes 1622024 | tf_op jit(solution)/shard_map/ppermute | solution.py:205
  39.5 8.4 %collective-permute-start.4 = (bf16[4,528,128]{2,1,0:T(8,128)(2,1)S(1)}, bf16[4,528,128]{2,1,0:T(8,128)(2,1)S(1)}, u32[]{:S(2)}, u32[]{:S(2)}) collective-permute-start(bf16[4,528,128]{2,1,0:T(8,128)(2,1)S(1)} %pad_maximum_fusion.refs_0_.refs_2_), channel_id=1, source_target_pairs={{0,16},{16,0},{1,17},{17,1},{2,18},{18,2},{3,19},{19,3},{4,20},{20... | collective-permute-start | bytes 1622024 | tf_op jit(solution)/shard_map/ppermute | solution.py:206
  48.0 1.1 broadcast_in_dim.3
  49.1 3.5 %all-to-all-start = ((bf16[4,2,512,128]{3,2,1,0:T(8,128)(2,1)}), bf16[4,2,512,128]{3,2,1,0:T(8,128)(2,1)S(1)}, u32[]{:S(2)}, u32[]{:S(2)}) async-start(bf16[4,2,512,128]{3,2,1,0:T(8,128)(2,1)} %broadcast_in_dim.3), calls=%async_computation | async-start | bytes 2097152 | tf_op jit(solution)/shard_map/all_to_all | solution.py:200
  52.7 4.5 %collective-permute-start.6 = (bf16[4,528,128]{2,1,0:T(8,128)(2,1)S(1)}, bf16[4,528,128]{2,1,0:T(8,128)(2,1)S(1)}, u32[]{:S(2)}, u32[]{:S(2)}) collective-permute-start(bf16[4,528,128]{2,1,0:T(8,128)(2,1)S(1)} %collective-permute-done.5.refs_2_.refs_4_), channel_id=1, source_target_pairs={{0,16},{16,0},{1,17},{17,1},{2,18},{18,2},{3,19},{19,3},{4,20},{20... | collective-permute-start | bytes 1622024 | tf_op jit(solution)/shard_map/ppermute | solution.py:210
  57.3 5.1 %collective-permute-start.9 = (bf16[2,512,128]{2,1,0:T(8,128)(2,1)S(1)}, bf16[2,512,128]{2,1,0:T(8,128)(2,1)S(1)}, u32[]{:S(2)}, u32[]{:S(2)}) collective-permute-start(bf16[2,512,128]{2,1,0:T(8,128)(2,1)S(1)} %pad_maximum_fusion.1.refs_4_.refs_6_), channel_id=1, source_target_pairs={{0,3},{1,0},{2,1},{3,2},{4,7},{5,4},{6,5},{7,6},{8,11},{9,8},{10,9... | collective-permute-start | bytes 786440 | tf_op jit(solution)/shard_map/ppermute | solution.py:209
  62.4 1.9 %collective-permute-start.8 = (bf16[2,512,128]{2,1,0:T(8,128)(2,1)S(1)}, bf16[2,512,128]{2,1,0:T(8,128)(2,1)S(1)}, u32[]{:S(2)}, u32[]{:S(2)}) collective-permute-start(bf16[2,512,128]{2,1,0:T(8,128)(2,1)S(1)} %pad_maximum_fusion.1.refs_4_.refs_6_), channel_id=1, source_target_pairs={{0,2},{1,3},{2,0},{3,1},{4,6},{5,7},{6,4},{7,5},{8,10},{9,11},{10,... | collective-permute-start | bytes 786440 | tf_op jit(solution)/shard_map/ppermute | solution.py:209
  64.3 2.5 %collective-permute-start.7 = (bf16[2,512,128]{2,1,0:T(8,128)(2,1)S(1)}, bf16[2,512,128]{2,1,0:T(8,128)(2,1)S(1)}, u32[]{:S(2)}, u32[]{:S(2)}) collective-permute-start(bf16[2,512,128]{2,1,0:T(8,128)(2,1)S(1)} %pad_maximum_fusion.1.refs_4_.refs_6_), channel_id=1, source_target_pairs={{0,1},{1,2},{2,3},{3,0},{4,5},{5,6},{6,7},{7,4},{8,9},{9,10},{10,1... | collective-permute-start | bytes 786440 | tf_op jit(solution)/shard_map/ppermute | solution.py:209
  66.8 5.2 %collective-permute-done.9.refs_7_.refs_9_ = bf16[2,512,128]{2,1,0:T(8,128)(2,1)S(1)} collective-permute-done((bf16[2,512,128]{2,1,0:T(8,128)(2,1)S(1)}, bf16[2,512,128]{2,1,0:T(8,128)(2,1)S(1)}, u32[]{:S(2)}, u32[]{:S(2)}) %collective-permute-start.9) | collective-permute-done | bytes 262176 | tf_op jit(solution)/shard_map/ppermute | solution.py:209
  72.0 0.7 copy-done
  72.7 0.7 collective-permute-done.8.refs_6_.refs_8_
  74.1 5.6 %collective-permute-done.7.refs_5_.refs_7_ = bf16[2,512,128]{2,1,0:T(8,128)(2,1)S(1)} collective-permute-done((bf16[2,512,128]{2,1,0:T(8,128)(2,1)S(1)}, bf16[2,512,128]{2,1,0:T(8,128)(2,1)S(1)}, u32[]{:S(2)}, u32[]{:S(2)}) %collective-permute-start.7) | collective-permute-done | bytes 262176 | tf_op jit(solution)/shard_map/ppermute | solution.py:209
  80.4 0.9 copy-done.1
  81.3 0.9 copy-done.3
  82.3 0.9 copy-done.5
  83.2 4.6 %norms.1.refs_1_ = f32[16,1,128]{2,1,0:T(1,128)S(1)} custom-call(bf16[4,528,128]{2,1,0:T(8,128)(2,1)S(1)} %pad_maximum_fusion.refs_0_.refs_2_, bf16[4,528,128]{2,1,0:T(8,128)(2,1)S(1)} %collective-permute-done.4.refs_1_.refs_3_, bf16[4,528,128]{2,1,0:T(8,128)(2,1)S(1)} %collective-permute-done.5.refs_2_.refs_4_, ...), custom_call_target="tpu_custom_call" | custom-call | tf_op jit(solution)/shard_map/norms/pallas_call | solution.py:219
  87.9 10.2 %all_to_all.15.refs_0_ = f32[16,1,128]{2,1,0:T(1,128)S(1)} all-to-all(f32[16,1,128]{2,1,0:T(1,128)S(1)} %norms.1.refs_1_), channel_id=1, replica_groups=mesh['zh'=4,'zl'=2,'yl'=2,'c'=2,'yh'=4,'x'=4] {'yl','c','x'}, dimensions={0} | all-to-all | bytes 16384 | tf_op jit(solution)/shard_map/all_to_all | solution.py:229
  98.0 1.3 %grads.1 = (f32[8,4,72,128]{3,2,1,0:T(8,128)S(1)}, f32[1,128]{1,0:T(1,128)S(1)}) custom-call(f32[16,1,128]{2,1,0:T(1,128)S(1)} %all_to_all.15.refs_0_, f32[16,1,128]{2,1,0:T(1,128)S(1)} %norms.1.refs_1_, bf16[4,528,128]{2,1,0:T(8,128)(2,1)S(1)} %pad_maximum_fusion.refs_0_.refs_2_, bf16[4,528,128]{2,1,0:T(8,128)(2,1)S(1)} %collective-permute-done.4.refs_1_.refs_3_, ...), custom_call_target="tpu_custom_call" | custom-call | tf_op jit(solution)/shard_map/grads/pallas_call | solution.py:230
  99.4 0.9 convert_element_type.6
  100.3 11.7 %all-to-all-start.2 = ((f16[32,72,128]{2,1,0:T(8,128)(2,1)}), f16[32,72,128]{2,1,0:T(8,128)(2,1)S(1)}, u32[]{:S(2)}, u32[]{:S(2)}) async-start(f16[32,72,128]{2,1,0:T(8,128)(2,1)} %bitcast.10), calls=%async_computation.2 | async-start | bytes 1179648 | tf_op jit(solution)/shard_map/all_to_all | solution.py:241
  112.0 5.2 %collective-permute-start.10 = (f32[1,128]{1,0:T(1,128)S(1)}, f32[1,128]{1,0:T(1,128)S(1)}, u32[]{:S(2)}, u32[]{:S(2)}) collective-permute-start(f32[1,128]{1,0:T(1,128)S(1)} %get-tuple-element.13), channel_id=1, source_target_pairs={{0,0},{1,1},{2,2},{3,3},{16,4},{17,5},{18,6},{19,7},{32,8},{33,9},... | collective-permute-start | bytes 1544 | tf_op jit(solution)/shard_map/ppermute | solution.py:244
  117.2 13.0 %collective-permute-done.10 = f32[1,128]{1,0:T(1,128)S(1)} collective-permute-done((f32[1,128]{1,0:T(1,128)S(1)}, f32[1,128]{1,0:T(1,128)S(1)}, u32[]{:S(2)}, u32[]{:S(2)}) %collective-permute-start.10) | collective-permute-done | bytes 544 | tf_op jit(solution)/shard_map/ppermute | solution.py:244
  130.2 1.6 %all-to-all-done.2 = f16[32,72,128]{2,1,0:T(8,128)(2,1)S(1)} async-done(((f16[32,72,128]{2,1,0:T(8,128)(2,1)}), f16[32,72,128]{2,1,0:T(8,128)(2,1)S(1)}, u32[]{:S(2)}, u32[]{:S(2)}) %all-to-all-start.2) | async-done | bytes 589856 | tf_op jit(solution)/shard_map/all_to_all | solution.py:241
  131.9 0.7 fusion
  (33 shorter events, 3.8 us)
Async XLA Ops:
  0.6 1.0 copy-start.6
  1.7 1.0 copy-start.7
  2.7 0.7 copy-start.8
  3.7 21.8 %collective-permute-start = (bf16[1040,128]{1,0:T(8,128)(2,1)S(1)}, bf16[1040,128]{1,0:T(8,128)(2,1)S(1)}, u32[]{:S(2)}, u32[]{:S(2)}) collective-permute-start(bf16[1040,128]{1,0:T(8,128)(2,1)S(1)} %get-tuple-element.8), channel_id=1, source_target_pairs={{0,17},{1,18},{2,19},{3,16},{4,1},{5,2},{6,3},{7,0},{8,49},{9,50},... | collective-permute-start | bytes 798728 | tf_op jit(solution)/shard_map/ppermute | solution.py:195
  12.9 23.1 %collective-permute-start.1 = (bf16[1040,128]{1,0:T(8,128)(2,1)S(1)}, bf16[1040,128]{1,0:T(8,128)(2,1)S(1)}, u32[]{:S(2)}, u32[]{:S(2)}) collective-permute-start(bf16[1040,128]{1,0:T(8,128)(2,1)S(1)} %get-tuple-element.9), channel_id=1, source_target_pairs={{0,51},{1,48},{2,49},{3,50},{4,35},{5,32},{6,33},{7,34},{8,19},{9,... | collective-permute-start | bytes 798728 | tf_op jit(solution)/shard_map/ppermute | solution.py:195
  15.8 20.8 %collective-permute-start.2 = (bf16[1040,128]{1,0:T(8,128)(2,1)S(1)}, bf16[1040,128]{1,0:T(8,128)(2,1)S(1)}, u32[]{:S(2)}, u32[]{:S(2)}) collective-permute-start(bf16[1040,128]{1,0:T(8,128)(2,1)S(1)} %get-tuple-element.10), channel_id=1, source_target_pairs={{0,0},{1,1},{2,2},{3,3},{4,16},{5,17},{6,18},{7,19},{8,32},{9,33},... | collective-permute-start | bytes 798728 | tf_op jit(solution)/shard_map/ppermute | solution.py:195
  23.6 13.9 %collective-permute-start.3 = (bf16[1040,128]{1,0:T(8,128)(2,1)S(1)}, bf16[1040,128]{1,0:T(8,128)(2,1)S(1)}, u32[]{:S(2)}, u32[]{:S(2)}) collective-permute-start(bf16[1040,128]{1,0:T(8,128)(2,1)S(1)} %get-tuple-element.11), channel_id=1, source_target_pairs={{0,34},{1,35},{2,32},{3,33},{4,50},{5,51},{6,48},{7,49},{8,2},{9,3... | collective-permute-start | bytes 798728 | tf_op jit(solution)/shard_map/ppermute | solution.py:195
  37.6 15.1 %collective-permute-start.5 = (bf16[4,528,128]{2,1,0:T(8,128)(2,1)S(1)}, bf16[4,528,128]{2,1,0:T(8,128)(2,1)S(1)}, u32[]{:S(2)}, u32[]{:S(2)}) collective-permute-start(bf16[4,528,128]{2,1,0:T(8,128)(2,1)S(1)} %pad_maximum_fusion.refs_0_.refs_2_), channel_id=1, source_target_pairs={{0,32},{32,0},{1,33},{33,1},{2,34},{34,2},{3,35},{35,3},{4,36},{36... | collective-permute-start | bytes 1622024 | tf_op jit(solution)/shard_map/ppermute | solution.py:205
  39.5 40.9 %collective-permute-start.4 = (bf16[4,528,128]{2,1,0:T(8,128)(2,1)S(1)}, bf16[4,528,128]{2,1,0:T(8,128)(2,1)S(1)}, u32[]{:S(2)}, u32[]{:S(2)}) collective-permute-start(bf16[4,528,128]{2,1,0:T(8,128)(2,1)S(1)} %pad_maximum_fusion.refs_0_.refs_2_), channel_id=1, source_target_pairs={{0,16},{16,0},{1,17},{17,1},{2,18},{18,2},{3,19},{19,3},{4,20},{20... | collective-permute-start | bytes 1622024 | tf_op jit(solution)/shard_map/ppermute | solution.py:206
  49.1 31.2 %all-to-all-start = ((bf16[4,2,512,128]{3,2,1,0:T(8,128)(2,1)}), bf16[4,2,512,128]{3,2,1,0:T(8,128)(2,1)S(1)}, u32[]{:S(2)}, u32[]{:S(2)}) async-start(bf16[4,2,512,128]{3,2,1,0:T(8,128)(2,1)} %broadcast_in_dim.3), calls=%async_computation | async-start | bytes 2097152 | tf_op jit(solution)/shard_map/all_to_all | solution.py:200
  52.7 27.6 %collective-permute-start.6 = (bf16[4,528,128]{2,1,0:T(8,128)(2,1)S(1)}, bf16[4,528,128]{2,1,0:T(8,128)(2,1)S(1)}, u32[]{:S(2)}, u32[]{:S(2)}) collective-permute-start(bf16[4,528,128]{2,1,0:T(8,128)(2,1)S(1)} %collective-permute-done.5.refs_2_.refs_4_), channel_id=1, source_target_pairs={{0,16},{16,0},{1,17},{17,1},{2,18},{18,2},{3,19},{19,3},{4,20},{20... | collective-permute-start | bytes 1622024 | tf_op jit(solution)/shard_map/ppermute | solution.py:210
  57.3 14.7 %collective-permute-start.9 = (bf16[2,512,128]{2,1,0:T(8,128)(2,1)S(1)}, bf16[2,512,128]{2,1,0:T(8,128)(2,1)S(1)}, u32[]{:S(2)}, u32[]{:S(2)}) collective-permute-start(bf16[2,512,128]{2,1,0:T(8,128)(2,1)S(1)} %pad_maximum_fusion.1.refs_4_.refs_6_), channel_id=1, source_target_pairs={{0,3},{1,0},{2,1},{3,2},{4,7},{5,4},{6,5},{7,6},{8,11},{9,8},{10,9... | collective-permute-start | bytes 786440 | tf_op jit(solution)/shard_map/ppermute | solution.py:209
  62.4 11.0 %collective-permute-start.8 = (bf16[2,512,128]{2,1,0:T(8,128)(2,1)S(1)}, bf16[2,512,128]{2,1,0:T(8,128)(2,1)S(1)}, u32[]{:S(2)}, u32[]{:S(2)}) collective-permute-start(bf16[2,512,128]{2,1,0:T(8,128)(2,1)S(1)} %pad_maximum_fusion.1.refs_4_.refs_6_), channel_id=1, source_target_pairs={{0,2},{1,3},{2,0},{3,1},{4,6},{5,7},{6,4},{7,5},{8,10},{9,11},{10,... | collective-permute-start | bytes 786440 | tf_op jit(solution)/shard_map/ppermute | solution.py:209
  64.3 15.3 %collective-permute-start.7 = (bf16[2,512,128]{2,1,0:T(8,128)(2,1)S(1)}, bf16[2,512,128]{2,1,0:T(8,128)(2,1)S(1)}, u32[]{:S(2)}, u32[]{:S(2)}) collective-permute-start(bf16[2,512,128]{2,1,0:T(8,128)(2,1)S(1)} %pad_maximum_fusion.1.refs_4_.refs_6_), channel_id=1, source_target_pairs={{0,1},{1,2},{2,3},{3,0},{4,5},{5,6},{6,7},{7,4},{8,9},{9,10},{10,1... | collective-permute-start | bytes 786440 | tf_op jit(solution)/shard_map/ppermute | solution.py:209
  72.0 0.7 copy-start
  73.4 0.7 copy-start.2
  79.6 0.7 copy-start.4
  80.4 1.0 copy-start.1
  81.3 0.9 copy-start.3
  82.3 0.9 copy-start.5
  100.3 31.5 %all-to-all-start.2 = ((f16[32,72,128]{2,1,0:T(8,128)(2,1)}), f16[32,72,128]{2,1,0:T(8,128)(2,1)S(1)}, u32[]{:S(2)}, u32[]{:S(2)}) async-start(f16[32,72,128]{2,1,0:T(8,128)(2,1)} %bitcast.10), calls=%async_computation.2 | async-start | bytes 1179648 | tf_op jit(solution)/shard_map/all_to_all | solution.py:241
  112.0 18.2 %collective-permute-start.10 = (f32[1,128]{1,0:T(1,128)S(1)}, f32[1,128]{1,0:T(1,128)S(1)}, u32[]{:S(2)}, u32[]{:S(2)}) collective-permute-start(f32[1,128]{1,0:T(1,128)S(1)} %get-tuple-element.13), channel_id=1, source_target_pairs={{0,0},{1,1},{2,2},{3,3},{16,4},{17,5},{18,6},{19,7},{32,8},{33,9},... | collective-permute-start | bytes 1544 | tf_op jit(solution)/shard_map/ppermute | solution.py:244

commit v3 on v2

--- a/solution.py
+++ b/solution.py
@@ -11,6 +11,7 @@
 
 
 INTERPRET = False
+HBM = pltpu.HBM
 CLIP = 600.0
 BLOCK = 128
 COLS = 64
@@ -42,8 +43,16 @@
     return dict(yl=j // 2, c=j % 2, yh=c * 2 + yl, x=(x + k) % 4)
 
 
-def prep_kernel(ids_ref, a_ref, g_ref, *rest):
-    outs, gt_ref = rest[:4], rest[4]
+def prep_kernel(ids_in, a_in, g_in, *rest):
+    outs, gt_ref, ids_ref, a_ref, g_ref, sems = rest[:4], *rest[4:]
+    copies = [
+        pltpu.make_async_copy(src, dst, sems.at[n])
+        for n, (src, dst) in enumerate(((g_in, g_ref), (ids_in, ids_ref), (a_in, a_ref)))
+    ]
+    for cp in copies:
+        cp.start()
+    copies[0].wait()
+    copies[1].wait()
     x, yh = lax.axis_index("x"), lax.axis_index("yh")
     chunks = g_ref.shape[1] // BLOCK
     ids = ids_ref[...]
@@ -54,6 +63,7 @@
         t = g_ref[:, n * BLOCK : (n + 1) * BLOCK].astype(jnp.float32).T
         gt_ref[n * BLOCK : (n + 1) * BLOCK, :] = jnp.where(kept, t, 0.0).astype(jnp.bfloat16)
     wide = chunks * BLOCK // 4
+    copies[2].wait()
     for n, k in enumerate(ORDER):
         i = (x + k) % 4
         j = yh ^ k
@@ -70,12 +80,6 @@
     return lax.axis_index("x"), lax.axis_index("yl") * 2 + lax.axis_index("c")
 
 
-def grads_of(parts, back, n, x):
-    if n < 2:
-        return parts[4 + back][n]
-    return parts[8][(x + 4 - back) % 4, n - 2]
-
-
 def features(slab):
     return jnp.concatenate([slab[r * BLOCK : (r + 1) * BLOCK] for r in range(4)], axis=1)
 
@@ -85,12 +89,20 @@
 
 
 def norm_kernel(*refs):
-    parts, out, a_s, g_s, acc, starts, norms = refs[:9], *refs[9:]
+    parts, out, a_s, g_s, acc, starts, norms, sems = refs[:9], *refs[9:]
     x, j = here()
+    copies = []
+    for n, k in enumerate(ORDER[2:]):
+        for m in range(4):
+            at = (j ^ k) * 4 + (m + 4 - k) % 4
+            copies.append(pltpu.make_async_copy(parts[8].at[m, n], g_s.at[at], sems.at[len(copies)]))
+    for cp in copies:
+        cp.start()
     for n, k in enumerate(ORDER):
         for m in range(4):
             a_s[(j ^ (m ^ k)) * 4 + (x + 4 - k) % 4] = parts[m][n]
-            g_s[(j ^ k) * 4 + (x + 8 - m - k) % 4] = grads_of(parts, m, n, x)
+            if n < 2:
+                g_s[(j ^ k) * 4 + (x + 8 - m - k) % 4] = parts[4 + m][n]
     a_s[SLABS] = jnp.zeros(a_s.shape[1:], a_s.dtype)
     norms[...] = jnp.zeros_like(norms)
     doc = jnp.int32(-1)
@@ -103,6 +115,8 @@
 
         doc = this
     starts[DOCS] = SLABS
+    for cp in copies:
+        cp.wait()
     lane = lax.broadcasted_iota(jnp.int32, (1, BLOCK), 1)
     second = lax.broadcasted_iota(jnp.int32, (1, 2 * BLOCK), 1) >= BLOCK
 
@@ -142,22 +156,31 @@
 
 def grad_kernel(*refs):
     norms, own, parts = refs[0], refs[1], refs[2:11]
-    out, clip_out, g_s, acc = refs[11:]
+    out, clip_out, g_s, acc, late, sem = refs[11:]
     x, _ = here()
+    copy = pltpu.make_async_copy(parts[8], late, sem)
+    copy.start()
     norm_sq = jnp.sum(norms[...], axis=0)
     clip = CLIP / jnp.sqrt(jnp.maximum(norm_sq, CLIP * CLIP))
-    clip_out[...] = clip
+    clip_out[...] = clip[:, :DOCS]
     bound = jnp.sum(jnp.minimum(jnp.sqrt(own[0]), CLIP), axis=1, keepdims=True)
     shift = jnp.ceil(jnp.log2(jnp.maximum(bound, 1e-18))) - 14.0
     lane = lax.broadcasted_iota(jnp.int32, (1, BLOCK), 1).astype(jnp.float32)
     acts = []
-    for n, k in enumerate(ORDER):
-        for m in range(4):
-            a = parts[m][n]
-            factor = jnp.sum(jnp.where(number(a)[0:1] == lane, clip, 0.0), axis=1, keepdims=True)
-            g = grads_of(parts, (k - (m ^ k)) % 4, ORDER.index(m ^ k), x)
-            g_s[len(acts)] = (g.astype(jnp.float32) * factor).astype(jnp.bfloat16)
-            acts.append(features(a))
+    for half in range(2):
+        if half:
+            copy.wait()
+        for n, k in enumerate(ORDER):
+            for m in range(4):
+                kg = m ^ k
+                ng, back = ORDER.index(kg), (k - kg) % 4
+                if (ng >= 2) != half:
+                    continue
+                a = parts[m][n]
+                g = late[(x + 4 - back) % 4, ng - 2] if half else parts[4 + back][ng]
+                factor = jnp.sum(jnp.where(number(a)[0:1] == lane, clip, 0.0), axis=1, keepdims=True)
+                g_s[len(acts)] = (g.astype(jnp.float32) * factor).astype(jnp.bfloat16)
+                acts.append(features(a))
     acc[...] = jnp.dot(
         jnp.concatenate([g_s[t] for t in range(SLABS)], axis=1),
         jnp.concatenate(acts, axis=0),
@@ -172,24 +195,35 @@
             out[z, y, COLS:] = tail
 
 
+def hbm(p):
+    return p if INTERPRET else pltpu.with_memory_space_constraint(p, HBM)
+
+
 def body(sizes, activations, out_grads, segment_ids):
     a, g, ids = activations[0], out_grads[0], segment_ids
     levels = sizes["zh"] * sizes["zl"]
     wide = levels * COLS
     bf16, f32 = jnp.bfloat16, jnp.float32
     vmem = pl.BlockSpec(memory_space=pltpu.VMEM)
+    anywhere = pl.BlockSpec(memory_space=HBM)
     small = pltpu.CompilerParams(vmem_limit_bytes=20 << 20)
 
     payload = pl.pallas_call(
         prep_kernel,
         out_shape=[jax.ShapeDtypeStruct((wide + PART + PAD, BLOCK), bf16)] * 4,
-        in_specs=[vmem, vmem, vmem],
+        in_specs=[anywhere] * 3,
         out_specs=[vmem] * 4,
-        scratch_shapes=[pltpu.VMEM((g.shape[1], BLOCK), bf16)],
+        scratch_shapes=[
+            pltpu.VMEM((g.shape[1], BLOCK), bf16),
+            pltpu.VMEM(ids.shape, ids.dtype),
+            pltpu.VMEM(a.shape, bf16),
+            pltpu.VMEM(g.shape, bf16),
+            pltpu.SemaphoreType.DMA((3,)),
+        ],
         interpret=INTERPRET,
         compiler_params=small,
         name="prep",
-    )(ids, a, g)
+    )(*[hbm(p) for p in (ids, a, g)])
 
     arrived = [
         lax.ppermute(payload[n], MOVE, table(sizes, MOVE, functools.partial(to_group, k)))
@@ -209,19 +243,19 @@
         g_parts.append(lax.ppermute(own_g, "x", [(s, (s + m) % 4) for s in range(4)]))
     partner_other = lax.ppermute(partner, "c", flip)
     a_parts = [own_a, own_other, partner, partner_other]
-    parts = a_parts + g_parts + [last_g]
+    parts = a_parts + g_parts + [hbm(last_g)]
 
     acts = pltpu.VMEM((SLABS + 1, PART + PAD, BLOCK), bf16)
     grads = pltpu.VMEM((SLABS + 1, wide, BLOCK), bf16)
     total = pltpu.VMEM((wide, PART), f32)
     starts = pltpu.SMEM((DOCS + 1,), jnp.int32)
-    row = jax.ShapeDtypeStruct((1, BLOCK), f32)
+    row = jax.ShapeDtypeStruct((1, DOCS), f32)
     partial = pl.pallas_call(
         norm_kernel,
         out_shape=jax.ShapeDtypeStruct((16, 1, BLOCK), f32),
-        in_specs=[vmem] * 9,
+        in_specs=[vmem] * 8 + [anywhere],
         out_specs=vmem,
-        scratch_shapes=[acts, grads, total, starts, pltpu.VMEM((1, BLOCK), f32)],
+        scratch_shapes=[acts, grads, total, starts, pltpu.VMEM((1, BLOCK), f32), pltpu.SemaphoreType.DMA((8,))],
         interpret=INTERPRET,
         compiler_params=small,
         name="norms",
@@ -230,9 +264,9 @@
     pieces, clip = pl.pallas_call(
         grad_kernel,
         out_shape=[jax.ShapeDtypeStruct((levels, 4, COLS + TAIL, BLOCK), f32), row],
-        in_specs=[vmem, vmem] + [vmem] * 9,
+        in_specs=[vmem] * 10 + [anywhere],
         out_specs=[vmem] * 2,
-        scratch_shapes=[grads, total],
+        scratch_shapes=[grads, total, pltpu.VMEM(last_g.shape, bf16), pltpu.SemaphoreType.DMA],
         interpret=INTERPRET,
         compiler_params=small,
         name="grads",
@@ -242,7 +276,7 @@
     weight_grad = jnp.sum(summands[:, :COLS] * jnp.exp2(summands[:, COLS : COLS + 1]), axis=0).T
     home = [(dst, src) for src, dst in table(sizes, MOVE, functools.partial(to_group, 0))]
     clip = lax.ppermute(clip, MOVE, home)
-    return weight_grad, clip[:, :DOCS]
+    return weight_grad, clip
 
 
 def solution(mesh):

time: 135 us -> 132 us (0.978)
  local copies, waits for them, and re-layouts: 9.37 us -> 1.73 us
  Pallas kernels: 6.32 us -> 9.72 us
  waiting for transfers between devices: 38 us -> 39.9 us
    unnamed x19 -> x1, local copies, waits for them, and re-layouts: 8.16 us -> 0.51 us
    ppermute x3, waiting for transfers between devices: 11.5 us -> 13.3 us  [body(): lax.ppermute(own_g, 'x', [(s, (s + m) % 4) for s in range(4)])]
where the time goes in v3:
time: 132 us; the launch traced here: 130 us
  starting transfers between devices  66.5 us (50%)
  waiting for transfers between devices  39.9 us (30%)
  blocking collectives  9.75 us (7%)
  Pallas kernels  9.72 us (7%)
  other arithmetic  1.85 us (1%)
  local copies, waits for them, and re-layouts  1.73 us (1%)
    ppermute x4, starting transfers between devices, body(): lax.ppermute(payload[n], MOVE, table(sizes, MOVE, functools.partial(to_gr...  21.8 us
    ppermute x3, waiting for transfers between devices, body(): lax.ppermute(own_g, 'x', [(s, (s + m) % 4) for s in range(4)])  13.3 us
    ppermute x1, waiting for transfers between devices, body(): clip = lax.ppermute(clip, MOVE, home)  13 us
    ppermute x4, waiting for transfers between devices, body(): lax.ppermute(payload[n], MOVE, table(sizes, MOVE, functools.partial(to_gr...  11.9 us
    all_to_all x1, starting transfers between devices, body(): lax.all_to_all(pieces, SUMMED, split_axis=0, concat_axis=0, tiled=True)  11.6 us
    all_to_all x1, blocking collectives, body(): lax.all_to_all(partial, GROUP, split_axis=0, concat_axis=0, tiled=True)  9.75 us
    ppermute x3, starting transfers between devices, body(): lax.ppermute(own_g, 'x', [(s, (s + m) % 4) for s in range(4)])  9.5 us
    ppermute x1, starting transfers between devices, body(): own_other = lax.ppermute(own_a, 'c', flip)  8.42 us
  transfers between devices with their start and end apart: 13, of which 8 were waited for; matrix products, arithmetic and copies ran while one was open for 1% of the time, Pallas kernels for 0%

profile of v3, /device:TPU:1, one launch (start us, length us, event | category | flops | bytes accessed | tf_op | source)
XLA Modules:
  0.0 130.3 jit_solution(1756522311438219956)
XLA Ops:
  0.6 1.5 %prep.1 = (bf16[1040,128]{1,0:T(8,128)(2,1)S(1)}, bf16[1040,128]{1,0:T(8,128)(2,1)S(1)}, bf16[1040,128]{1,0:T(8,128)(2,1)S(1)}, bf16[1040,128]{1,0:T(8,128)(2,1)S(1)}) custom-call(s32[1,128]{1,0:T(1,128)} %ids_in.1, bf16[128,2048]{1,0:T(8,128)(2,1)} %bitcast.21, bf16[128,2048]{1,0:T(8,128)(2,1)} %bitcast.22), custom_call_target="tpu_custom_call" | custom-call | tf_op jit(solution)/shard_map/prep/pallas_call | solution.py:211
  2.1 9.2 %collective-permute-start = (bf16[1040,128]{1,0:T(8,128)(2,1)S(1)}, bf16[1040,128]{1,0:T(8,128)(2,1)S(1)}, u32[]{:S(2)}, u32[]{:S(2)}) collective-permute-start(bf16[1040,128]{1,0:T(8,128)(2,1)S(1)} %get-tuple-element.8), channel_id=1, source_target_pairs={{0,17},{1,18},{2,19},{3,16},{4,1},{5,2},{6,3},{7,0},{8,49},{9,50},... | collective-permute-start | bytes 798728 | tf_op jit(solution)/shard_map/ppermute | solution.py:229
  11.3 2.8 %collective-permute-start.1 = (bf16[1040,128]{1,0:T(8,128)(2,1)S(1)}, bf16[1040,128]{1,0:T(8,128)(2,1)S(1)}, u32[]{:S(2)}, u32[]{:S(2)}) collective-permute-start(bf16[1040,128]{1,0:T(8,128)(2,1)S(1)} %get-tuple-element.9), channel_id=1, source_target_pairs={{0,51},{1,48},{2,49},{3,50},{4,35},{5,32},{6,33},{7,34},{8,19},{9,... | collective-permute-start | bytes 798728 | tf_op jit(solution)/shard_map/ppermute | solution.py:229
  14.1 7.8 %collective-permute-start.2 = (bf16[1040,128]{1,0:T(8,128)(2,1)S(1)}, bf16[1040,128]{1,0:T(8,128)(2,1)S(1)}, u32[]{:S(2)}, u32[]{:S(2)}) collective-permute-start(bf16[1040,128]{1,0:T(8,128)(2,1)S(1)} %get-tuple-element.10), channel_id=1, source_target_pairs={{0,0},{1,1},{2,2},{3,3},{4,16},{5,17},{6,18},{7,19},{8,32},{9,33},... | collective-permute-start | bytes 798728 | tf_op jit(solution)/shard_map/ppermute | solution.py:229
  22.0 1.9 %collective-permute-start.3 = (bf16[1040,128]{1,0:T(8,128)(2,1)S(1)}, bf16[1040,128]{1,0:T(8,128)(2,1)S(1)}, u32[]{:S(2)}, u32[]{:S(2)}) collective-permute-start(bf16[1040,128]{1,0:T(8,128)(2,1)S(1)} %get-tuple-element.11), channel_id=1, source_target_pairs={{0,34},{1,35},{2,32},{3,33},{4,50},{5,51},{6,48},{7,49},{8,2},{9,3... | collective-permute-start | bytes 798728 | tf_op jit(solution)/shard_map/ppermute | solution.py:229
  24.0 10.4 %collective-permute-done.1 = bf16[1040,128]{1,0:T(8,128)(2,1)S(1)} collective-permute-done((bf16[1040,128]{1,0:T(8,128)(2,1)S(1)}, bf16[1040,128]{1,0:T(8,128)(2,1)S(1)}, u32[]{:S(2)}, u32[]{:S(2)}) %collective-permute-start.1) | collective-permute-done | bytes 266272 | tf_op jit(solution)/shard_map/ppermute | solution.py:229
  34.4 0.6 collective-permute-done.2
  35.0 0.9 collective-permute-done.3
  35.9 0.1 pad_maximum_fusion.refs_0_.refs_2_
  36.0 1.9 %collective-permute-start.5 = (bf16[4,528,128]{2,1,0:T(8,128)(2,1)S(1)}, bf16[4,528,128]{2,1,0:T(8,128)(2,1)S(1)}, u32[]{:S(2)}, u32[]{:S(2)}) collective-permute-start(bf16[4,528,128]{2,1,0:T(8,128)(2,1)S(1)} %pad_maximum_fusion.refs_0_.refs_2_), channel_id=1, source_target_pairs={{0,32},{32,0},{1,33},{33,1},{2,34},{34,2},{3,35},{35,3},{4,36},{36... | collective-permute-start | bytes 1622024 | tf_op jit(solution)/shard_map/ppermute | solution.py:239
  37.9 8.4 %collective-permute-start.4 = (bf16[4,528,128]{2,1,0:T(8,128)(2,1)S(1)}, bf16[4,528,128]{2,1,0:T(8,128)(2,1)S(1)}, u32[]{:S(2)}, u32[]{:S(2)}) collective-permute-start(bf16[4,528,128]{2,1,0:T(8,128)(2,1)S(1)} %pad_maximum_fusion.refs_0_.refs_2_), channel_id=1, source_target_pairs={{0,16},{16,0},{1,17},{17,1},{2,18},{18,2},{3,19},{19,3},{4,20},{20... | collective-permute-start | bytes 1622024 | tf_op jit(solution)/shard_map/ppermute | solution.py:240
  46.4 1.1 broadcast_in_dim.3
  47.5 4.2 %all-to-all-start = ((bf16[4,2,512,128]{3,2,1,0:T(8,128)(2,1)}), bf16[4,2,512,128]{3,2,1,0:T(8,128)(2,1)}, u32[]{:S(2)}, u32[]{:S(2)}) async-start(bf16[4,2,512,128]{3,2,1,0:T(8,128)(2,1)} %broadcast_in_dim.3), calls=%async_computation | async-start | bytes 2097152 | tf_op jit(solution)/shard_map/all_to_all | solution.py:234
  51.8 0.0 collective-permute-done.5.refs_2_.refs_4_
  51.8 3.8 %collective-permute-start.6 = (bf16[4,528,128]{2,1,0:T(8,128)(2,1)S(1)}, bf16[4,528,128]{2,1,0:T(8,128)(2,1)S(1)}, u32[]{:S(2)}, u32[]{:S(2)}) collective-permute-start(bf16[4,528,128]{2,1,0:T(8,128)(2,1)S(1)} %collective-permute-done.5.refs_2_.refs_4_), channel_id=1, source_target_pairs={{0,16},{16,0},{1,17},{17,1},{2,18},{18,2},{3,19},{19,3},{4,20},{20... | collective-permute-start | bytes 1622024 | tf_op jit(solution)/shard_map/ppermute | solution.py:244
  55.7 5.1 %collective-permute-start.9 = (bf16[2,512,128]{2,1,0:T(8,128)(2,1)S(1)}, bf16[2,512,128]{2,1,0:T(8,128)(2,1)S(1)}, u32[]{:S(2)}, u32[]{:S(2)}) collective-permute-start(bf16[2,512,128]{2,1,0:T(8,128)(2,1)S(1)} %pad_maximum_fusion.1.refs_4_.refs_6_), channel_id=1, source_target_pairs={{0,3},{1,0},{2,1},{3,2},{4,7},{5,4},{6,5},{7,6},{8,11},{9,8},{10,9... | collective-permute-start | bytes 786440 | tf_op jit(solution)/shard_map/ppermute | solution.py:243
  60.8 1.9 %collective-permute-start.8 = (bf16[2,512,128]{2,1,0:T(8,128)(2,1)S(1)}, bf16[2,512,128]{2,1,0:T(8,128)(2,1)S(1)}, u32[]{:S(2)}, u32[]{:S(2)}) collective-permute-start(bf16[2,512,128]{2,1,0:T(8,128)(2,1)S(1)} %pad_maximum_fusion.1.refs_4_.refs_6_), channel_id=1, source_target_pairs={{0,2},{1,3},{2,0},{3,1},{4,6},{5,7},{6,4},{7,5},{8,10},{9,11},{10,... | collective-permute-start | bytes 786440 | tf_op jit(solution)/shard_map/ppermute | solution.py:243
  62.7 2.5 %collective-permute-start.7 = (bf16[2,512,128]{2,1,0:T(8,128)(2,1)S(1)}, bf16[2,512,128]{2,1,0:T(8,128)(2,1)S(1)}, u32[]{:S(2)}, u32[]{:S(2)}) collective-permute-start(bf16[2,512,128]{2,1,0:T(8,128)(2,1)S(1)} %pad_maximum_fusion.1.refs_4_.refs_6_), channel_id=1, source_target_pairs={{0,1},{1,2},{2,3},{3,0},{4,5},{5,6},{6,7},{7,4},{8,9},{9,10},{10,1... | collective-permute-start | bytes 786440 | tf_op jit(solution)/shard_map/ppermute | solution.py:243
  65.2 5.9 %collective-permute-done.9.refs_7_.refs_9_ = bf16[2,512,128]{2,1,0:T(8,128)(2,1)S(1)} collective-permute-done((bf16[2,512,128]{2,1,0:T(8,128)(2,1)S(1)}, bf16[2,512,128]{2,1,0:T(8,128)(2,1)S(1)}, u32[]{:S(2)}, u32[]{:S(2)}) %collective-permute-start.9) | collective-permute-done | bytes 262176 | tf_op jit(solution)/shard_map/ppermute | solution.py:243
  71.1 1.5 %collective-permute-done.8.refs_6_.refs_8_ = bf16[2,512,128]{2,1,0:T(8,128)(2,1)S(1)} collective-permute-done((bf16[2,512,128]{2,1,0:T(8,128)(2,1)S(1)}, bf16[2,512,128]{2,1,0:T(8,128)(2,1)S(1)}, u32[]{:S(2)}, u32[]{:S(2)}) %collective-permute-start.8) | collective-permute-done | bytes 262176 | tf_op jit(solution)/shard_map/ppermute | solution.py:243
  72.6 6.0 %collective-permute-done.7.refs_5_.refs_7_ = bf16[2,512,128]{2,1,0:T(8,128)(2,1)S(1)} collective-permute-done((bf16[2,512,128]{2,1,0:T(8,128)(2,1)S(1)}, bf16[2,512,128]{2,1,0:T(8,128)(2,1)S(1)}, u32[]{:S(2)}, u32[]{:S(2)}) %collective-permute-start.7) | collective-permute-done | bytes 262176 | tf_op jit(solution)/shard_map/ppermute | solution.py:243
  78.6 5.8 %norms.1.refs_1_ = f32[16,1,128]{2,1,0:T(1,128)S(1)} custom-call(bf16[4,528,128]{2,1,0:T(8,128)(2,1)S(1)} %pad_maximum_fusion.refs_0_.refs_2_, bf16[4,528,128]{2,1,0:T(8,128)(2,1)S(1)} %collective-permute-done.4.refs_1_.refs_3_, bf16[4,528,128]{2,1,0:T(8,128)(2,1)S(1)} %collective-permute-done.5.refs_2_.refs_4_, ...), custom_call_target="tpu_custom_call" | custom-call | tf_op jit(solution)/shard_map/norms/pallas_call | solution.py:253
  84.3 9.8 %all_to_all.15.refs_0_ = f32[16,1,128]{2,1,0:T(1,128)S(1)} all-to-all(f32[16,1,128]{2,1,0:T(1,128)S(1)} %norms.1.refs_1_), channel_id=1, replica_groups=mesh['zh'=4,'zl'=2,'yl'=2,'c'=2,'yh'=4,'x'=4] {'yl','c','x'}, dimensions={0} | all-to-all | bytes 16384 | tf_op jit(solution)/shard_map/all_to_all | solution.py:263
  94.1 2.5 %grads.1 = (f32[8,4,72,128]{3,2,1,0:T(8,128)S(1)}, f32[1,8]{1,0:T(1,128)S(1)}) custom-call(f32[16,1,128]{2,1,0:T(1,128)S(1)} %all_to_all.15.refs_0_, f32[16,1,128]{2,1,0:T(1,128)S(1)} %norms.1.refs_1_, bf16[4,528,128]{2,1,0:T(8,128)(2,1)S(1)} %pad_maximum_fusion.refs_0_.refs_2_, bf16[4,528,128]{2,1,0:T(8,128)(2,1)S(1)} %collective-permute-done.4.refs_1_.refs_3_, ...), custom_call_target="tpu_custom_call" | custom-call | tf_op jit(solution)/shard_map/grads/pallas_call | solution.py:264
  96.6 0.9 convert_element_type.6
  97.5 11.6 %all-to-all-start.2 = ((f16[32,72,128]{2,1,0:T(8,128)(2,1)}), f16[32,72,128]{2,1,0:T(8,128)(2,1)S(1)}, u32[]{:S(2)}, u32[]{:S(2)}) async-start(f16[32,72,128]{2,1,0:T(8,128)(2,1)} %bitcast.10), calls=%async_computation.2 | async-start | bytes 1179648 | tf_op jit(solution)/shard_map/all_to_all | solution.py:275
  109.1 5.2 %collective-permute-start.10 = (f32[1,8]{1,0:T(1,128)S(1)}, f32[1,8]{1,0:T(1,128)S(1)}, u32[]{:S(2)}, u32[]{:S(2)}) collective-permute-start(f32[1,8]{1,0:T(1,128)S(1)} %get-tuple-element.13), channel_id=1, source_target_pairs={{0,0},{1,1},{2,2},{3,3},{16,4},{17,5},{18,6},{19,7},{32,8},{33,9},... | collective-permute-start | bytes 104 | tf_op jit(solution)/shard_map/ppermute | solution.py:278
  114.3 13.0 %collective-permute-done.10 = f32[1,8]{1,0:T(1,128)S(1)} collective-permute-done((f32[1,8]{1,0:T(1,128)S(1)}, f32[1,8]{1,0:T(1,128)S(1)}, u32[]{:S(2)}, u32[]{:S(2)}) %collective-permute-start.10) | collective-permute-done | bytes 64 | tf_op jit(solution)/shard_map/ppermute | solution.py:278
  127.3 1.6 %all-to-all-done.2 = f16[32,72,128]{2,1,0:T(8,128)(2,1)S(1)} async-done(((f16[32,72,128]{2,1,0:T(8,128)(2,1)}), f16[32,72,128]{2,1,0:T(8,128)(2,1)S(1)}, u32[]{:S(2)}, u32[]{:S(2)}) %all-to-all-start.2) | async-done | bytes 589856 | tf_op jit(solution)/shard_map/all_to_all | solution.py:275
  128.9 0.1 convert_element_type.7
  129.0 0.7 fusion
  129.8 0.5 copy.6
  (15 shorter events, 0.2 us)
Async XLA Ops:
  2.1 21.8 %collective-permute-start = (bf16[1040,128]{1,0:T(8,128)(2,1)S(1)}, bf16[1040,128]{1,0:T(8,128)(2,1)S(1)}, u32[]{:S(2)}, u32[]{:S(2)}) collective-permute-start(bf16[1040,128]{1,0:T(8,128)(2,1)S(1)} %get-tuple-element.8), channel_id=1, source_target_pairs={{0,17},{1,18},{2,19},{3,16},{4,1},{5,2},{6,3},{7,0},{8,49},{9,50},... | collective-permute-start | bytes 798728 | tf_op jit(solution)/shard_map/ppermute | solution.py:229
  11.3 23.1 %collective-permute-start.1 = (bf16[1040,128]{1,0:T(8,128)(2,1)S(1)}, bf16[1040,128]{1,0:T(8,128)(2,1)S(1)}, u32[]{:S(2)}, u32[]{:S(2)}) collective-permute-start(bf16[1040,128]{1,0:T(8,128)(2,1)S(1)} %get-tuple-element.9), channel_id=1, source_target_pairs={{0,51},{1,48},{2,49},{3,50},{4,35},{5,32},{6,33},{7,34},{8,19},{9,... | collective-permute-start | bytes 798728 | tf_op jit(solution)/shard_map/ppermute | solution.py:229
  14.1 20.8 %collective-permute-start.2 = (bf16[1040,128]{1,0:T(8,128)(2,1)S(1)}, bf16[1040,128]{1,0:T(8,128)(2,1)S(1)}, u32[]{:S(2)}, u32[]{:S(2)}) collective-permute-start(bf16[1040,128]{1,0:T(8,128)(2,1)S(1)} %get-tuple-element.10), channel_id=1, source_target_pairs={{0,0},{1,1},{2,2},{3,3},{4,16},{5,17},{6,18},{7,19},{8,32},{9,33},... | collective-permute-start | bytes 798728 | tf_op jit(solution)/shard_map/ppermute | solution.py:229
  22.0 13.9 %collective-permute-start.3 = (bf16[1040,128]{1,0:T(8,128)(2,1)S(1)}, bf16[1040,128]{1,0:T(8,128)(2,1)S(1)}, u32[]{:S(2)}, u32[]{:S(2)}) collective-permute-start(bf16[1040,128]{1,0:T(8,128)(2,1)S(1)} %get-tuple-element.11), channel_id=1, source_target_pairs={{0,34},{1,35},{2,32},{3,33},{4,50},{5,51},{6,48},{7,49},{8,2},{9,3... | collective-permute-start | bytes 798728 | tf_op jit(solution)/shard_map/ppermute | solution.py:229
  36.0 15.8 %collective-permute-start.5 = (bf16[4,528,128]{2,1,0:T(8,128)(2,1)S(1)}, bf16[4,528,128]{2,1,0:T(8,128)(2,1)S(1)}, u32[]{:S(2)}, u32[]{:S(2)}) collective-permute-start(bf16[4,528,128]{2,1,0:T(8,128)(2,1)S(1)} %pad_maximum_fusion.refs_0_.refs_2_), channel_id=1, source_target_pairs={{0,32},{32,0},{1,33},{33,1},{2,34},{34,2},{3,35},{35,3},{4,36},{36... | collective-permute-start | bytes 1622024 | tf_op jit(solution)/shard_map/ppermute | solution.py:239
  37.9 40.7 %collective-permute-start.4 = (bf16[4,528,128]{2,1,0:T(8,128)(2,1)S(1)}, bf16[4,528,128]{2,1,0:T(8,128)(2,1)S(1)}, u32[]{:S(2)}, u32[]{:S(2)}) collective-permute-start(bf16[4,528,128]{2,1,0:T(8,128)(2,1)S(1)} %pad_maximum_fusion.refs_0_.refs_2_), channel_id=1, source_target_pairs={{0,16},{16,0},{1,17},{17,1},{2,18},{18,2},{3,19},{19,3},{4,20},{20... | collective-permute-start | bytes 1622024 | tf_op jit(solution)/shard_map/ppermute | solution.py:240
  47.5 31.0 %all-to-all-start = ((bf16[4,2,512,128]{3,2,1,0:T(8,128)(2,1)}), bf16[4,2,512,128]{3,2,1,0:T(8,128)(2,1)}, u32[]{:S(2)}, u32[]{:S(2)}) async-start(bf16[4,2,512,128]{3,2,1,0:T(8,128)(2,1)} %broadcast_in_dim.3), calls=%async_computation | async-start | bytes 2097152 | tf_op jit(solution)/shard_map/all_to_all | solution.py:234
  51.8 26.7 %collective-permute-start.6 = (bf16[4,528,128]{2,1,0:T(8,128)(2,1)S(1)}, bf16[4,528,128]{2,1,0:T(8,128)(2,1)S(1)}, u32[]{:S(2)}, u32[]{:S(2)}) collective-permute-start(bf16[4,528,128]{2,1,0:T(8,128)(2,1)S(1)} %collective-permute-done.5.refs_2_.refs_4_), channel_id=1, source_target_pairs={{0,16},{16,0},{1,17},{17,1},{2,18},{18,2},{3,19},{19,3},{4,20},{20... | collective-permute-start | bytes 1622024 | tf_op jit(solution)/shard_map/ppermute | solution.py:244
  55.7 15.4 %collective-permute-start.9 = (bf16[2,512,128]{2,1,0:T(8,128)(2,1)S(1)}, bf16[2,512,128]{2,1,0:T(8,128)(2,1)S(1)}, u32[]{:S(2)}, u32[]{:S(2)}) collective-permute-start(bf16[2,512,128]{2,1,0:T(8,128)(2,1)S(1)} %pad_maximum_fusion.1.refs_4_.refs_6_), channel_id=1, source_target_pairs={{0,3},{1,0},{2,1},{3,2},{4,7},{5,4},{6,5},{7,6},{8,11},{9,8},{10,9... | collective-permute-start | bytes 786440 | tf_op jit(solution)/shard_map/ppermute | solution.py:243
  60.8 11.8 %collective-permute-start.8 = (bf16[2,512,128]{2,1,0:T(8,128)(2,1)S(1)}, bf16[2,512,128]{2,1,0:T(8,128)(2,1)S(1)}, u32[]{:S(2)}, u32[]{:S(2)}) collective-permute-start(bf16[2,512,128]{2,1,0:T(8,128)(2,1)S(1)} %pad_maximum_fusion.1.refs_4_.refs_6_), channel_id=1, source_target_pairs={{0,2},{1,3},{2,0},{3,1},{4,6},{5,7},{6,4},{7,5},{8,10},{9,11},{10,... | collective-permute-start | bytes 786440 | tf_op jit(solution)/shard_map/ppermute | solution.py:243
  62.7 15.8 %collective-permute-start.7 = (bf16[2,512,128]{2,1,0:T(8,128)(2,1)S(1)}, bf16[2,512,128]{2,1,0:T(8,128)(2,1)S(1)}, u32[]{:S(2)}, u32[]{:S(2)}) collective-permute-start(bf16[2,512,128]{2,1,0:T(8,128)(2,1)S(1)} %pad_maximum_fusion.1.refs_4_.refs_6_), channel_id=1, source_target_pairs={{0,1},{1,2},{2,3},{3,0},{4,5},{5,6},{6,7},{7,4},{8,9},{9,10},{10,1... | collective-permute-start | bytes 786440 | tf_op jit(solution)/shard_map/ppermute | solution.py:243
  97.5 31.4 %all-to-all-start.2 = ((f16[32,72,128]{2,1,0:T(8,128)(2,1)}), f16[32,72,128]{2,1,0:T(8,128)(2,1)S(1)}, u32[]{:S(2)}, u32[]{:S(2)}) async-start(f16[32,72,128]{2,1,0:T(8,128)(2,1)} %bitcast.10), calls=%async_computation.2 | async-start | bytes 1179648 | tf_op jit(solution)/shard_map/all_to_all | solution.py:275
  109.1 18.2 %collective-permute-start.10 = (f32[1,8]{1,0:T(1,128)S(1)}, f32[1,8]{1,0:T(1,128)S(1)}, u32[]{:S(2)}, u32[]{:S(2)}) collective-permute-start(f32[1,8]{1,0:T(1,128)S(1)} %get-tuple-element.13), channel_id=1, source_target_pairs={{0,0},{1,1},{2,2},{3,3},{16,4},{17,5},{18,6},{19,7},{32,8},{33,9},... | collective-permute-start | bytes 104 | tf_op jit(solution)/shard_map/ppermute | solution.py:278

commit v4 on v3

--- a/solution.py
+++ b/solution.py
@@ -25,7 +25,7 @@
 AXES = ("zh", "zl", "yl", "c", "yh", "x")
 MOVE = ("yl", "c", "yh", "x")
 GROUP = ("yl", "c", "x")
-SUMMED = ("zh", "zl", "yh")
+LEVELS = ("zh", "zl")
 
 
 def table(sizes, axes, to):
@@ -271,9 +271,11 @@
         compiler_params=small,
         name="grads",
     )(norms, partial, *parts)
-    pieces = pieces.astype(jnp.float16).reshape(levels * 4, COLS + TAIL, BLOCK)
-    summands = lax.all_to_all(pieces, SUMMED, split_axis=0, concat_axis=0, tiled=True).astype(f32)
-    weight_grad = jnp.sum(summands[:, :COLS] * jnp.exp2(summands[:, COLS : COLS + 1]), axis=0).T
+    pieces = pieces.astype(jnp.float16)
+    shares = lax.all_to_all(pieces, LEVELS, split_axis=0, concat_axis=0, tiled=True).astype(f32)
+    shares = jnp.sum(shares[:, :, :COLS] * jnp.exp2(shares[:, :, COLS : COLS + 1]), axis=0)
+    summands = lax.all_to_all(shares, "yh", split_axis=0, concat_axis=0, tiled=True)
+    weight_grad = jnp.sum(summands, axis=0).T
     home = [(dst, src) for src, dst in table(sizes, MOVE, functools.partial(to_group, 0))]
     clip = lax.ppermute(clip, MOVE, home)
     return weight_grad, clip

time: 132 us -> 141 us (1.068)
  blocking collectives: 9.75 us -> 37.3 us
  waiting for transfers between devices: 39.9 us -> 29.5 us
  starting transfers between devices: 66.5 us -> 59.7 us
    all_to_all x0 -> x1, blocking collectives: none -> 27.6 us  [body(): lax.all_to_all(pieces, LEVELS, split_axis=0, concat_axis=0, tiled=True)]
    ppermute x1, waiting for transfers between devices: 13 us -> 4.25 us  [body(): clip = lax.ppermute(clip, MOVE, home)]
    all_to_all x1, starting transfers between devices: 11.6 us -> 3.32 us  [body(): lax.all_to_all(shares, 'yh', split_axis=0, concat_axis=0, tiled=True)]
    all_to_all x1, waiting for transfers between devices: 1.62 us -> 0.01 us  [body(): lax.all_to_all(shares, 'yh', split_axis=0, concat_axis=0, tiled=True)]
    ppermute x1, starting transfers between devices: 5.16 us -> 6.69 us  [body(): clip = lax.ppermute(clip, MOVE, home)]
  transfers between devices with their start and end apart: 13 -> 13, of which waited for: 8 -> 7; matrix products, arithmetic and copies ran while one was open for 1% -> 1% of each run, Pallas kernels for 0% -> 0%
where the time goes in v4:
time: 141 us
  starting transfers between devices  59.7 us (42%)
  blocking collectives  37.3 us (26%)
  waiting for transfers between devices  29.5 us (21%)
  Pallas kernels  9.74 us (7%)
  local copies, waits for them, and re-layouts  1.73 us (1%)
  other arithmetic  1.65 us (1%)
    all_to_all x1, blocking collectives, body(): lax.all_to_all(pieces, LEVELS, split_axis=0, concat_axis=0, tiled=True)  27.6 us
    ppermute x4, starting transfers between devices, body(): lax.ppermute(payload[n], MOVE, table(sizes, MOVE, functools.partial(to_gr...  21.8 us
    ppermute x3, waiting for transfers between devices, body(): lax.ppermute(own_g, 'x', [(s, (s + m) % 4) for s in range(4)])  13.3 us
    ppermute x4, waiting for transfers between devices, body(): lax.ppermute(payload[n], MOVE, table(sizes, MOVE, functools.partial(to_gr...  11.9 us
    all_to_all x1, blocking collectives, body(): lax.all_to_all(partial, GROUP, split_axis=0, concat_axis=0, tiled=True)  9.72 us
    ppermute x3, starting transfers between devices, body(): lax.ppermute(own_g, 'x', [(s, (s + m) % 4) for s in range(4)])  9.5 us
    ppermute x1, starting transfers between devices, body(): own_other = lax.ppermute(own_a, 'c', flip)  8.42 us
    ppermute x1, starting transfers between devices, body(): clip = lax.ppermute(clip, MOVE, home)  6.69 us
  transfers between devices with their start and end apart: 13, of which 7 were waited for; matrix products, arithmetic and copies ran while one was open for 1% of the time, Pallas kernels for 0%

profile of v4, /device:TPU:1, one launch (start us, length us, event | category | flops | bytes accessed | tf_op | source)
XLA Modules:
  0.0 140.5 jit_solution(10850679088947554470)
XLA Ops:
  0.6 1.5 %prep.1 = (bf16[1040,128]{1,0:T(8,128)(2,1)S(1)}, bf16[1040,128]{1,0:T(8,128)(2,1)S(1)}, bf16[1040,128]{1,0:T(8,128)(2,1)S(1)}, bf16[1040,128]{1,0:T(8,128)(2,1)S(1)}) custom-call(s32[1,128]{1,0:T(1,128)} %ids_in.1, bf16[128,2048]{1,0:T(8,128)(2,1)} %bitcast.20, bf16[128,2048]{1,0:T(8,128)(2,1)} %bitcast.21), custom_call_target="tpu_custom_call" | custom-call | tf_op jit(solution)/shard_map/prep/pallas_call | solution.py:211
  2.1 9.2 %collective-permute-start = (bf16[1040,128]{1,0:T(8,128)(2,1)S(1)}, bf16[1040,128]{1,0:T(8,128)(2,1)S(1)}, u32[]{:S(2)}, u32[]{:S(2)}) collective-permute-start(bf16[1040,128]{1,0:T(8,128)(2,1)S(1)} %get-tuple-element.8), channel_id=1, source_target_pairs={{0,17},{1,18},{2,19},{3,16},{4,1},{5,2},{6,3},{7,0},{8,49},{9,50},... | collective-permute-start | bytes 798728 | tf_op jit(solution)/shard_map/ppermute | solution.py:229
  11.3 2.8 %collective-permute-start.1 = (bf16[1040,128]{1,0:T(8,128)(2,1)S(1)}, bf16[1040,128]{1,0:T(8,128)(2,1)S(1)}, u32[]{:S(2)}, u32[]{:S(2)}) collective-permute-start(bf16[1040,128]{1,0:T(8,128)(2,1)S(1)} %get-tuple-element.9), channel_id=1, source_target_pairs={{0,51},{1,48},{2,49},{3,50},{4,35},{5,32},{6,33},{7,34},{8,19},{9,... | collective-permute-start | bytes 798728 | tf_op jit(solution)/shard_map/ppermute | solution.py:229
  14.1 7.8 %collective-permute-start.2 = (bf16[1040,128]{1,0:T(8,128)(2,1)S(1)}, bf16[1040,128]{1,0:T(8,128)(2,1)S(1)}, u32[]{:S(2)}, u32[]{:S(2)}) collective-permute-start(bf16[1040,128]{1,0:T(8,128)(2,1)S(1)} %get-tuple-element.10), channel_id=1, source_target_pairs={{0,0},{1,1},{2,2},{3,3},{4,16},{5,17},{6,18},{7,19},{8,32},{9,33},... | collective-permute-start | bytes 798728 | tf_op jit(solution)/shard_map/ppermute | solution.py:229
  22.0 1.9 %collective-permute-start.3 = (bf16[1040,128]{1,0:T(8,128)(2,1)S(1)}, bf16[1040,128]{1,0:T(8,128)(2,1)S(1)}, u32[]{:S(2)}, u32[]{:S(2)}) collective-permute-start(bf16[1040,128]{1,0:T(8,128)(2,1)S(1)} %get-tuple-element.11), channel_id=1, source_target_pairs={{0,34},{1,35},{2,32},{3,33},{4,50},{5,51},{6,48},{7,49},{8,2},{9,3... | collective-permute-start | bytes 798728 | tf_op jit(solution)/shard_map/ppermute | solution.py:229
  24.0 10.4 %collective-permute-done.1 = bf16[1040,128]{1,0:T(8,128)(2,1)S(1)} collective-permute-done((bf16[1040,128]{1,0:T(8,128)(2,1)S(1)}, bf16[1040,128]{1,0:T(8,128)(2,1)S(1)}, u32[]{:S(2)}, u32[]{:S(2)}) %collective-permute-start.1) | collective-permute-done | bytes 266272 | tf_op jit(solution)/shard_map/ppermute | solution.py:229
  34.4 0.6 collective-permute-done.2
  35.0 0.9 collective-permute-done.3
  35.9 0.1 pad_maximum_fusion.refs_0_.refs_2_
  36.0 1.9 %collective-permute-start.5 = (bf16[4,528,128]{2,1,0:T(8,128)(2,1)S(1)}, bf16[4,528,128]{2,1,0:T(8,128)(2,1)S(1)}, u32[]{:S(2)}, u32[]{:S(2)}) collective-permute-start(bf16[4,528,128]{2,1,0:T(8,128)(2,1)S(1)} %pad_maximum_fusion.refs_0_.refs_2_), channel_id=1, source_target_pairs={{0,32},{32,0},{1,33},{33,1},{2,34},{34,2},{3,35},{35,3},{4,36},{36... | collective-permute-start | bytes 1622024 | tf_op jit(solution)/shard_map/ppermute | solution.py:239
  37.9 8.4 %collective-permute-start.4 = (bf16[4,528,128]{2,1,0:T(8,128)(2,1)S(1)}, bf16[4,528,128]{2,1,0:T(8,128)(2,1)S(1)}, u32[]{:S(2)}, u32[]{:S(2)}) collective-permute-start(bf16[4,528,128]{2,1,0:T(8,128)(2,1)S(1)} %pad_maximum_fusion.refs_0_.refs_2_), channel_id=1, source_target_pairs={{0,16},{16,0},{1,17},{17,1},{2,18},{18,2},{3,19},{19,3},{4,20},{20... | collective-permute-start | bytes 1622024 | tf_op jit(solution)/shard_map/ppermute | solution.py:240
  46.4 1.1 broadcast_in_dim.3
  47.5 4.2 %all-to-all-start = ((bf16[4,2,512,128]{3,2,1,0:T(8,128)(2,1)}), bf16[4,2,512,128]{3,2,1,0:T(8,128)(2,1)}, u32[]{:S(2)}, u32[]{:S(2)}) async-start(bf16[4,2,512,128]{3,2,1,0:T(8,128)(2,1)} %broadcast_in_dim.3), calls=%async_computation | async-start | bytes 2097152 | tf_op jit(solution)/shard_map/all_to_all | solution.py:234
  51.8 3.8 %collective-permute-start.6 = (bf16[4,528,128]{2,1,0:T(8,128)(2,1)S(1)}, bf16[4,528,128]{2,1,0:T(8,128)(2,1)S(1)}, u32[]{:S(2)}, u32[]{:S(2)}) collective-permute-start(bf16[4,528,128]{2,1,0:T(8,128)(2,1)S(1)} %collective-permute-done.5.refs_2_.refs_4_), channel_id=1, source_target_pairs={{0,16},{16,0},{1,17},{17,1},{2,18},{18,2},{3,19},{19,3},{4,20},{20... | collective-permute-start | bytes 1622024 | tf_op jit(solution)/shard_map/ppermute | solution.py:244
  55.7 5.1 %collective-permute-start.9 = (bf16[2,512,128]{2,1,0:T(8,128)(2,1)S(1)}, bf16[2,512,128]{2,1,0:T(8,128)(2,1)S(1)}, u32[]{:S(2)}, u32[]{:S(2)}) collective-permute-start(bf16[2,512,128]{2,1,0:T(8,128)(2,1)S(1)} %pad_maximum_fusion.1.refs_4_.refs_6_), channel_id=1, source_target_pairs={{0,3},{1,0},{2,1},{3,2},{4,7},{5,4},{6,5},{7,6},{8,11},{9,8},{10,9... | collective-permute-start | bytes 786440 | tf_op jit(solution)/shard_map/ppermute | solution.py:243
  60.8 1.9 %collective-permute-start.8 = (bf16[2,512,128]{2,1,0:T(8,128)(2,1)S(1)}, bf16[2,512,128]{2,1,0:T(8,128)(2,1)S(1)}, u32[]{:S(2)}, u32[]{:S(2)}) collective-permute-start(bf16[2,512,128]{2,1,0:T(8,128)(2,1)S(1)} %pad_maximum_fusion.1.refs_4_.refs_6_), channel_id=1, source_target_pairs={{0,2},{1,3},{2,0},{3,1},{4,6},{5,7},{6,4},{7,5},{8,10},{9,11},{10,... | collective-permute-start | bytes 786440 | tf_op jit(solution)/shard_map/ppermute | solution.py:243
  62.7 2.5 %collective-permute-start.7 = (bf16[2,512,128]{2,1,0:T(8,128)(2,1)S(1)}, bf16[2,512,128]{2,1,0:T(8,128)(2,1)S(1)}, u32[]{:S(2)}, u32[]{:S(2)}) collective-permute-start(bf16[2,512,128]{2,1,0:T(8,128)(2,1)S(1)} %pad_maximum_fusion.1.refs_4_.refs_6_), channel_id=1, source_target_pairs={{0,1},{1,2},{2,3},{3,0},{4,5},{5,6},{6,7},{7,4},{8,9},{9,10},{10,1... | collective-permute-start | bytes 786440 | tf_op jit(solution)/shard_map/ppermute | solution.py:243
  65.2 5.9 %collective-permute-done.9.refs_7_.refs_9_ = bf16[2,512,128]{2,1,0:T(8,128)(2,1)S(1)} collective-permute-done((bf16[2,512,128]{2,1,0:T(8,128)(2,1)S(1)}, bf16[2,512,128]{2,1,0:T(8,128)(2,1)S(1)}, u32[]{:S(2)}, u32[]{:S(2)}) %collective-permute-start.9) | collective-permute-done | bytes 262176 | tf_op jit(solution)/shard_map/ppermute | solution.py:243
  71.1 1.5 %collective-permute-done.8.refs_6_.refs_8_ = bf16[2,512,128]{2,1,0:T(8,128)(2,1)S(1)} collective-permute-done((bf16[2,512,128]{2,1,0:T(8,128)(2,1)S(1)}, bf16[2,512,128]{2,1,0:T(8,128)(2,1)S(1)}, u32[]{:S(2)}, u32[]{:S(2)}) %collective-permute-start.8) | collective-permute-done | bytes 262176 | tf_op jit(solution)/shard_map/ppermute | solution.py:243
  72.6 6.0 %collective-permute-done.7.refs_5_.refs_7_ = bf16[2,512,128]{2,1,0:T(8,128)(2,1)S(1)} collective-permute-done((bf16[2,512,128]{2,1,0:T(8,128)(2,1)S(1)}, bf16[2,512,128]{2,1,0:T(8,128)(2,1)S(1)}, u32[]{:S(2)}, u32[]{:S(2)}) %collective-permute-start.7) | collective-permute-done | bytes 262176 | tf_op jit(solution)/shard_map/ppermute | solution.py:243
  78.6 5.8 %norms.1.refs_1_ = f32[16,1,128]{2,1,0:T(1,128)S(1)} custom-call(bf16[4,528,128]{2,1,0:T(8,128)(2,1)S(1)} %pad_maximum_fusion.refs_0_.refs_2_, bf16[4,528,128]{2,1,0:T(8,128)(2,1)S(1)} %collective-permute-done.4.refs_1_.refs_3_, bf16[4,528,128]{2,1,0:T(8,128)(2,1)S(1)} %collective-permute-done.5.refs_2_.refs_4_, ...), custom_call_target="tpu_custom_call" | custom-call | tf_op jit(solution)/shard_map/norms/pallas_call | solution.py:253
  84.3 9.7 %all_to_all.20.refs_0_ = f32[16,1,128]{2,1,0:T(1,128)S(1)} all-to-all(f32[16,1,128]{2,1,0:T(1,128)S(1)} %norms.1.refs_1_), channel_id=1, replica_groups=mesh['zh'=4,'zl'=2,'yl'=2,'c'=2,'yh'=4,'x'=4] {'yl','c','x'}, dimensions={0} | all-to-all | bytes 16384 | tf_op jit(solution)/shard_map/all_to_all | solution.py:263
  94.1 2.5 %grads.1 = (f32[8,4,72,128]{3,2,1,0:T(8,128)S(1)}, f32[1,8]{1,0:T(1,128)S(1)}) custom-call(f32[16,1,128]{2,1,0:T(1,128)S(1)} %all_to_all.20.refs_0_, f32[16,1,128]{2,1,0:T(1,128)S(1)} %norms.1.refs_1_, bf16[4,528,128]{2,1,0:T(8,128)(2,1)S(1)} %pad_maximum_fusion.refs_0_.refs_2_, bf16[4,528,128]{2,1,0:T(8,128)(2,1)S(1)} %collective-permute-done.4.refs_1_.refs_3_, ...), custom_call_target="tpu_custom_call" | custom-call | tf_op jit(solution)/shard_map/grads/pallas_call | solution.py:264
  96.6 0.1 convert_element_type.6
  96.7 27.6 %all_to_all.21 = f16[8,4,72,128]{3,2,1,0:T(8,128)(2,1)S(1)} all-to-all(f16[8,4,72,128]{3,2,1,0:T(8,128)(2,1)S(1)} %convert_element_type.6), channel_id=1, replica_groups=mesh['zh'=4,'zl'=2,'yl'=2,'c'=2,'yh'=4,'x'=4] {'zh','zl'}, dimensions={0} | all-to-all | bytes 1179648 | tf_op jit(solution)/shard_map/all_to_all | solution.py:275
  124.3 0.1 convert_element_type.7
  124.4 0.7 fusion
  125.1 3.3 %all-to-all-start.3 = ((f32[4,64,128]{2,1,0:T(8,128)}), f32[4,64,128]{2,1,0:T(8,128)S(1)}, u32[]{:S(2)}, u32[]{:S(2)}) async-start(f32[4,64,128]{2,1,0:T(8,128)} %fusion), calls=%async_computation.3 | async-start | bytes 262144 | tf_op jit(solution)/shard_map/all_to_all | solution.py:277
  128.4 6.7 %collective-permute-start.10 = (f32[1,8]{1,0:T(1,128)S(1)}, f32[1,8]{1,0:T(1,128)S(1)}, u32[]{:S(2)}, u32[]{:S(2)}) collective-permute-start(f32[1,8]{1,0:T(1,128)S(1)} %get-tuple-element.13), channel_id=1, source_target_pairs={{0,0},{1,1},{2,2},{3,3},{16,4},{17,5},{18,6},{19,7},{32,8},{33,9},... | collective-permute-start | bytes 104 | tf_op jit(solution)/shard_map/ppermute | solution.py:280
  135.1 4.2 %collective-permute-done.10 = f32[1,8]{1,0:T(1,128)S(1)} collective-permute-done((f32[1,8]{1,0:T(1,128)S(1)}, f32[1,8]{1,0:T(1,128)S(1)}, u32[]{:S(2)}, u32[]{:S(2)}) %collective-permute-start.10) | collective-permute-done | bytes 64 | tf_op jit(solution)/shard_map/ppermute | solution.py:280
  139.4 0.6 reduce_sum.19
  140.0 0.5 copy.6
  (17 shorter events, 0.2 us)
Async XLA Ops:
  2.1 21.8 %collective-permute-start = (bf16[1040,128]{1,0:T(8,128)(2,1)S(1)}, bf16[1040,128]{1,0:T(8,128)(2,1)S(1)}, u32[]{:S(2)}, u32[]{:S(2)}) collective-permute-start(bf16[1040,128]{1,0:T(8,128)(2,1)S(1)} %get-tuple-element.8), channel_id=1, source_target_pairs={{0,17},{1,18},{2,19},{3,16},{4,1},{5,2},{6,3},{7,0},{8,49},{9,50},... | collective-permute-start | bytes 798728 | tf_op jit(solution)/shard_map/ppermute | solution.py:229
  11.3 23.1 %collective-permute-start.1 = (bf16[1040,128]{1,0:T(8,128)(2,1)S(1)}, bf16[1040,128]{1,0:T(8,128)(2,1)S(1)}, u32[]{:S(2)}, u32[]{:S(2)}) collective-permute-start(bf16[1040,128]{1,0:T(8,128)(2,1)S(1)} %get-tuple-element.9), channel_id=1, source_target_pairs={{0,51},{1,48},{2,49},{3,50},{4,35},{5,32},{6,33},{7,34},{8,19},{9,... | collective-permute-start | bytes 798728 | tf_op jit(solution)/shard_map/ppermute | solution.py:229
  14.1 20.8 %collective-permute-start.2 = (bf16[1040,128]{1,0:T(8,128)(2,1)S(1)}, bf16[1040,128]{1,0:T(8,128)(2,1)S(1)}, u32[]{:S(2)}, u32[]{:S(2)}) collective-permute-start(bf16[1040,128]{1,0:T(8,128)(2,1)S(1)} %get-tuple-element.10), channel_id=1, source_target_pairs={{0,0},{1,1},{2,2},{3,3},{4,16},{5,17},{6,18},{7,19},{8,32},{9,33},... | collective-permute-start | bytes 798728 | tf_op jit(solution)/shard_map/ppermute | solution.py:229
  22.0 13.9 %collective-permute-start.3 = (bf16[1040,128]{1,0:T(8,128)(2,1)S(1)}, bf16[1040,128]{1,0:T(8,128)(2,1)S(1)}, u32[]{:S(2)}, u32[]{:S(2)}) collective-permute-start(bf16[1040,128]{1,0:T(8,128)(2,1)S(1)} %get-tuple-element.11), channel_id=1, source_target_pairs={{0,34},{1,35},{2,32},{3,33},{4,50},{5,51},{6,48},{7,49},{8,2},{9,3... | collective-permute-start | bytes 798728 | tf_op jit(solution)/shard_map/ppermute | solution.py:229
  36.0 15.8 %collective-permute-start.5 = (bf16[4,528,128]{2,1,0:T(8,128)(2,1)S(1)}, bf16[4,528,128]{2,1,0:T(8,128)(2,1)S(1)}, u32[]{:S(2)}, u32[]{:S(2)}) collective-permute-start(bf16[4,528,128]{2,1,0:T(8,128)(2,1)S(1)} %pad_maximum_fusion.refs_0_.refs_2_), channel_id=1, source_target_pairs={{0,32},{32,0},{1,33},{33,1},{2,34},{34,2},{3,35},{35,3},{4,36},{36... | collective-permute-start | bytes 1622024 | tf_op jit(solution)/shard_map/ppermute | solution.py:239
  37.9 40.7 %collective-permute-start.4 = (bf16[4,528,128]{2,1,0:T(8,128)(2,1)S(1)}, bf16[4,528,128]{2,1,0:T(8,128)(2,1)S(1)}, u32[]{:S(2)}, u32[]{:S(2)}) collective-permute-start(bf16[4,528,128]{2,1,0:T(8,128)(2,1)S(1)} %pad_maximum_fusion.refs_0_.refs_2_), channel_id=1, source_target_pairs={{0,16},{16,0},{1,17},{17,1},{2,18},{18,2},{3,19},{19,3},{4,20},{20... | collective-permute-start | bytes 1622024 | tf_op jit(solution)/shard_map/ppermute | solution.py:240
  47.5 31.0 %all-to-all-start = ((bf16[4,2,512,128]{3,2,1,0:T(8,128)(2,1)}), bf16[4,2,512,128]{3,2,1,0:T(8,128)(2,1)}, u32[]{:S(2)}, u32[]{:S(2)}) async-start(bf16[4,2,512,128]{3,2,1,0:T(8,128)(2,1)} %broadcast_in_dim.3), calls=%async_computation | async-start | bytes 2097152 | tf_op jit(solution)/shard_map/all_to_all | solution.py:234
  51.8 26.7 %collective-permute-start.6 = (bf16[4,528,128]{2,1,0:T(8,128)(2,1)S(1)}, bf16[4,528,128]{2,1,0:T(8,128)(2,1)S(1)}, u32[]{:S(2)}, u32[]{:S(2)}) collective-permute-start(bf16[4,528,128]{2,1,0:T(8,128)(2,1)S(1)} %collective-permute-done.5.refs_2_.refs_4_), channel_id=1, source_target_pairs={{0,16},{16,0},{1,17},{17,1},{2,18},{18,2},{3,19},{19,3},{4,20},{20... | collective-permute-start | bytes 1622024 | tf_op jit(solution)/shard_map/ppermute | solution.py:244
  55.7 15.4 %collective-permute-start.9 = (bf16[2,512,128]{2,1,0:T(8,128)(2,1)S(1)}, bf16[2,512,128]{2,1,0:T(8,128)(2,1)S(1)}, u32[]{:S(2)}, u32[]{:S(2)}) collective-permute-start(bf16[2,512,128]{2,1,0:T(8,128)(2,1)S(1)} %pad_maximum_fusion.1.refs_4_.refs_6_), channel_id=1, source_target_pairs={{0,3},{1,0},{2,1},{3,2},{4,7},{5,4},{6,5},{7,6},{8,11},{9,8},{10,9... | collective-permute-start | bytes 786440 | tf_op jit(solution)/shard_map/ppermute | solution.py:243
  60.8 11.8 %collective-permute-start.8 = (bf16[2,512,128]{2,1,0:T(8,128)(2,1)S(1)}, bf16[2,512,128]{2,1,0:T(8,128)(2,1)S(1)}, u32[]{:S(2)}, u32[]{:S(2)}) collective-permute-start(bf16[2,512,128]{2,1,0:T(8,128)(2,1)S(1)} %pad_maximum_fusion.1.refs_4_.refs_6_), channel_id=1, source_target_pairs={{0,2},{1,3},{2,0},{3,1},{4,6},{5,7},{6,4},{7,5},{8,10},{9,11},{10,... | collective-permute-start | bytes 786440 | tf_op jit(solution)/shard_map/ppermute | solution.py:243
  62.7 15.8 %collective-permute-start.7 = (bf16[2,512,128]{2,1,0:T(8,128)(2,1)S(1)}, bf16[2,512,128]{2,1,0:T(8,128)(2,1)S(1)}, u32[]{:S(2)}, u32[]{:S(2)}) collective-permute-start(bf16[2,512,128]{2,1,0:T(8,128)(2,1)S(1)} %pad_maximum_fusion.1.refs_4_.refs_6_), channel_id=1, source_target_pairs={{0,1},{1,2},{2,3},{3,0},{4,5},{5,6},{6,7},{7,4},{8,9},{9,10},{10,1... | collective-permute-start | bytes 786440 | tf_op jit(solution)/shard_map/ppermute | solution.py:243
  125.1 14.3 %all-to-all-start.3 = ((f32[4,64,128]{2,1,0:T(8,128)}), f32[4,64,128]{2,1,0:T(8,128)S(1)}, u32[]{:S(2)}, u32[]{:S(2)}) async-start(f32[4,64,128]{2,1,0:T(8,128)} %fusion), calls=%async_computation.3 | async-start | bytes 262144 | tf_op jit(solution)/shard_map/all_to_all | solution.py:277
  128.4 11.0 %collective-permute-start.10 = (f32[1,8]{1,0:T(1,128)S(1)}, f32[1,8]{1,0:T(1,128)S(1)}, u32[]{:S(2)}, u32[]{:S(2)}) collective-permute-start(f32[1,8]{1,0:T(1,128)S(1)} %get-tuple-element.13), channel_id=1, source_target_pairs={{0,0},{1,1},{2,2},{3,3},{16,4},{17,5},{18,6},{19,7},{32,8},{33,9},... | collective-permute-start | bytes 104 | tf_op jit(solution)/shard_map/ppermute | solution.py:280

commit v5 on v3

--- a/solution.py
+++ b/solution.py
@@ -25,7 +25,7 @@
 AXES = ("zh", "zl", "yl", "c", "yh", "x")
 MOVE = ("yl", "c", "yh", "x")
 GROUP = ("yl", "c", "x")
-SUMMED = ("zh", "zl", "yh")
+SUMMED = ("yh", "zh", "zl")
 
 
 def table(sizes, axes, to):
@@ -89,7 +89,7 @@
 
 
 def norm_kernel(*refs):
-    parts, out, a_s, g_s, acc, starts, norms, sems = refs[:9], *refs[9:]
+    parts, out, a_s, g_s, acc, starts, numbers, norms, sems = refs[:9], *refs[9:]
     x, j = here()
     copies = []
     for n, k in enumerate(ORDER[2:]):
@@ -100,20 +100,19 @@
         cp.start()
     for n, k in enumerate(ORDER):
         for m in range(4):
-            a_s[(j ^ (m ^ k)) * 4 + (x + 4 - k) % 4] = parts[m][n]
+            t = (j ^ (m ^ k)) * 4 + (x + 4 - k) % 4
+            a_s[t] = parts[m][n]
+            numbers[t] = jnp.max(number(parts[m][n])[0:1]).astype(jnp.int32)
             if n < 2:
                 g_s[(j ^ k) * 4 + (x + 8 - m - k) % 4] = parts[4 + m][n]
     a_s[SLABS] = jnp.zeros(a_s.shape[1:], a_s.dtype)
     norms[...] = jnp.zeros_like(norms)
-    doc = jnp.int32(-1)
+    reached, doc = [], jnp.int32(0)
     for t in range(SLABS):
-        this = jnp.maximum(doc, jnp.max(number(a_s[t])).astype(jnp.int32))
-
-        @pl.when(this != doc)
-        def _(this=this, t=t):
-            starts[this] = t
-
-        doc = this
+        doc = jnp.maximum(doc, numbers[t])
+        reached.append(doc)
+    for t in reversed(range(SLABS)):
+        starts[reached[t]] = t
     starts[DOCS] = SLABS
     for cp in copies:
         cp.wait()
@@ -188,11 +187,11 @@
     )
     scale = jnp.exp2(-shift)
     tail = jnp.broadcast_to(shift, (TAIL, BLOCK))
-    for z in range(out.shape[0]):
+    for z in range(out.shape[1]):
         for y in range(4):
             piece = acc[z * COLS : (z + 1) * COLS, y * BLOCK : (y + 1) * BLOCK]
-            out[z, y, :COLS] = piece * scale
-            out[z, y, COLS:] = tail
+            out[y, z, :COLS] = piece * scale
+            out[y, z, COLS:] = tail
 
 
 def hbm(p):
@@ -255,7 +254,7 @@
         out_shape=jax.ShapeDtypeStruct((16, 1, BLOCK), f32),
         in_specs=[vmem] * 8 + [anywhere],
         out_specs=vmem,
-        scratch_shapes=[acts, grads, total, starts, pltpu.VMEM((1, BLOCK), f32), pltpu.SemaphoreType.DMA((8,))],
+        scratch_shapes=[acts, grads, total, starts, pltpu.SMEM((SLABS,), jnp.int32), pltpu.VMEM((1, BLOCK), f32), pltpu.SemaphoreType.DMA((8,))],
         interpret=INTERPRET,
         compiler_params=small,
         name="norms",
@@ -263,7 +262,7 @@
     norms = lax.all_to_all(partial, GROUP, split_axis=0, concat_axis=0, tiled=True)
     pieces, clip = pl.pallas_call(
         grad_kernel,
-        out_shape=[jax.ShapeDtypeStruct((levels, 4, COLS + TAIL, BLOCK), f32), row],
+        out_shape=[jax.ShapeDtypeStruct((4, levels, COLS + TAIL, BLOCK), f32), row],
         in_specs=[vmem] * 10 + [anywhere],
         out_specs=[vmem] * 2,
         scratch_shapes=[grads, total, pltpu.VMEM(last_g.shape, bf16), pltpu.SemaphoreType.DMA],

time: 132 us -> 131 us (level)
  no operation moved by 1% of the time
where the time goes in v5:
time: 131 us
  starting transfers between devices  66.5 us (51%)
  waiting for transfers between devices  40.2 us (31%)
  Pallas kernels  9.74 us (7%)
  blocking collectives  9.72 us (7%)
  other arithmetic  1.85 us (1%)
  local copies, waits for them, and re-layouts  1.73 us (1%)
    ppermute x4, starting transfers between devices, body(): lax.ppermute(payload[n], MOVE, table(sizes, MOVE, functools.partial(to_gr...  21.8 us
    ppermute x3, waiting for transfers between devices, body(): lax.ppermute(own_g, 'x', [(s, (s + m) % 4) for s in range(4)])  13.3 us
    ppermute x1, waiting for transfers between devices, body(): clip = lax.ppermute(clip, MOVE, home)  12.6 us
    ppermute x4, waiting for transfers between devices, body(): lax.ppermute(payload[n], MOVE, table(sizes, MOVE, functools.partial(to_gr...  11.9 us
    all_to_all x1, starting transfers between devices, body(): lax.all_to_all(pieces, SUMMED, split_axis=0, concat_axis=0, tiled=True)  11.6 us
    all_to_all x1, blocking collectives, body(): lax.all_to_all(partial, GROUP, split_axis=0, concat_axis=0, tiled=True)  9.72 us
    ppermute x3, starting transfers between devices, body(): lax.ppermute(own_g, 'x', [(s, (s + m) % 4) for s in range(4)])  9.5 us
    ppermute x1, starting transfers between devices, body(): own_other = lax.ppermute(own_a, 'c', flip)  8.42 us
  transfers between devices with their start and end apart: 13, of which 8 were waited for; matrix products, arithmetic and copies ran while one was open for 1% of the time, Pallas kernels for 0%

profile of v5, /device:TPU:1, one launch (start us, length us, event | category | flops | bytes accessed | tf_op | source)
XLA Modules:
  0.0 130.6 jit_solution(14998685891978456498)
XLA Ops:
  0.6 1.5 %prep.1 = (bf16[1040,128]{1,0:T(8,128)(2,1)S(1)}, bf16[1040,128]{1,0:T(8,128)(2,1)S(1)}, bf16[1040,128]{1,0:T(8,128)(2,1)S(1)}, bf16[1040,128]{1,0:T(8,128)(2,1)S(1)}) custom-call(s32[1,128]{1,0:T(1,128)} %ids_in.1, bf16[128,2048]{1,0:T(8,128)(2,1)} %bitcast.21, bf16[128,2048]{1,0:T(8,128)(2,1)} %bitcast.22), custom_call_target="tpu_custom_call" | custom-call | tf_op jit(solution)/shard_map/prep/pallas_call | solution.py:210
  2.1 9.2 %collective-permute-start = (bf16[1040,128]{1,0:T(8,128)(2,1)S(1)}, bf16[1040,128]{1,0:T(8,128)(2,1)S(1)}, u32[]{:S(2)}, u32[]{:S(2)}) collective-permute-start(bf16[1040,128]{1,0:T(8,128)(2,1)S(1)} %get-tuple-element.8), channel_id=1, source_target_pairs={{0,17},{1,18},{2,19},{3,16},{4,1},{5,2},{6,3},{7,0},{8,49},{9,50},... | collective-permute-start | bytes 798728 | tf_op jit(solution)/shard_map/ppermute | solution.py:228
  11.3 2.8 %collective-permute-start.1 = (bf16[1040,128]{1,0:T(8,128)(2,1)S(1)}, bf16[1040,128]{1,0:T(8,128)(2,1)S(1)}, u32[]{:S(2)}, u32[]{:S(2)}) collective-permute-start(bf16[1040,128]{1,0:T(8,128)(2,1)S(1)} %get-tuple-element.9), channel_id=1, source_target_pairs={{0,51},{1,48},{2,49},{3,50},{4,35},{5,32},{6,33},{7,34},{8,19},{9,... | collective-permute-start | bytes 798728 | tf_op jit(solution)/shard_map/ppermute | solution.py:228
  14.1 7.8 %collective-permute-start.2 = (bf16[1040,128]{1,0:T(8,128)(2,1)S(1)}, bf16[1040,128]{1,0:T(8,128)(2,1)S(1)}, u32[]{:S(2)}, u32[]{:S(2)}) collective-permute-start(bf16[1040,128]{1,0:T(8,128)(2,1)S(1)} %get-tuple-element.10), channel_id=1, source_target_pairs={{0,0},{1,1},{2,2},{3,3},{4,16},{5,17},{6,18},{7,19},{8,32},{9,33},... | collective-permute-start | bytes 798728 | tf_op jit(solution)/shard_map/ppermute | solution.py:228
  22.0 1.9 %collective-permute-start.3 = (bf16[1040,128]{1,0:T(8,128)(2,1)S(1)}, bf16[1040,128]{1,0:T(8,128)(2,1)S(1)}, u32[]{:S(2)}, u32[]{:S(2)}) collective-permute-start(bf16[1040,128]{1,0:T(8,128)(2,1)S(1)} %get-tuple-element.11), channel_id=1, source_target_pairs={{0,34},{1,35},{2,32},{3,33},{4,50},{5,51},{6,48},{7,49},{8,2},{9,3... | collective-permute-start | bytes 798728 | tf_op jit(solution)/shard_map/ppermute | solution.py:228
  24.0 10.4 %collective-permute-done.1 = bf16[1040,128]{1,0:T(8,128)(2,1)S(1)} collective-permute-done((bf16[1040,128]{1,0:T(8,128)(2,1)S(1)}, bf16[1040,128]{1,0:T(8,128)(2,1)S(1)}, u32[]{:S(2)}, u32[]{:S(2)}) %collective-permute-start.1) | collective-permute-done | bytes 266272 | tf_op jit(solution)/shard_map/ppermute | solution.py:228
  34.4 0.6 collective-permute-done.2
  35.0 0.9 collective-permute-done.3
  35.9 0.1 pad_maximum_fusion.refs_0_.refs_2_
  36.0 1.9 %collective-permute-start.5 = (bf16[4,528,128]{2,1,0:T(8,128)(2,1)S(1)}, bf16[4,528,128]{2,1,0:T(8,128)(2,1)S(1)}, u32[]{:S(2)}, u32[]{:S(2)}) collective-permute-start(bf16[4,528,128]{2,1,0:T(8,128)(2,1)S(1)} %pad_maximum_fusion.refs_0_.refs_2_), channel_id=1, source_target_pairs={{0,32},{32,0},{1,33},{33,1},{2,34},{34,2},{3,35},{35,3},{4,36},{36... | collective-permute-start | bytes 1622024 | tf_op jit(solution)/shard_map/ppermute | solution.py:238
  37.9 8.4 %collective-permute-start.4 = (bf16[4,528,128]{2,1,0:T(8,128)(2,1)S(1)}, bf16[4,528,128]{2,1,0:T(8,128)(2,1)S(1)}, u32[]{:S(2)}, u32[]{:S(2)}) collective-permute-start(bf16[4,528,128]{2,1,0:T(8,128)(2,1)S(1)} %pad_maximum_fusion.refs_0_.refs_2_), channel_id=1, source_target_pairs={{0,16},{16,0},{1,17},{17,1},{2,18},{18,2},{3,19},{19,3},{4,20},{20... | collective-permute-start | bytes 1622024 | tf_op jit(solution)/shard_map/ppermute | solution.py:239
  46.4 1.1 broadcast_in_dim.3
  47.5 4.2 %all-to-all-start = ((bf16[4,2,512,128]{3,2,1,0:T(8,128)(2,1)}), bf16[4,2,512,128]{3,2,1,0:T(8,128)(2,1)}, u32[]{:S(2)}, u32[]{:S(2)}) async-start(bf16[4,2,512,128]{3,2,1,0:T(8,128)(2,1)} %broadcast_in_dim.3), calls=%async_computation | async-start | bytes 2097152 | tf_op jit(solution)/shard_map/all_to_all | solution.py:233
  51.8 0.0 collective-permute-done.5.refs_2_.refs_4_
  51.8 3.8 %collective-permute-start.6 = (bf16[4,528,128]{2,1,0:T(8,128)(2,1)S(1)}, bf16[4,528,128]{2,1,0:T(8,128)(2,1)S(1)}, u32[]{:S(2)}, u32[]{:S(2)}) collective-permute-start(bf16[4,528,128]{2,1,0:T(8,128)(2,1)S(1)} %collective-permute-done.5.refs_2_.refs_4_), channel_id=1, source_target_pairs={{0,16},{16,0},{1,17},{17,1},{2,18},{18,2},{3,19},{19,3},{4,20},{20... | collective-permute-start | bytes 1622024 | tf_op jit(solution)/shard_map/ppermute | solution.py:243
  55.7 5.1 %collective-permute-start.9 = (bf16[2,512,128]{2,1,0:T(8,128)(2,1)S(1)}, bf16[2,512,128]{2,1,0:T(8,128)(2,1)S(1)}, u32[]{:S(2)}, u32[]{:S(2)}) collective-permute-start(bf16[2,512,128]{2,1,0:T(8,128)(2,1)S(1)} %pad_maximum_fusion.1.refs_4_.refs_6_), channel_id=1, source_target_pairs={{0,3},{1,0},{2,1},{3,2},{4,7},{5,4},{6,5},{7,6},{8,11},{9,8},{10,9... | collective-permute-start | bytes 786440 | tf_op jit(solution)/shard_map/ppermute | solution.py:242
  60.8 1.9 %collective-permute-start.8 = (bf16[2,512,128]{2,1,0:T(8,128)(2,1)S(1)}, bf16[2,512,128]{2,1,0:T(8,128)(2,1)S(1)}, u32[]{:S(2)}, u32[]{:S(2)}) collective-permute-start(bf16[2,512,128]{2,1,0:T(8,128)(2,1)S(1)} %pad_maximum_fusion.1.refs_4_.refs_6_), channel_id=1, source_target_pairs={{0,2},{1,3},{2,0},{3,1},{4,6},{5,7},{6,4},{7,5},{8,10},{9,11},{10,... | collective-permute-start | bytes 786440 | tf_op jit(solution)/shard_map/ppermute | solution.py:242
  62.7 2.5 %collective-permute-start.7 = (bf16[2,512,128]{2,1,0:T(8,128)(2,1)S(1)}, bf16[2,512,128]{2,1,0:T(8,128)(2,1)S(1)}, u32[]{:S(2)}, u32[]{:S(2)}) collective-permute-start(bf16[2,512,128]{2,1,0:T(8,128)(2,1)S(1)} %pad_maximum_fusion.1.refs_4_.refs_6_), channel_id=1, source_target_pairs={{0,1},{1,2},{2,3},{3,0},{4,5},{5,6},{6,7},{7,4},{8,9},{9,10},{10,1... | collective-permute-start | bytes 786440 | tf_op jit(solution)/shard_map/ppermute | solution.py:242
  65.2 5.9 %collective-permute-done.9.refs_7_.refs_9_ = bf16[2,512,128]{2,1,0:T(8,128)(2,1)S(1)} collective-permute-done((bf16[2,512,128]{2,1,0:T(8,128)(2,1)S(1)}, bf16[2,512,128]{2,1,0:T(8,128)(2,1)S(1)}, u32[]{:S(2)}, u32[]{:S(2)}) %collective-permute-start.9) | collective-permute-done | bytes 262176 | tf_op jit(solution)/shard_map/ppermute | solution.py:242
  71.1 1.5 %collective-permute-done.8.refs_6_.refs_8_ = bf16[2,512,128]{2,1,0:T(8,128)(2,1)S(1)} collective-permute-done((bf16[2,512,128]{2,1,0:T(8,128)(2,1)S(1)}, bf16[2,512,128]{2,1,0:T(8,128)(2,1)S(1)}, u32[]{:S(2)}, u32[]{:S(2)}) %collective-permute-start.8) | collective-permute-done | bytes 262176 | tf_op jit(solution)/shard_map/ppermute | solution.py:242
  72.6 6.0 %collective-permute-done.7.refs_5_.refs_7_ = bf16[2,512,128]{2,1,0:T(8,128)(2,1)S(1)} collective-permute-done((bf16[2,512,128]{2,1,0:T(8,128)(2,1)S(1)}, bf16[2,512,128]{2,1,0:T(8,128)(2,1)S(1)}, u32[]{:S(2)}, u32[]{:S(2)}) %collective-permute-start.7) | collective-permute-done | bytes 262176 | tf_op jit(solution)/shard_map/ppermute | solution.py:242
  78.6 5.8 %norms.1.refs_1_ = f32[16,1,128]{2,1,0:T(1,128)S(1)} custom-call(bf16[4,528,128]{2,1,0:T(8,128)(2,1)S(1)} %pad_maximum_fusion.refs_0_.refs_2_, bf16[4,528,128]{2,1,0:T(8,128)(2,1)S(1)} %collective-permute-done.4.refs_1_.refs_3_, bf16[4,528,128]{2,1,0:T(8,128)(2,1)S(1)} %collective-permute-done.5.refs_2_.refs_4_, ...), custom_call_target="tpu_custom_call" | custom-call | tf_op jit(solution)/shard_map/norms/pallas_call | solution.py:252
  84.3 9.7 %all_to_all.15.refs_0_ = f32[16,1,128]{2,1,0:T(1,128)S(1)} all-to-all(f32[16,1,128]{2,1,0:T(1,128)S(1)} %norms.1.refs_1_), channel_id=1, replica_groups=mesh['zh'=4,'zl'=2,'yl'=2,'c'=2,'yh'=4,'x'=4] {'yl','c','x'}, dimensions={0} | all-to-all | bytes 16384 | tf_op jit(solution)/shard_map/all_to_all | solution.py:262
  94.1 2.5 %grads.1 = (f32[4,8,72,128]{3,2,1,0:T(8,128)S(1)}, f32[1,8]{1,0:T(1,128)S(1)}) custom-call(f32[16,1,128]{2,1,0:T(1,128)S(1)} %all_to_all.15.refs_0_, f32[16,1,128]{2,1,0:T(1,128)S(1)} %norms.1.refs_1_, bf16[4,528,128]{2,1,0:T(8,128)(2,1)S(1)} %pad_maximum_fusion.refs_0_.refs_2_, bf16[4,528,128]{2,1,0:T(8,128)(2,1)S(1)} %collective-permute-done.4.refs_1_.refs_3_, ...), custom_call_target="tpu_custom_call" | custom-call | tf_op jit(solution)/shard_map/grads/pallas_call | solution.py:263
  96.6 0.9 convert_element_type.6
  97.5 11.6 %all-to-all-start.2 = ((f16[32,72,128]{2,1,0:T(8,128)(2,1)}), f16[32,72,128]{2,1,0:T(8,128)(2,1)S(1)}, u32[]{:S(2)}, u32[]{:S(2)}) async-start(f16[32,72,128]{2,1,0:T(8,128)(2,1)} %bitcast.10), calls=%async_computation.2 | async-start | bytes 1179648 | tf_op jit(solution)/shard_map/all_to_all | solution.py:274
  109.1 5.2 %collective-permute-start.10 = (f32[1,8]{1,0:T(1,128)S(1)}, f32[1,8]{1,0:T(1,128)S(1)}, u32[]{:S(2)}, u32[]{:S(2)}) collective-permute-start(f32[1,8]{1,0:T(1,128)S(1)} %get-tuple-element.13), channel_id=1, source_target_pairs={{0,0},{1,1},{2,2},{3,3},{16,4},{17,5},{18,6},{19,7},{32,8},{33,9},... | collective-permute-start | bytes 104 | tf_op jit(solution)/shard_map/ppermute | solution.py:277
  114.3 12.6 %collective-permute-done.10 = f32[1,8]{1,0:T(1,128)S(1)} collective-permute-done((f32[1,8]{1,0:T(1,128)S(1)}, f32[1,8]{1,0:T(1,128)S(1)}, u32[]{:S(2)}, u32[]{:S(2)}) %collective-permute-start.10) | collective-permute-done | bytes 64 | tf_op jit(solution)/shard_map/ppermute | solution.py:277
  126.9 2.3 %all-to-all-done.2 = f16[32,72,128]{2,1,0:T(8,128)(2,1)S(1)} async-done(((f16[32,72,128]{2,1,0:T(8,128)(2,1)}), f16[32,72,128]{2,1,0:T(8,128)(2,1)S(1)}, u32[]{:S(2)}, u32[]{:S(2)}) %all-to-all-start.2) | async-done | bytes 589856 | tf_op jit(solution)/shard_map/all_to_all | solution.py:274
  129.2 0.1 convert_element_type.7
  129.3 0.7 fusion
  130.0 0.5 copy.6
  (15 shorter events, 0.2 us)
Async XLA Ops:
  2.1 21.8 %collective-permute-start = (bf16[1040,128]{1,0:T(8,128)(2,1)S(1)}, bf16[1040,128]{1,0:T(8,128)(2,1)S(1)}, u32[]{:S(2)}, u32[]{:S(2)}) collective-permute-start(bf16[1040,128]{1,0:T(8,128)(2,1)S(1)} %get-tuple-element.8), channel_id=1, source_target_pairs={{0,17},{1,18},{2,19},{3,16},{4,1},{5,2},{6,3},{7,0},{8,49},{9,50},... | collective-permute-start | bytes 798728 | tf_op jit(solution)/shard_map/ppermute | solution.py:228
  11.3 23.1 %collective-permute-start.1 = (bf16[1040,128]{1,0:T(8,128)(2,1)S(1)}, bf16[1040,128]{1,0:T(8,128)(2,1)S(1)}, u32[]{:S(2)}, u32[]{:S(2)}) collective-permute-start(bf16[1040,128]{1,0:T(8,128)(2,1)S(1)} %get-tuple-element.9), channel_id=1, source_target_pairs={{0,51},{1,48},{2,49},{3,50},{4,35},{5,32},{6,33},{7,34},{8,19},{9,... | collective-permute-start | bytes 798728 | tf_op jit(solution)/shard_map/ppermute | solution.py:228
  14.1 20.8 %collective-permute-start.2 = (bf16[1040,128]{1,0:T(8,128)(2,1)S(1)}, bf16[1040,128]{1,0:T(8,128)(2,1)S(1)}, u32[]{:S(2)}, u32[]{:S(2)}) collective-permute-start(bf16[1040,128]{1,0:T(8,128)(2,1)S(1)} %get-tuple-element.10), channel_id=1, source_target_pairs={{0,0},{1,1},{2,2},{3,3},{4,16},{5,17},{6,18},{7,19},{8,32},{9,33},... | collective-permute-start | bytes 798728 | tf_op jit(solution)/shard_map/ppermute | solution.py:228
  22.0 13.9 %collective-permute-start.3 = (bf16[1040,128]{1,0:T(8,128)(2,1)S(1)}, bf16[1040,128]{1,0:T(8,128)(2,1)S(1)}, u32[]{:S(2)}, u32[]{:S(2)}) collective-permute-start(bf16[1040,128]{1,0:T(8,128)(2,1)S(1)} %get-tuple-element.11), channel_id=1, source_target_pairs={{0,34},{1,35},{2,32},{3,33},{4,50},{5,51},{6,48},{7,49},{8,2},{9,3... | collective-permute-start | bytes 798728 | tf_op jit(solution)/shard_map/ppermute | solution.py:228
  36.0 15.8 %collective-permute-start.5 = (bf16[4,528,128]{2,1,0:T(8,128)(2,1)S(1)}, bf16[4,528,128]{2,1,0:T(8,128)(2,1)S(1)}, u32[]{:S(2)}, u32[]{:S(2)}) collective-permute-start(bf16[4,528,128]{2,1,0:T(8,128)(2,1)S(1)} %pad_maximum_fusion.refs_0_.refs_2_), channel_id=1, source_target_pairs={{0,32},{32,0},{1,33},{33,1},{2,34},{34,2},{3,35},{35,3},{4,36},{36... | collective-permute-start | bytes 1622024 | tf_op jit(solution)/shard_map/ppermute | solution.py:238
  37.9 40.7 %collective-permute-start.4 = (bf16[4,528,128]{2,1,0:T(8,128)(2,1)S(1)}, bf16[4,528,128]{2,1,0:T(8,128)(2,1)S(1)}, u32[]{:S(2)}, u32[]{:S(2)}) collective-permute-start(bf16[4,528,128]{2,1,0:T(8,128)(2,1)S(1)} %pad_maximum_fusion.refs_0_.refs_2_), channel_id=1, source_target_pairs={{0,16},{16,0},{1,17},{17,1},{2,18},{18,2},{3,19},{19,3},{4,20},{20... | collective-permute-start | bytes 1622024 | tf_op jit(solution)/shard_map/ppermute | solution.py:239
  47.5 31.0 %all-to-all-start = ((bf16[4,2,512,128]{3,2,1,0:T(8,128)(2,1)}), bf16[4,2,512,128]{3,2,1,0:T(8,128)(2,1)}, u32[]{:S(2)}, u32[]{:S(2)}) async-start(bf16[4,2,512,128]{3,2,1,0:T(8,128)(2,1)} %broadcast_in_dim.3), calls=%async_computation | async-start | bytes 2097152 | tf_op jit(solution)/shard_map/all_to_all | solution.py:233
  51.8 26.7 %collective-permute-start.6 = (bf16[4,528,128]{2,1,0:T(8,128)(2,1)S(1)}, bf16[4,528,128]{2,1,0:T(8,128)(2,1)S(1)}, u32[]{:S(2)}, u32[]{:S(2)}) collective-permute-start(bf16[4,528,128]{2,1,0:T(8,128)(2,1)S(1)} %collective-permute-done.5.refs_2_.refs_4_), channel_id=1, source_target_pairs={{0,16},{16,0},{1,17},{17,1},{2,18},{18,2},{3,19},{19,3},{4,20},{20... | collective-permute-start | bytes 1622024 | tf_op jit(solution)/shard_map/ppermute | solution.py:243
  55.7 15.4 %collective-permute-start.9 = (bf16[2,512,128]{2,1,0:T(8,128)(2,1)S(1)}, bf16[2,512,128]{2,1,0:T(8,128)(2,1)S(1)}, u32[]{:S(2)}, u32[]{:S(2)}) collective-permute-start(bf16[2,512,128]{2,1,0:T(8,128)(2,1)S(1)} %pad_maximum_fusion.1.refs_4_.refs_6_), channel_id=1, source_target_pairs={{0,3},{1,0},{2,1},{3,2},{4,7},{5,4},{6,5},{7,6},{8,11},{9,8},{10,9... | collective-permute-start | bytes 786440 | tf_op jit(solution)/shard_map/ppermute | solution.py:242
  60.8 11.8 %collective-permute-start.8 = (bf16[2,512,128]{2,1,0:T(8,128)(2,1)S(1)}, bf16[2,512,128]{2,1,0:T(8,128)(2,1)S(1)}, u32[]{:S(2)}, u32[]{:S(2)}) collective-permute-start(bf16[2,512,128]{2,1,0:T(8,128)(2,1)S(1)} %pad_maximum_fusion.1.refs_4_.refs_6_), channel_id=1, source_target_pairs={{0,2},{1,3},{2,0},{3,1},{4,6},{5,7},{6,4},{7,5},{8,10},{9,11},{10,... | collective-permute-start | bytes 786440 | tf_op jit(solution)/shard_map/ppermute | solution.py:242
  62.7 15.8 %collective-permute-start.7 = (bf16[2,512,128]{2,1,0:T(8,128)(2,1)S(1)}, bf16[2,512,128]{2,1,0:T(8,128)(2,1)S(1)}, u32[]{:S(2)}, u32[]{:S(2)}) collective-permute-start(bf16[2,512,128]{2,1,0:T(8,128)(2,1)S(1)} %pad_maximum_fusion.1.refs_4_.refs_6_), channel_id=1, source_target_pairs={{0,1},{1,2},{2,3},{3,0},{4,5},{5,6},{6,7},{7,4},{8,9},{9,10},{10,1... | collective-permute-start | bytes 786440 | tf_op jit(solution)/shard_map/ppermute | solution.py:242
  97.5 31.7 %all-to-all-start.2 = ((f16[32,72,128]{2,1,0:T(8,128)(2,1)}), f16[32,72,128]{2,1,0:T(8,128)(2,1)S(1)}, u32[]{:S(2)}, u32[]{:S(2)}) async-start(f16[32,72,128]{2,1,0:T(8,128)(2,1)} %bitcast.10), calls=%async_computation.2 | async-start | bytes 1179648 | tf_op jit(solution)/shard_map/all_to_all | solution.py:274
  109.1 17.8 %collective-permute-start.10 = (f32[1,8]{1,0:T(1,128)S(1)}, f32[1,8]{1,0:T(1,128)S(1)}, u32[]{:S(2)}, u32[]{:S(2)}) collective-permute-start(f32[1,8]{1,0:T(1,128)S(1)} %get-tuple-element.13), channel_id=1, source_target_pairs={{0,0},{1,1},{2,2},{3,3},{16,4},{17,5},{18,6},{19,7},{32,8},{33,9},... | collective-permute-start | bytes 104 | tf_op jit(solution)/shard_map/ppermute | solution.py:277
